TPU v7x, 32 devices: a whole 2x2x4 slice. The times are simulated.
32 devices in a mesh: dp: 8 (over z, x), tensor: 4 (over y, core).
Axes of the slice: x: 2, y: 2, z: 4, core: 2. Of those that a mesh axis runs over, the one named last changes fastest.
Arguments:
- frames: bfloat16 [2, 32768, 512], P(None, ('dp', 'tensor')), may hold values from -6 to 6
- cotangent: bfloat16 [2, 32768, 512], P(None, ('dp', 'tensor')), may hold values from -6 to 6
- clip_lengths: int32 [2, 32, 4], P(None, 'dp'), may hold values from 1 to 512, 1024 in all within a row
- in_proj: float32 [512, 8, 192], P('dp', 'tensor'), may hold values from -0.25 to 0.25
- out_proj: float32 [8, 64, 512], P('tensor', None, 'dp'), may hold values from -1 to 1
- up_proj: float32 [512, 2048], P('dp', 'tensor'), may hold values from -0.25 to 0.25
- down_proj: float32 [2048, 512], P('tensor', 'dp'), may hold values from -0.125 to 0.125
- small_params: float32 [6, 512], replicated, may hold values from 0.5 to 1.5
- in_first: float32 [512, 8, 192], P('dp', 'tensor'), may hold values from -384 to 384
- in_second: float32 [512, 8, 192], P('dp', 'tensor'), may hold values from 4194.304 to 16777.217
- out_first: float32 [8, 64, 512], P('tensor', None, 'dp'), may hold values from -128 to 128
- out_second: float32 [8, 64, 512], P('tensor', None, 'dp'), may hold values from 589.824 to 2359.296
- up_first: float32 [512, 2048], P('dp', 'tensor'), may hold values from -384 to 384
- up_second: float32 [512, 2048], P('dp', 'tensor'), may hold values from 4096 to 16384
- down_first: float32 [2048, 512], P('tensor', 'dp'), may hold values from -768 to 768
- down_second: float32 [2048, 512], P('tensor', 'dp'), may hold values from 16384 to 65536
- small_first: float32 [6, 512], replicated, may hold values from -1536 to 1536
- small_second: float32 [6, 512], replicated, may hold values from 65536 to 262144
Outputs:
- block_out: bfloat16 [2, 32768, 512], P(None, ('dp', 'tensor'))
- input_grad: bfloat16 [2, 32768, 512], P(None, ('dp', 'tensor'))
- in_new: float32 [512, 8, 192], P('dp', 'tensor')
- in_new_first: float32 [512, 8, 192], P('dp', 'tensor')
- in_new_second: float32 [512, 8, 192], P('dp', 'tensor')
- in_copy: bfloat16 [512, 8, 192], P('dp', 'tensor')
- out_new: float32 [8, 64, 512], P('tensor', None, 'dp')
- out_new_first: float32 [8, 64, 512], P('tensor', None, 'dp')
- out_new_second: float32 [8, 64, 512], P('tensor', None, 'dp')
- out_copy: bfloat16 [8, 64, 512], P('tensor', None, 'dp')
- up_new: float32 [512, 2048], P('dp', 'tensor')
- up_new_first: float32 [512, 2048], P('dp', 'tensor')
- up_new_second: float32 [512, 2048], P('dp', 'tensor')
- up_copy: bfloat16 [512, 2048], P('dp', 'tensor')
- down_new: float32 [2048, 512], P('tensor', 'dp')
- down_new_first: float32 [2048, 512], P('tensor', 'dp')
- down_new_second: float32 [2048, 512], P('tensor', 'dp')
- down_copy: bfloat16 [2048, 512], P('tensor', 'dp')
- small_grad: float32 [6, 512], replicated
- small_new: float32 [6, 512], replicated
- small_new_first: float32 [6, 512], replicated
- small_new_second: float32 [6, 512], replicated
- norms: float32 [2, 10], replicated
Inputs may be any that keep to these rules, and one draw needn't show every extreme that they name: `clip_lengths`: each bucket's 4 runs are whole numbers that sum to 1024; the last run of each bucket is padding.
All inputs are finite; a program needn't handle non-finite values.
Results may differ from a plain program's by a relative error of at most 0.015.
Values may be sent and summed in bfloat16 or wider, within the bound.
A program may use at most 256 MiB of HBM per device.

v0:
```python
import math

import jax
import jax.numpy as jnp
from jax import lax
from jax.sharding import PartitionSpec as P

D = 512
HEAD_DIM = 64
WINDOW = 250
LEN = 1024
CLIPS = 4
MICRO = 2
STEP = 3


beta_first = 0.5
beta_second = 0.5
adam_eps = 1e-06
decay_rate = 0.01
learn_rate = 0.3


def clip_layout(lengths):
    clip_ends = jnp.cumsum(lengths)
    position = jnp.arange(LEN, dtype=jnp.int32)
    clip_of = jnp.sum((position[:, None] >= clip_ends[None, : CLIPS - 1]).astype(jnp.int32), axis=1)
    starts = clip_ends - lengths
    belongs = clip_of[:, None] == jnp.arange(CLIPS, dtype=jnp.int32)[None, :]
    clip_begin = jnp.sum(jnp.where(belongs, starts[None, :], 0), axis=1)
    return (clip_of, position - clip_begin)


def allowed_pairs(clip_of):
    position = jnp.arange(LEN, dtype=jnp.int32)
    causal = position[None, :] <= position[:, None]
    inside = position[:, None] - position[None, :] < WINDOW
    same_clip = clip_of[:, None] == clip_of[None, :]
    return causal & inside & same_clip


def rotate(values_in, offset):
    half_dim = HEAD_DIM // 2
    frequency = jnp.exp(
        jnp.arange(half_dim, dtype=jnp.float32) * (-2.0 * math.log(10000.0) / HEAD_DIM)
    )
    angles = offset.astype(jnp.float32)[:, None] * frequency[None, :]
    cosine = jnp.cos(angles)
    sine = jnp.sin(angles)
    paired = values_in.reshape(values_in.shape[:-1] + (half_dim, 2))
    even_part = paired[..., 0]
    odd_part = paired[..., 1]
    turned = jnp.stack(
        [even_part * cosine - odd_part * sine, even_part * sine + odd_part * cosine], axis=-1
    )
    return turned.reshape(values_in.shape)


def layer_norm(rows, gain, bias):
    centred = rows - jnp.mean(rows, -1, keepdims=True)
    inverse = lax.rsqrt(jnp.mean(centred * centred, -1, keepdims=True) + 1e-05)
    normal = centred * inverse
    return (normal * gain + bias, normal, inverse)


def norm_back(incoming, normal, inverse, gain):
    scaled = incoming * gain
    return inverse * (
        scaled
        - jnp.mean(scaled, -1, keepdims=True)
        - normal * jnp.mean(scaled * normal, -1, keepdims=True)
    )


def gelu_value(values_in):
    return values_in * 0.5 * (1.0 + lax.erf(values_in * (1.0 / math.sqrt(2.0))))


def gelu_slope(values_in):
    cumulative = 0.5 * (1.0 + lax.erf(values_in * (1.0 / math.sqrt(2.0))))
    density = jnp.exp(-0.5 * values_in * values_in) * (1.0 / math.sqrt(2.0 * math.pi))
    return cumulative + values_in * density


def head_scores(queries, keys_rot, clip_of):
    raw = jnp.einsum("qd,kd->qk", queries, keys_rot, preferred_element_type=jnp.float32)
    return jnp.where(allowed_pairs(clip_of), raw * HEAD_DIM ** (-0.5), -1e30)


def attend_forward(head_item):
    head_part, clip_size = head_item
    clip_of, offset = clip_layout(clip_size)
    queries = rotate(head_part[:, 0], offset).astype(jnp.bfloat16)
    keys_rot = rotate(head_part[:, 1], offset).astype(jnp.bfloat16)
    values = head_part[:, 2].astype(jnp.bfloat16)
    scores = head_scores(queries, keys_rot, clip_of)
    top_score = jnp.max(scores, -1, keepdims=True)
    log_total = top_score + jnp.log(jnp.sum(jnp.exp(scores - top_score), -1, keepdims=True))
    attn = jnp.exp(scores - log_total)
    mixed_head = jnp.dot(
        attn.astype(jnp.bfloat16), values, preferred_element_type=jnp.float32
    ).astype(jnp.bfloat16)
    return (jnp.stack([queries, keys_rot, values]), log_total[:, 0], mixed_head)


def attend_back(head_item):
    kept_qkv, log_total, grad_head, clip_size = head_item
    clip_of, offset = clip_layout(clip_size)
    queries = kept_qkv[0]
    keys_rot = kept_qkv[1]
    values = kept_qkv[2]
    attn = jnp.exp(head_scores(queries, keys_rot, clip_of) - log_total[:, None])
    grad_values = jnp.einsum(
        "qk,qd->kd", attn.astype(jnp.bfloat16), grad_head, preferred_element_type=jnp.float32
    )
    grad_attn = jnp.einsum("qd,kd->qk", grad_head, values, preferred_element_type=jnp.float32)
    grad_scores = attn * (grad_attn - jnp.sum(grad_attn * attn, -1, keepdims=True))
    grad_raw = (grad_scores * HEAD_DIM ** (-0.5)).astype(jnp.bfloat16)
    grad_queries = jnp.dot(grad_raw, keys_rot, preferred_element_type=jnp.float32)
    grad_keys = jnp.einsum("qk,qd->kd", grad_raw, queries, preferred_element_type=jnp.float32)
    return jnp.stack(
        [rotate(grad_queries, -offset), rotate(grad_keys, -offset), grad_values], axis=1
    ).astype(jnp.bfloat16)


def split_heads(flat_rows, head_count, item_width):
    blocks = flat_rows.reshape(-1, LEN, head_count, item_width)
    return jnp.moveaxis(blocks, 2, 1).reshape(-1, LEN, item_width)


def merge_heads(head_items, head_count):
    item_width = head_items.shape[-1]
    blocks = head_items.reshape(-1, head_count, LEN, item_width)
    return jnp.moveaxis(blocks, 1, 2).reshape(-1, head_count * item_width)


def reduce_grads(local_grads):
    return (
        lax.psum_scatter(local_grads[0], "dp", scatter_dimension=0, tiled=True),
        lax.psum_scatter(local_grads[1], "dp", scatter_dimension=2, tiled=True),
        lax.psum_scatter(local_grads[2], "dp", scatter_dimension=0, tiled=True),
        lax.psum_scatter(local_grads[3], "dp", scatter_dimension=1, tiled=True),
    )


def on_device(
    frames,
    cotangent,
    clip_lengths,
    in_proj,
    out_proj,
    up_proj,
    down_proj,
    small_params,
    in_first,
    in_second,
    out_first,
    out_second,
    up_first,
    up_second,
    down_first,
    down_second,
    small_first,
    small_second,
):
    rows_here = frames.shape[1]
    own_buckets = rows_here // LEN
    first_bucket = lax.axis_index("tensor") * own_buckets
    copies = (
        in_proj.astype(jnp.bfloat16),
        out_proj.astype(jnp.bfloat16),
        up_proj.astype(jnp.bfloat16),
        down_proj.astype(jnp.bfloat16),
    )
    gathered = (
        lax.all_gather(copies[0], "dp", axis=0, tiled=True),
        lax.all_gather(copies[1], "dp", axis=2, tiled=True),
        lax.all_gather(copies[2], "dp", axis=0, tiled=True),
        lax.all_gather(copies[3], "dp", axis=1, tiled=True),
    )
    in_w, out_w, up_w, down_w = gathered
    head_count = in_w.shape[1]
    in_mat = in_w.reshape(D, -1)
    out_mat = out_w.reshape(-1, D)
    outputs = []
    input_grads = []
    small_terms = jnp.zeros((6, D), jnp.float32)
    owned = None
    for batch_index in range(MICRO):
        group_sizes = clip_lengths[batch_index]
        own_sizes = lax.dynamic_slice_in_dim(group_sizes, first_bucket, own_buckets, 0)
        rows_in = frames[batch_index].astype(jnp.float32)
        normed1, normal1, inverse1 = layer_norm(rows_in, small_params[0], small_params[1])
        enter1 = normed1.astype(jnp.bfloat16)
        enter1_all = lax.all_gather(enter1, "tensor", axis=0, tiled=True)
        projected = jnp.dot(enter1_all, in_mat, preferred_element_type=jnp.float32)
        head_items = split_heads(projected, head_count, 3 * HEAD_DIM).reshape(-1, LEN, 3, HEAD_DIM)
        item_sizes = jnp.repeat(group_sizes, head_count, axis=0)
        kept_qkv, log_totals, mixed_items = lax.map(attend_forward, (head_items, item_sizes))
        mixed_rows = merge_heads(mixed_items, head_count)
        branch = lax.psum_scatter(
            jnp.dot(mixed_rows, out_mat, preferred_element_type=jnp.float32),
            "tensor",
            scatter_dimension=0,
            tiled=True,
        )
        y_first = rows_in + small_params[4] * branch
        normed2, normal2, inverse2 = layer_norm(y_first, small_params[2], small_params[3])
        enter2 = normed2.astype(jnp.bfloat16)
        enter2_all = lax.all_gather(enter2, "tensor", axis=0, tiled=True)
        upval = jnp.dot(enter2_all, up_w, preferred_element_type=jnp.float32)
        act = gelu_value(upval).astype(jnp.bfloat16)
        mlp = lax.psum_scatter(
            jnp.dot(act, down_w, preferred_element_type=jnp.float32).astype(jnp.bfloat16),
            "tensor",
            scatter_dimension=0,
            tiled=True,
        ).astype(jnp.float32)
        outputs.append((y_first + small_params[5] * mlp).astype(jnp.bfloat16))
        clip_of = jax.vmap(lambda length_row: clip_layout(length_row)[0])(own_sizes)
        valid_rows = (clip_of < CLIPS - 1).astype(jnp.float32).reshape(-1)
        grad_y = cotangent[batch_index].astype(jnp.float32) * valid_rows[:, None]
        grad_mlp = (small_params[5] * grad_y).astype(jnp.bfloat16)
        grad_mlp_all = lax.all_gather(grad_mlp, "tensor", axis=0, tiled=True)
        grad_downproj = jnp.einsum(
            "rf,rd->fd", act, grad_mlp_all, preferred_element_type=jnp.float32
        )
        grad_act = jnp.einsum("rd,fd->rf", grad_mlp_all, down_w, preferred_element_type=jnp.float32)
        grad_up = (grad_act * gelu_slope(upval)).astype(jnp.bfloat16)
        grad_upproj = jnp.einsum(
            "rd,rf->df", enter2_all, grad_up, preferred_element_type=jnp.float32
        )
        grad_enter2 = lax.psum_scatter(
            jnp.einsum("rf,df->rd", grad_up, up_w, preferred_element_type=jnp.float32),
            "tensor",
            scatter_dimension=0,
            tiled=True,
        )
        grad_y_first = grad_y + norm_back(grad_enter2, normal2, inverse2, small_params[2])
        grad_branch = (small_params[4] * grad_y_first).astype(jnp.bfloat16)
        grad_branch_all = lax.all_gather(grad_branch, "tensor", axis=0, tiled=True)
        grad_outproj = jnp.einsum(
            "rh,rd->hd", mixed_rows, grad_branch_all, preferred_element_type=jnp.float32
        )
        grad_mixed = jnp.einsum(
            "rd,hd->rh", grad_branch_all, out_mat, preferred_element_type=jnp.float32
        ).astype(jnp.bfloat16)
        grad_items = split_heads(grad_mixed, head_count, HEAD_DIM)
        grad_heads = lax.map(attend_back, (kept_qkv, log_totals, grad_items, item_sizes))
        grad_projected = merge_heads(grad_heads.reshape(-1, LEN, 3 * HEAD_DIM), head_count)
        grad_inproj = jnp.einsum(
            "rd,re->de", enter1_all, grad_projected, preferred_element_type=jnp.float32
        )
        grad_enter1 = lax.psum_scatter(
            jnp.einsum(
                "re,de->rd", grad_projected, in_mat, preferred_element_type=jnp.float32
            ).astype(jnp.bfloat16),
            "tensor",
            scatter_dimension=0,
            tiled=True,
        ).astype(jnp.float32)
        grad_frames = grad_y_first + norm_back(grad_enter1, normal1, inverse1, small_params[0])
        input_grads.append(grad_frames.astype(jnp.bfloat16))
        small_terms = small_terms + jnp.stack(
            [
                jnp.sum(grad_enter1 * normal1, 0),
                jnp.sum(grad_enter1, 0),
                jnp.sum(grad_enter2 * normal2, 0),
                jnp.sum(grad_enter2, 0),
                jnp.sum(grad_y_first * branch, 0),
                jnp.sum(grad_y * mlp, 0),
            ]
        )
        micro_grads = (
            grad_inproj.reshape(in_w.shape),
            grad_outproj.reshape(out_w.shape),
            grad_upproj,
            grad_downproj,
        )
        summed = reduce_grads(micro_grads)
        owned = (
            summed if owned is None else tuple((left + right for left, right in zip(owned, summed)))
        )
    weights_in = (in_proj, out_proj, up_proj, down_proj)
    firsts = (in_first, out_first, up_first, down_first)
    seconds = (in_second, out_second, up_second, down_second)
    own_squares = jnp.stack([jnp.sum(weight * weight) for weight in weights_in])
    small_grad, weight_squares = lax.psum((small_terms, own_squares), ("dp", "tensor"))
    new_firsts = []
    new_seconds = []
    updates = []
    for weight, gradient, first, second in zip(weights_in, owned, firsts, seconds):
        first = beta_first * first + (1.0 - beta_first) * gradient
        second = beta_second * second + (1.0 - beta_second) * gradient * gradient
        update = (
            first
            / (1.0 - beta_first**STEP)
            / (jnp.sqrt(second / (1.0 - beta_second**STEP)) + adam_eps)
            + decay_rate * weight
        )
        new_firsts.append(first)
        new_seconds.append(second)
        updates.append(update)
    update_squares = lax.psum(
        jnp.stack([jnp.sum(update * update) for update in updates]), ("dp", "tensor")
    )
    trust_ratio = jnp.sqrt(weight_squares) * lax.rsqrt(update_squares + 1e-12)
    new_weights = [
        weights_in[index] - learn_rate * trust_ratio[index] * updates[index] for index in range(4)
    ]
    small_first_new = beta_first * small_first + (1.0 - beta_first) * small_grad
    small_second_new = beta_second * small_second + (1.0 - beta_second) * small_grad * small_grad
    small_update = (
        small_first_new
        / (1.0 - beta_first**STEP)
        / (jnp.sqrt(small_second_new / (1.0 - beta_second**STEP)) + adam_eps)
        + decay_rate * small_params
    )
    small_weight_sq = jnp.sum(small_params * small_params, axis=1, keepdims=True)
    small_update_sq = jnp.sum(small_update * small_update, axis=1, keepdims=True)
    small_new = (
        small_params
        - learn_rate * jnp.sqrt(small_weight_sq) * lax.rsqrt(small_update_sq + 1e-12) * small_update
    )
    norms = jnp.stack(
        [
            jnp.concatenate([jnp.sqrt(weight_squares), jnp.sqrt(small_weight_sq).reshape(-1)]),
            jnp.concatenate([jnp.sqrt(update_squares), jnp.sqrt(small_update_sq).reshape(-1)]),
        ]
    )
    block_out = jnp.stack(outputs)
    input_grad = jnp.stack(input_grads)
    return (
        block_out,
        input_grad,
        new_weights[0],
        new_firsts[0],
        new_seconds[0],
        new_weights[0].astype(jnp.bfloat16),
        new_weights[1],
        new_firsts[1],
        new_seconds[1],
        new_weights[1].astype(jnp.bfloat16),
        new_weights[2],
        new_firsts[2],
        new_seconds[2],
        new_weights[2].astype(jnp.bfloat16),
        new_weights[3],
        new_firsts[3],
        new_seconds[3],
        new_weights[3].astype(jnp.bfloat16),
        small_grad,
        small_new,
        small_first_new,
        small_second_new,
        norms,
    )


def solution(mesh):
    return jax.shard_map(
        on_device,
        mesh=mesh,
        in_specs=(
            P(None, ("dp", "tensor"), None),
            P(None, ("dp", "tensor"), None),
            P(None, "dp", None),
            P("dp", "tensor", None),
            P("tensor", None, "dp"),
            P("dp", "tensor"),
            P("tensor", "dp"),
            P(),
            P("dp", "tensor", None),
            P("dp", "tensor", None),
            P("tensor", None, "dp"),
            P("tensor", None, "dp"),
            P("dp", "tensor"),
            P("dp", "tensor"),
            P("tensor", "dp"),
            P("tensor", "dp"),
            P(),
            P(),
        ),
        out_specs=(
            P(None, ("dp", "tensor"), None),
            P(None, ("dp", "tensor"), None),
            P("dp", "tensor", None),
            P("dp", "tensor", None),
            P("dp", "tensor", None),
            P("dp", "tensor", None),
            P("tensor", None, "dp"),
            P("tensor", None, "dp"),
            P("tensor", None, "dp"),
            P("tensor", None, "dp"),
            P("dp", "tensor"),
            P("dp", "tensor"),
            P("dp", "tensor"),
            P("dp", "tensor"),
            P("tensor", "dp"),
            P("tensor", "dp"),
            P("tensor", "dp"),
            P("tensor", "dp"),
            P(),
            P(),
            P(),
            P(),
            P(),
        ),
        check_vma=False,
    )
```

profile of v0, /device:TPU:0, one launch (start us, length us, event | category | flops | bytes accessed | tf_op | source)
XLA Modules:
  0.0 1468.0 jit_solution(3563805246009885565)
XLA Ops:
  14.0 32.6 %all_gather.38 = bf16[2,64,512]{1,0,2:T(2,128)(2,1)S(1)} all-gather(bf16[2,64,64]{1,0,2:T(2,128)(2,1)S(1)} %copy.265), channel_id=1, replica_groups=mesh['dp'=8,'tensor'=4] {'dp'}, dimensions={2}, use_global_device_ids=true | all-gather | bytes 147456 | tf_op jit(solution)/shard_map/all_gather | solution.py:177
  48.0 31.3 %all_gather.37 = bf16[512,2,192]{2,1,0:T(2,128)(2,1)S(1)} all-gather(bf16[64,2,192]{2,1,0:T(2,128)(2,1)S(1)} %get-tuple-element.540), channel_id=1, replica_groups=mesh['dp'=8,'tensor'=4] {'dp'}, dimensions={0}, use_global_device_ids=true | all-gather | bytes 442368 | tf_op jit(solution)/shard_map/all_gather | solution.py:176
  80.4 6.8 fusion.222
  87.2 6.7 fusion.224
  98.3 124.4 %while.48 = (s32[]{:T(128)}, bf16[8,3,1024,64]{2,3,1,0:T(8,128)(2,1)}, f32[8,1024]{1,0:T(8,128)}, bf16[8,1024,64]{1,2,0:T(8,128)(2,1)}, f32[8,1024,3,64]{1,3,2,0...) while((s32[]{:T(128)}, bf16[8,3,1024,64]{2,3,1,0:T(8,128)(2,1)}, f32[8,1024]{1,0:T(8,128)}, ...), condition=%wide.region_8.9_spmd, body=%wide.region_2.8_spmd.sunk | while | flops 284020800 | bytes 21299740 | solution.py:199
  226.2 4.5 fusion.261
  235.7 124.8 %while.49 = (s32[]{:T(128)}, bf16[8,3,1024,64]{2,3,1,0:T(8,128)(2,1)}, f32[8,1024]{1,0:T(8,128)}, bf16[8,1024,64]{1,2,0:T(8,128)(2,1)}, f32[8,1024,3,64]{1,3,2,0...) while((s32[]{:T(128)}, bf16[8,3,1024,64]{2,3,1,0:T(8,128)(2,1)}, f32[8,1024]{1,0:T(8,128)}, ...), condition=%wide.region_21.22_spmd, body=%wide.region_15.21_spmd.sunk | while | flops 284020800 | bytes 21299740 | solution.py:199
  364.1 4.5 fusion.262
  368.7 72.5 %reduce-scatter.19.cloned.1.call-done = f32[1024,512]{1,0:T(8,128)} async-done(((f32[4096,512]{1,0:T(8,128)}), f32[1024,512]{1,0:T(8,128)}) %reduce-scatter.19.cloned.1.call-update) | async-done | bytes 2097168 | tf_op jit(solution)/shard_map/reduce_scatter | solution.py:201
  450.1 31.5 %all_gather.41 = bf16[512,512]{0,1:T(8,128)(2,1)S(1)} all-gather(bf16[512,64]{0,1:T(8,128)(2,1)S(1)} %convert_element_type.346), channel_id=1, replica_groups=mesh['dp'=8,'tensor'=4] {'dp'}, dimensions={1}, use_global_device_ids=true | all-gather | bytes 589824 | tf_op jit(solution)/shard_map/all_gather | solution.py:179
  481.6 31.6 %all_gather.40 = bf16[512,512]{1,0:T(8,128)(2,1)S(1)} all-gather(bf16[64,512]{1,0:T(8,128)(2,1)S(1)} %convert_element_type.344), channel_id=1, replica_groups=mesh['dp'=8,'tensor'=4] {'dp'}, dimensions={0}, use_global_device_ids=true | all-gather | bytes 589824 | tf_op jit(solution)/shard_map/all_gather | solution.py:178
  513.2 7.6 multiply_convert_fusion.3
  520.8 7.6 fusion.149
  530.4 5.8 fusion.263
  536.2 17.3 %all-gather.15.cloned.1.call-done = bf16[4096,512]{1,0:T(8,128)(2,1)} async-done(((bf16[1024,512]{1,0:T(8,128)(2,1)}), bf16[4096,512]{1,0:T(8,128)(2,1)}) %all-gather.15.cloned.1.call-update) | async-done | bytes 4194320 | tf_op jit(solution)/shard_map/all_gather | solution.py:210
  553.5 6.6 multiply_convert_fusion.2
  562.2 5.3 convolution_convert_fusion.2
  567.5 7.5 convolution_convert_fusion.3
  575.6 51.9 %reduce-scatter.23.cloned.1.call-done = f32[1024,512]{1,0:T(8,128)} async-done(((f32[4096,512]{1,0:T(8,128)}), f32[1024,512]{1,0:T(8,128)}) %reduce-scatter.23.cloned.1.call-update) | async-done | bytes 2097168 | tf_op jit(solution)/shard_map/reduce_scatter | solution.py:233
  630.7 44.0 %reduce-scatter.21.cloned.1.call-done = bf16[1024,512]{1,0:T(8,128)(2,1)} async-done(((bf16[4096,512]{1,0:T(8,128)(2,1)}), bf16[1024,512]{1,0:T(8,128)(2,1)}) %reduce-scatter.21.cloned.1.call-update) | async-done | bytes 1048592 | tf_op jit(solution)/shard_map/reduce_scatter | solution.py:213
  674.6 47.0 %reduce-scatter.17.cloned.1.call-done = bf16[1024,512]{1,0:T(8,128)(2,1)} async-done(((bf16[4096,512]{1,0:T(8,128)(2,1)}), bf16[1024,512]{1,0:T(8,128)(2,1)}) %reduce-scatter.17.cloned.1.call-update) | async-done | bytes 1048592 | tf_op jit(solution)/shard_map/reduce_scatter | solution.py:213
  721.6 6.3 fusion.201
  728.0 34.6 %all-gather.21.cloned.1.call-done = bf16[4096,512]{1,0:T(8,128)(2,1)} async-done(((bf16[1024,512]{1,0:T(8,128)(2,1)}), bf16[4096,512]{1,0:T(8,128)(2,1)}) %all-gather.21.cloned.1.call-update) | async-done | bytes 4194320 | tf_op jit(solution)/shard_map/all_gather | solution.py:224
  762.5 7.6 fusion.155
  772.1 5.8 fusion.264
  778.0 71.5 %reduce-scatter.27.cloned.1.call-done = f32[1024,512]{1,0:T(8,128)} async-done(((f32[4096,512]{1,0:T(8,128)}), f32[1024,512]{1,0:T(8,128)}) %reduce-scatter.27.cloned.1.call-update) | async-done | bytes 2097168 | tf_op jit(solution)/shard_map/reduce_scatter | solution.py:233
  852.9 4.0 multiply_reduce_fusion.2
  859.7 6.0 fusion.266
  869.3 5.9 fusion.265
  875.3 3.4 convolution_add_fusion.1
  879.1 14.4 all-gather.19.cloned.1.call-done
  893.5 3.4 convolution_convert_fusion.5
  899.1 30.3 %all-gather.23.cloned.1.call-done = bf16[4096,512]{1,0:T(8,128)(2,1)} async-done(((bf16[1024,512]{1,0:T(8,128)(2,1)}), bf16[4096,512]{1,0:T(8,128)(2,1)}) %all-gather.23.cloned.1.call-update) | async-done | bytes 4194320 | tf_op jit(solution)/shard_map/all_gather | solution.py:241
  929.4 3.4 convolution_convert_fusion.4
  940.0 100.4 %while.51 = (s32[]{:T(128)}, bf16[8,1024,3,64]{1,3,2,0:T(8,128)(2,1)}, s32[8,4]{1,0:T(8,128)}, bf16[8,3,1024,64]{2,3,1,0:T(8,128)(2,1)}, f32[8,1024]{1,0:T(8,128...) while((s32[]{:T(128)}, bf16[8,1024,3,64]{1,3,2,0:T(8,128)(2,1)}, ...), condition=%wide.region_50.51_spmd, body=%wide.region_45.50_spmd.sunk | while | flops 689820672 | bytes 37543496 | solution.py:249
  1040.5 3.6 copy.298
  1046.2 108.9 %while.50 = (s32[]{:T(128)}, bf16[8,1024,3,64]{1,3,2,0:T(8,128)(2,1)}, s32[8,4]{1,0:T(8,128)}, bf16[8,3,1024,64]{2,3,1,0:T(8,128)(2,1)}, f32[8,1024]{1,0:T(8,128...) while((s32[]{:T(128)}, bf16[8,1024,3,64]{1,3,2,0:T(8,128)(2,1)}, ...), condition=%wide.region_36.37_spmd, body=%wide.region_31.36_spmd.sunk | while | flops 689820672 | bytes 37543496 | solution.py:249
  1172.4 5.7 fusion.160
  1178.1 3.4 fusion.212
  1181.5 6.2 convolution_convert_fusion
  1188.1 4.4 convolution_convert_fusion.1
  1201.0 33.4 %reduce-scatter.37.cloned.1.call-done = f32[64,128]{1,0:T(8,128)} async-done(((f32[512,128]{1,0:T(8,128)}), f32[64,128]{1,0:T(8,128)}) %reduce-scatter.37.cloned.1.call-update) | async-done | bytes 32784
  1240.6 60.2 %reduce-scatter.31.cloned.1.call-done = f32[64,2,192]{2,0,1:T(8,128)} async-done(((f32[512,2,192]{2,0,1:T(8,128)}), f32[64,2,192]{2,0,1:T(8,128)}) %reduce-scatter.31.cloned.1.call-update) | async-done | bytes 98320 | tf_op jit(solution)/shard_map/reduce_scatter | solution.py:139
  1308.0 38.9 %reduce-scatter.29.cloned.1.call-done = bf16[1024,512]{1,0:T(8,128)(2,1)} async-done(((bf16[4096,512]{1,0:T(8,128)(2,1)}), bf16[1024,512]{1,0:T(8,128)(2,1)}) %reduce-scatter.29.cloned.1.call-update) | async-done | bytes 1048592 | tf_op jit(solution)/shard_map/reduce_scatter | solution.py:254
  1346.9 47.0 %reduce-scatter.25.cloned.1.call-done = bf16[1024,512]{1,0:T(8,128)(2,1)} async-done(((bf16[4096,512]{1,0:T(8,128)(2,1)}), bf16[1024,512]{1,0:T(8,128)(2,1)}) %reduce-scatter.25.cloned.1.call-update) | async-done | bytes 1048592 | tf_op jit(solution)/shard_map/reduce_scatter | solution.py:254
  1393.9 4.2 fusion.204
  1405.2 39.8 %all-reduce = (f32[4]{0:T(128)}, f32[4]{0:T(128)}, f32[6,512]{1,0:T(8,128)}) all-reduce(f32[4]{0:T(128)} %pad_maximum_fusion.8, f32[4]{0:T(128)} %pad_maximum_fusion.7, f32[6,512]{1,0:T(8,128)} %add.375), channel_id=1, replica_groups=mesh['dp'=8,'tensor'=4] {'dp','tensor'}, use_global_device_ids=true, to_apply=%region_71.72 | all-reduce | flops 3080 | bytes 24640 | tf_op jit(solution)/shard_map/psum | solution.py:304
  1451.3 4.2 fusion.220
  (1121 shorter events, 577.0 us)
Async XLA Ops:
  7.2 73.2 %all-gather.13.cloned.1.call-start = ((), (), s32[]{:S(2)}) async-start(), calls=%async_computation.16 | async-start | bytes 5242880 | tf_op jit(solution)/shard_map/all_gather | solution.py:195
  11.1 36.3 %copy-start.30 = (f32[64,2,192]{2,1,0:T(2,128)S(1)}, f32[64,2,192]{2,1,0:T(2,128)}, u32[]{:S(2)}) copy-start(f32[64,2,192]{2,1,0:T(2,128)} %param.29) | copy-start | bytes 294916
  13.0 66.8 %copy-start.67 = (s32[2,4,4]{2,1,0:T(4,128)S(1)}, s32[2,4,4]{2,1,0:T(4,128)}, u32[]{:S(2)}) copy-start(s32[2,4,4]{2,1,0:T(4,128)} %param.28) | copy-start | bytes 388
  13.0 74.2 %all-gather.9.cloned.1.call-start = ((), (), s32[]{:S(2)}) async-start(), calls=%async_computation.12 | async-start | bytes 5242880 | tf_op jit(solution)/shard_map/all_gather | solution.py:195
  13.8 354.8 %reduce-scatter.15.cloned.1.call-start = ((), (), s32[]{:S(2)}) async-start(), calls=%async_computation.13 | async-start | bytes 10485760 | tf_op jit(solution)/shard_map/reduce_scatter | solution.py:201
  79.8 7.4 copy-start.26
  230.7 210.4 %reduce-scatter.19.cloned.1.call-start = ((), (), s32[]{:S(2)}) async-start(), calls=%async_computation.17 | async-start | bytes 10485760 | tf_op jit(solution)/shard_map/reduce_scatter | solution.py:201
  368.6 72.6 %copy-start.61 = (f32[1,512]{1,0:T(1,128)S(1)}, f32[1,512]{1,0:T(1,128)}, u32[]{:S(2)}) copy-start(f32[1,512]{1,0:T(1,128)} %get-tuple-element.546) | copy-start | bytes 6148
  368.6 144.6 %all-gather.11.cloned.1.call-start = ((), (), s32[]{:S(2)}) async-start(), calls=%async_computation.14 | async-start | bytes 5242880 | tf_op jit(solution)/shard_map/all_gather | solution.py:210
  446.9 73.9 %all-gather.17.cloned.1.call-start = ((), (), s32[]{:S(2)}) async-start(), calls=%async_computation.20 | async-start | bytes 5242880 | tf_op jit(solution)/shard_map/all_gather | solution.py:224
  449.3 104.2 %all-gather.15.cloned.1.call-start = ((), (), s32[]{:S(2)}) async-start(), calls=%async_computation.18 | async-start | bytes 5242880 | tf_op jit(solution)/shard_map/all_gather | solution.py:210
  450.0 177.4 %reduce-scatter.23.cloned.1.call-start = ((), (), s32[]{:S(2)}) async-start(), calls=%async_computation.21 | async-start | bytes 10485760 | tf_op jit(solution)/shard_map/reduce_scatter | solution.py:233
  536.2 138.5 %reduce-scatter.21.cloned.1.call-start = ((), (), s32[]{:S(2)}) async-start(), calls=%async_computation.19 | async-start | bytes 5242880 | tf_op jit(solution)/shard_map/reduce_scatter | solution.py:213
  567.5 154.2 %reduce-scatter.17.cloned.1.call-start = ((), (), s32[]{:S(2)}) async-start(), calls=%async_computation.15 | async-start | bytes 5242880 | tf_op jit(solution)/shard_map/reduce_scatter | solution.py:213
  575.0 52.4 %copy-start.5 = (f32[1024,512]{1,0:T(8,128)S(1)}, f32[1024,512]{1,0:T(8,128)}, u32[]{:S(2)}) copy-start(f32[1024,512]{1,0:T(8,128)} %copy-done.4) | copy-start | bytes 6291460
  575.1 187.5 %all-gather.21.cloned.1.call-start = ((), (), s32[]{:S(2)}) async-start(), calls=%async_computation.24 | async-start | bytes 5242880 | tf_op jit(solution)/shard_map/all_gather | solution.py:224
  727.9 121.6 %reduce-scatter.27.cloned.1.call-start = ((), (), s32[]{:S(2)}) async-start(), calls=%async_computation.25 | async-start | bytes 10485760 | tf_op jit(solution)/shard_map/reduce_scatter | solution.py:233
  777.9 71.6 %copy-start.3 = (f32[1024,512]{1,0:T(8,128)S(1)}, f32[1024,512]{1,0:T(8,128)}, u32[]{:S(2)}) copy-start(f32[1024,512]{1,0:T(8,128)} %copy-done.2) | copy-start | bytes 6291460
  777.9 74.9 %copy-start.25 = (bf16[1024,512]{1,0:T(8,128)(2,1)S(1)}, bf16[1024,512]{1,0:T(8,128)(2,1)}, u32[]{:S(2)}) copy-start(bf16[1024,512]{1,0:T(8,128)(2,1)} %reduce-scatter.21.cloned.1.call-done) | copy-start | bytes 3145732
  778.0 115.5 %all-gather.19.cloned.1.call-start = ((), (), s32[]{:S(2)}) async-start(), calls=%async_computation.22 | async-start | bytes 5242880 | tf_op jit(solution)/shard_map/all_gather | solution.py:241
  852.9 4.0 copy-start.10
  858.9 70.5 %all-gather.23.cloned.1.call-start = ((), (), s32[]{:S(2)}) async-start(), calls=%async_computation.26 | async-start | bytes 5242880 | tf_op jit(solution)/shard_map/all_gather | solution.py:241
  859.5 333.1 %reduce-scatter.35.cloned.1.call-start = ((), (), s32[]{:S(2)}) async-start(), calls=%async_computation.30 | async-start | bytes 1179648 | tf_op jit(solution)/shard_map/reduce_scatter | solution.py:142
  859.7 6.0 copy-start.68
  859.7 6.2 copy-start.70
  869.3 326.5 %reduce-scatter.33.cloned.1.call-start = ((), (), s32[]{:S(2)}) async-start(), calls=%async_computation.29 | async-start | bytes 1179648 | tf_op jit(solution)/shard_map/reduce_scatter | solution.py:141
  869.3 6.0 copy-start.8
  869.3 6.0 copy-start.18
  878.7 355.7 %reduce-scatter.37.cloned.1.call-start = ((), (), s32[]{:S(2)}) async-start(), calls=%async_computation.31 | async-start | bytes 294912
  1046.2 108.9 %copy-start.13 = (bf16[16,8,4,1024]{3,1,2,0:T(8,128)(2,1)S(1)}, bf16[16,8,4,1024]{3,1,2,0:T(8,128)(2,1)}, u32[]{:S(2)}) copy-start(bf16[16,8,4,1024]{3,1,2,0:T(8,128)(2,1)} %copy-done.12) | copy-start | bytes 3145732
  1155.2 3.7 copy-start.15
  1158.9 3.8 copy-start.17
  1172.1 128.8 %reduce-scatter.31.cloned.1.call-start = ((), (), s32[]{:S(2)}) async-start(), calls=%async_computation.28 | async-start | bytes 1179648 | tf_op jit(solution)/shard_map/reduce_scatter | solution.py:139
  1172.4 5.7 copy-start.23
  1181.5 165.5 %reduce-scatter.29.cloned.1.call-start = ((), (), s32[]{:S(2)}) async-start(), calls=%async_computation.27 | async-start | bytes 5242880 | tf_op jit(solution)/shard_map/reduce_scatter | solution.py:254
  1187.8 206.1 %reduce-scatter.25.cloned.1.call-start = ((), (), s32[]{:S(2)}) async-start(), calls=%async_computation.23 | async-start | bytes 5242880 | tf_op jit(solution)/shard_map/reduce_scatter | solution.py:254
  1192.5 5.6 copy-start.24
  1192.5 108.4 %copy-start.31 = (f32[64,2,192]{2,1,0:T(2,128)S(1)}, f32[64,2,192]{2,1,0:T(2,128)}, u32[]{:S(2)}) copy-start(f32[64,2,192]{2,1,0:T(2,128)} %param.29) | copy-start | bytes 294916
  1198.1 195.8 %copy-start.1 = (bf16[2,1024,512]{2,1,0:T(8,128)(2,1)S(1)}, bf16[2,1024,512]{2,1,0:T(8,128)(2,1)}, u32[]{:S(2)}) copy-start(bf16[2,1024,512]{2,1,0:T(8,128)(2,1)} %param.26) | copy-start | bytes 6291460
  1198.1 195.8 %copy-start.51 = (f32[1024]{0:T(1024)S(1)}, f32[1024]{0:T(1024)}, u32[]{:S(2)}) copy-start(f32[1024]{0:T(1024)} %copy-done.50) | copy-start | bytes 12292
  1198.1 195.8 %copy-start.53 = (f32[1024]{0:T(1024)S(1)}, f32[1024]{0:T(1024)}, u32[]{:S(2)}) copy-start(f32[1024]{0:T(1024)} %copy-done.52) | copy-start | bytes 12292
  1198.1 195.8 %copy-start.57 = (f32[1024]{0:T(1024)S(1)}, f32[1024]{0:T(1024)}, u32[]{:S(2)}) copy-start(f32[1024]{0:T(1024)} %copy-done.56) | copy-start | bytes 12292
  1198.1 195.8 %copy-start.59 = (f32[1024]{0:T(1024)S(1)}, f32[1024]{0:T(1024)}, u32[]{:S(2)}) copy-start(f32[1024]{0:T(1024)} %copy-done.58) | copy-start | bytes 12292
  1346.9 104.4 %copy-start.22 = (bf16[1024,512]{1,0:T(8,128)(2,1)S(1)}, bf16[1024,512]{1,0:T(8,128)(2,1)}, u32[]{:S(2)}) copy-start(bf16[1024,512]{1,0:T(8,128)(2,1)} %reduce-scatter.29.cloned.1.call-done) | copy-start | bytes 3145732
  1455.6 3.9 copy-start.38
  1455.6 3.8 copy-start.39
  1455.6 4.6 copy-start.40
  1455.6 4.6 copy-start.41
  (43 other events, 111.8 us)
Sparse Core Ops, SparseCore 0:
  13.1 37.1 all-gather.12
  52.5 34.4 all-gather.8
  230.8 72.4 reduce-scatter.14
  368.7 72.3 reduce-scatter.18
  447.0 34.4 all-gather.10
  482.9 34.4 all-gather.16
  519.0 34.4 all-gather.14
  556.1 71.3 reduce-scatter.22
  630.0 44.5 reduce-scatter.20
  677.0 44.5 reduce-scatter.16
  728.0 34.4 all-gather.20
  778.1 71.3 reduce-scatter.26
  859.0 34.4 all-gather.18
  894.9 34.4 all-gather.22
  932.6 64.2 reduce-scatter.34
  1000.2 63.2 reduce-scatter.32
  1172.2 62.0 reduce-scatter.36
  1237.6 63.1 reduce-scatter.30
  1303.4 43.4 reduce-scatter.28
  1349.3 44.5 reduce-scatter.24
where the time goes:
time: 1480 us; the launch traced here: 1470 us
  waiting for transfers between devices  565 us (38%)
  matrix products  269 us (18%)
  local copies, waits for them, and re-layouts  228 us (15%)
  other arithmetic  216 us (15%)
  blocking collectives  167 us (11%)
  between operations  18.1 us (1%)
    reduce_scatter x2, waiting for transfers between devices, on_device(): lax.psum_scatter(jnp.einsum('rf,df->rd', grad_up, up_w, preferred_element...  123 us
    reduce_scatter x2, waiting for transfers between devices, on_device(): lax.psum_scatter(jnp.dot(act, down_w, preferred_element_type=jnp.float32)...  90.9 us
    reduce_scatter x2, waiting for transfers between devices, on_device(): lax.psum_scatter(jnp.einsum('re,de->rd', grad_projected, in_mat, preferre...  85.9 us
    reduce_scatter x2, waiting for transfers between devices, on_device(): lax.psum_scatter(jnp.dot(mixed_rows, out_mat, preferred_element_type=jnp....  72.5 us
    reduce_scatter x1, waiting for transfers between devices, reduce_grads(): lax.psum_scatter(local_grads[0], 'dp', scatter_dimension=0, tiled=True)  60.2 us
    dot_general x32, matrix products, head_scores(): jnp.einsum('qd,kd->qk', queries, keys_rot, preferred_element_type=jnp.flo...  53.3 us
    all_gather x2, waiting for transfers between devices, on_device(): grad_branch_all = lax.all_gather(grad_branch, 'tensor', axis=0, tiled=True)  44.6 us
    psum x1, blocking collectives, on_device(): lax.psum(jnp.stack([jnp.sum(update * update) for update in updates]), ('d...  39.8 us
  transfers between devices with their start and end apart: 20, of which 13 were waited for; matrix products, arithmetic and copies ran while one was open for 34% of the time, Pallas kernels for 0%

commit v1 on v0

v1 whole, which is shorter than its diff:
```python
import functools
import math

import jax
import jax.numpy as jnp
from jax import lax
from jax.experimental import pallas as pl
from jax.experimental.pallas import tpu as pltpu
from jax.sharding import PartitionSpec as P

D = 512
HEADS = 8
HEAD_DIM = 64
FF = 2048
PAIRS = HEADS // 2
WINDOW = 250
LEN = 1024
CLIPS = 4
MICRO = 2
STEP = 3

BQ = 256
MLP_ROWS = 256
VMEM_LIMIT = 62 * 1024 * 1024

beta_first = 0.5
beta_second = 0.5
adam_eps = 1e-06
decay_rate = 0.01
learn_rate = 0.3

NT = (((1,), (1,)), ((), ()))
NN = (((1,), (0,)), ((), ()))
TN = (((0,), (0,)), ((), ()))


def dot(a, b, dims=NN):
    return lax.dot_general(a, b, dims, preferred_element_type=jnp.float32)


def norm_parts(rows):
    mean = jnp.mean(rows, -1, keepdims=True)
    centred = rows - mean
    inverse = lax.rsqrt(jnp.mean(centred * centred, -1, keepdims=True) + 1e-05)
    return centred * inverse, inverse


def norm_back(scaled, normal, inverse):
    return inverse * (
        scaled
        - jnp.mean(scaled, -1, keepdims=True)
        - normal * jnp.mean(scaled * normal, -1, keepdims=True)
    )


def lane_ids(shape):
    return lax.broadcasted_iota(jnp.int32, shape, len(shape) - 1)


def swap_pairs(rows):
    even = (lane_ids(rows.shape) & 1) == 0
    return jnp.where(even, pltpu.roll(rows, 127, 1), pltpu.roll(rows, 1, 1))


def run_starts(lengths_ref, bucket, position):
    end0 = lengths_ref[bucket, 0]
    end1 = end0 + lengths_ref[bucket, 1]
    end2 = end1 + lengths_ref[bucket, 2]
    start = jnp.where(position >= end0, end0, 0)
    start = jnp.where(position >= end1, end1, start)
    return jnp.where(position >= end2, end2, start), position < end2


def block_bias(lengths_ref, bucket, first_row, first_key, keys):
    position = first_row + lax.broadcasted_iota(jnp.int32, (BQ, 1), 0)
    start, _ = run_starts(lengths_ref, bucket, position)
    lowest = jnp.maximum(start, position - (WINDOW - 1))
    key = first_key + lax.broadcasted_iota(jnp.int32, (BQ, keys), 1)
    return jnp.where((key >= lowest) & (key <= position), 0.0, -1e30)


def head_lanes(tile, head):
    return jnp.where((lane_ids(tile.shape) // HEAD_DIM) == head, tile, jnp.zeros_like(tile))


def forward_kernel(lengths_ref, x_ref, small_ref, cos_ref, sin_ref, in_ref, qkv_ref, mixed_ref, total_ref, enter_ref):
    bucket = pl.program_id(0)

    def project(chunk, carry):
        rows = pl.ds(pl.multiple_of(chunk * BQ, BQ), BQ)
        normal, _ = norm_parts(x_ref[0, rows, :].astype(jnp.float32))
        enter = (normal * small_ref[0:1, :] + small_ref[1:2, :]).astype(jnp.bfloat16)
        enter_ref[0, rows, :] = enter
        cosine = cos_ref[0, rows, :]
        sine = sin_ref[0, rows, :]
        for pair in range(PAIRS):
            part = dot(enter, in_ref[:, pair * 384 : pair * 384 + 384])
            for which in range(2):
                piece = part[:, which * 128 : which * 128 + 128]
                turned = piece * cosine + swap_pairs(piece) * sine
                if which == 0:
                    turned = turned * (HEAD_DIM**-0.5)
                qkv_ref[0, rows, pair * 384 + which * 128 : pair * 384 + which * 128 + 128] = turned.astype(jnp.bfloat16)
            qkv_ref[0, rows, pair * 384 + 256 : pair * 384 + 384] = part[:, 256:].astype(jnp.bfloat16)
        return carry

    lax.fori_loop(0, LEN // BQ, project, 0)

    def attend(first_row, first_key, keys):
        rows = pl.ds(first_row, BQ)
        key_rows = pl.ds(first_key, keys)
        bias = block_bias(lengths_ref, bucket, first_row, first_key, keys)
        for pair in range(PAIRS):
            base = pair * 384
            queries = qkv_ref[0, rows, base : base + 128]
            keys_rot = qkv_ref[0, key_rows, base + 128 : base + 256]
            values = qkv_ref[0, key_rows, base + 256 : base + 384]
            outs = []
            totals = []
            for head in range(2):
                scores = dot(head_lanes(queries, head), keys_rot, NT) + bias
                top = jnp.max(scores, -1, keepdims=True)
                powers = jnp.exp(scores - top)
                total = jnp.sum(powers, -1, keepdims=True)
                outs.append(dot(powers.astype(jnp.bfloat16), values) / total)
                totals.append(jnp.broadcast_to(top + jnp.log(total), (BQ, 128)))
            low = lane_ids((BQ, 128)) < HEAD_DIM
            mixed_ref[0, rows, pair * 128 : pair * 128 + 128] = jnp.where(low, outs[0], outs[1]).astype(jnp.bfloat16)
            total_ref[0, rows, pair * 128 : pair * 128 + 128] = jnp.where(low, totals[0], totals[1])

    attend(0, 0, BQ)

    def later(step, carry):
        first_row = pl.multiple_of(step * BQ, BQ)
        attend(first_row, pl.multiple_of(first_row - BQ, BQ), 2 * BQ)
        return carry

    lax.fori_loop(1, LEN // BQ, later, 0)


def mlp_kernel(
    lengths_ref, x_ref, cot_ref, mixed_ref, small_ref, out_ref, up_ref, down_ref,
    block_ref, act_ref, gup_ref, gmlp_ref, enter_ref, gy1_ref, gbranch_ref, gmixed_ref, sums_ref,
):
    bucket = pl.program_id(0)
    chunk = pl.program_id(1)

    @pl.when((bucket == 0) & (chunk == 0))
    def _():
        sums_ref[...] = jnp.zeros_like(sums_ref)

    small = [small_ref[row : row + 1, :] for row in range(6)]
    x = x_ref[0].astype(jnp.float32)
    branch = dot(mixed_ref[0], out_ref[...], NT)
    y_first = x + small[4] * branch
    normal, inverse = norm_parts(y_first)
    enter = (normal * small[2] + small[3]).astype(jnp.bfloat16)
    enter_ref[0] = enter
    position = chunk * MLP_ROWS + lax.broadcasted_iota(jnp.int32, (MLP_ROWS, 1), 0)
    _, valid = run_starts(lengths_ref, bucket, position)
    grad_y = jnp.where(valid, cot_ref[0].astype(jnp.float32), 0.0)
    grad_mlp = (small[5] * grad_y).astype(jnp.bfloat16)
    gmlp_ref[0] = grad_mlp
    mlp = jnp.zeros((MLP_ROWS, D), jnp.float32)
    grad_enter = jnp.zeros((MLP_ROWS, D), jnp.float32)
    for part in range(FF // 512):
        cols = slice(part * 512, part * 512 + 512)
        upval = dot(enter, up_ref[:, cols])
        grad_act = dot(grad_mlp, down_ref[:, cols])
        cumulative = 0.5 + 0.5 * lax.erf(upval * (1.0 / math.sqrt(2.0)))
        act = (upval * cumulative).astype(jnp.bfloat16)
        act_ref[0, :, cols] = act
        density = jnp.exp(-0.5 * upval * upval) * (1.0 / math.sqrt(2.0 * math.pi))
        grad_up = (grad_act * (cumulative + upval * density)).astype(jnp.bfloat16)
        gup_ref[0, :, cols] = grad_up
        mlp = mlp + dot(act, down_ref[:, cols], NT)
        grad_enter = grad_enter + dot(grad_up, up_ref[:, cols], NT)
    block_ref[0] = (y_first + small[5] * mlp).astype(jnp.bfloat16)
    grad_y_first = grad_y + norm_back(grad_enter * small[2], normal, inverse)
    gy1_ref[0] = grad_y_first
    grad_branch = (small[4] * grad_y_first).astype(jnp.bfloat16)
    gbranch_ref[0] = grad_branch
    gmixed_ref[0] = dot(grad_branch, out_ref[...]).astype(jnp.bfloat16)

    def fold(terms):
        return jnp.sum(terms.reshape(MLP_ROWS // 8, 8, D), 0)

    sums_ref[0] += fold(grad_enter * normal)
    sums_ref[1] += fold(grad_enter)
    sums_ref[2] += fold(grad_y_first * branch)
    sums_ref[3] += fold(grad_y * mlp)


def backward_kernel(lengths_ref, qkv_ref, mixed_ref, gmixed_ref, total_ref, cos_ref, sin_ref, gproj_ref, dk_ref, dv_ref):
    bucket = pl.program_id(0)

    def attend(first_row, first_key, keys):
        rows = pl.ds(first_row, BQ)
        key_rows = pl.ds(first_key, keys)
        bias = block_bias(lengths_ref, bucket, first_row, first_key, keys)
        low = lane_ids((BQ, 128)) < HEAD_DIM
        for pair in range(PAIRS):
            base = pair * 384
            queries = qkv_ref[0, rows, base : base + 128]
            keys_rot = qkv_ref[0, key_rows, base + 128 : base + 256]
            values = qkv_ref[0, key_rows, base + 256 : base + 384]
            grad = gmixed_ref[0, rows, pair * 128 : pair * 128 + 128]
            totals = total_ref[0, rows, pair * 128 : pair * 128 + 128]
            product = grad.astype(jnp.float32) * mixed_ref[0, rows, pair * 128 : pair * 128 + 128].astype(jnp.float32)
            grad_q = jnp.zeros((BQ, 128), jnp.float32)
            grad_k = jnp.zeros((keys, 128), jnp.float32)
            grad_v = jnp.zeros((keys, 128), jnp.float32)
            for head in range(2):
                query = head_lanes(queries, head)
                grad_head = head_lanes(grad, head)
                inner = jnp.sum(jnp.where(low == (head == 0), product, 0.0), -1, keepdims=True)
                total = totals[:, head * HEAD_DIM : head * HEAD_DIM + 1]
                attn = jnp.exp(dot(query, keys_rot, NT) + bias - total)
                grad_attn = dot(grad_head, values, NT)
                grad_scores = (attn * (grad_attn - inner)).astype(jnp.bfloat16)
                grad_v = grad_v + dot(attn.astype(jnp.bfloat16), grad_head, TN)
                grad_k = grad_k + dot(grad_scores, query, TN)
                grad_q = grad_q + dot(grad_scores, head_lanes(keys_rot, head))
            cosine = cos_ref[0, rows, :]
            sine = sin_ref[0, rows, :]
            grad_q = grad_q * (HEAD_DIM**-0.5)
            gproj_ref[0, rows, base : base + 128] = (grad_q * cosine - swap_pairs(grad_q) * sine).astype(jnp.bfloat16)
            lanes = slice(pair * 128, pair * 128 + 128)
            if keys > BQ:
                before = pl.ds(first_key, BQ)
                dk_ref[before, lanes] += grad_k[:BQ]
                dv_ref[before, lanes] += grad_v[:BQ]
                dk_ref[rows, lanes] = grad_k[BQ:]
                dv_ref[rows, lanes] = grad_v[BQ:]
            else:
                dk_ref[rows, lanes] = grad_k
                dv_ref[rows, lanes] = grad_v

    attend(0, 0, BQ)

    def later(step, carry):
        first_row = pl.multiple_of(step * BQ, BQ)
        attend(first_row, pl.multiple_of(first_row - BQ, BQ), 2 * BQ)
        return carry

    lax.fori_loop(1, LEN // BQ, later, 0)

    def finish(chunk, carry):
        rows = pl.ds(pl.multiple_of(chunk * BQ, BQ), BQ)
        cosine = cos_ref[0, rows, :]
        sine = sin_ref[0, rows, :]
        for pair in range(PAIRS):
            grad_k = dk_ref[rows, pair * 128 : pair * 128 + 128]
            turned = grad_k * cosine - swap_pairs(grad_k) * sine
            gproj_ref[0, rows, pair * 384 + 128 : pair * 384 + 256] = turned.astype(jnp.bfloat16)
            gproj_ref[0, rows, pair * 384 + 256 : pair * 384 + 384] = dv_ref[rows, pair * 128 : pair * 128 + 128].astype(jnp.bfloat16)
        return carry

    lax.fori_loop(0, LEN // BQ, finish, 0)


def whole(shape):
    return pl.BlockSpec(shape, lambda *ids: (0,) * len(shape))


def per_bucket(*shape):
    return pl.BlockSpec((1,) + shape, lambda b: (b, 0, 0))


def bf16(*shape):
    return jax.ShapeDtypeStruct(shape, jnp.bfloat16)


def f32(*shape):
    return jax.ShapeDtypeStruct(shape, jnp.float32)


SCALARS = pl.BlockSpec(memory_space=pltpu.SMEM)


def params(count):
    return pltpu.CompilerParams(dimension_semantics=("arbitrary",) * count, vmem_limit_bytes=VMEM_LIMIT)


def turn_tables(lengths):
    ends = jnp.cumsum(lengths, axis=1)
    position = jnp.arange(LEN, dtype=jnp.int32)
    passed = position[None, :, None] >= ends[:, None, : CLIPS - 1]
    start = jnp.max(jnp.where(passed, ends[:, None, : CLIPS - 1], 0), axis=2)
    offset = (position[None, :] - start).astype(jnp.float32)
    frequency = jnp.exp(jnp.arange(HEAD_DIM // 2, dtype=jnp.float32) * (-2.0 * math.log(10000.0) / HEAD_DIM))
    angles = offset[:, :, None] * frequency
    cosine = jnp.repeat(jnp.cos(angles), 2, axis=-1)
    sine = jnp.sin(angles)
    sine = jnp.stack([-sine, sine], axis=-1).reshape(cosine.shape)
    return jnp.concatenate([cosine, cosine], -1), jnp.concatenate([sine, sine], -1)


def attention_forward(lengths, x, small, cosine, sine, in_mat):
    count = x.shape[0]
    return pl.pallas_call(
        forward_kernel,
        grid=(count,),
        in_specs=[SCALARS, per_bucket(LEN, D), whole((6, D)), per_bucket(LEN, 128), per_bucket(LEN, 128), whole((D, 3 * D))],
        out_specs=[per_bucket(LEN, 3 * D), per_bucket(LEN, D), per_bucket(LEN, D), per_bucket(LEN, D)],
        out_shape=[bf16(count, LEN, 3 * D), bf16(count, LEN, D), f32(count, LEN, D), bf16(count, LEN, D)],
        compiler_params=params(1),
        name="attention_forward",
    )(lengths, x, small, cosine, sine, in_mat)


def mlp_both(lengths, x, cot, mixed, small, out_mat, up_mat, down_mat):
    count = x.shape[0]

    def chunked(width):
        return pl.BlockSpec((1, MLP_ROWS, width), lambda b, i: (b, i, 0))

    return pl.pallas_call(
        mlp_kernel,
        grid=(count, LEN // MLP_ROWS),
        in_specs=[SCALARS, chunked(D), chunked(D), chunked(D), whole((6, D)), whole((D, D)), whole((D, FF)), whole((D, FF))],
        out_specs=[chunked(D), chunked(FF), chunked(FF), chunked(D), chunked(D), chunked(D), chunked(D), chunked(D), whole((4, 8, D))],
        out_shape=[
            bf16(count, LEN, D), bf16(count, LEN, FF), bf16(count, LEN, FF), bf16(count, LEN, D), bf16(count, LEN, D),
            f32(count, LEN, D), bf16(count, LEN, D), bf16(count, LEN, D), f32(4, 8, D),
        ],
        compiler_params=params(2),
        name="mlp_both",
    )(lengths, x, cot, mixed, small, out_mat, up_mat, down_mat)


def attention_backward(lengths, qkv, mixed, gmixed, totals, cosine, sine):
    count = qkv.shape[0]
    return pl.pallas_call(
        backward_kernel,
        grid=(count,),
        in_specs=[SCALARS, per_bucket(LEN, 3 * D), per_bucket(LEN, D), per_bucket(LEN, D), per_bucket(LEN, D), per_bucket(LEN, 128), per_bucket(LEN, 128)],
        out_specs=per_bucket(LEN, 3 * D),
        out_shape=bf16(count, LEN, 3 * D),
        scratch_shapes=[pltpu.VMEM((LEN, D), jnp.float32), pltpu.VMEM((LEN, D), jnp.float32)],
        compiler_params=params(1),
        name="attention_backward",
    )(lengths, qkv, mixed, gmixed, totals, cosine, sine)


def on_device(
    frames, cotangent, clip_lengths, in_proj, out_proj, up_proj, down_proj, small_params,
    in_first, in_second, out_first, out_second, up_first, up_second, down_first, down_second,
    small_first, small_second,
):
    rows_here = frames.shape[1]
    own_buckets = rows_here // LEN
    first_bucket = lax.axis_index("tensor") * own_buckets
    lengths = lax.dynamic_slice_in_dim(clip_lengths, first_bucket, own_buckets, 1).reshape(-1, CLIPS)
    count = MICRO * own_buckets
    x = frames.reshape(count, LEN, D)
    cot = cotangent.reshape(count, LEN, D)
    tensor_size = lax.axis_size("tensor")
    dp_size = lax.axis_size("dp")
    depth = in_proj.shape[0]
    heads_here = in_proj.shape[1]
    ff_here = up_proj.shape[1]

    def column_major(out_like, down_like):
        return out_like.reshape(heads_here * HEAD_DIM, depth).T, down_like.T

    out_cols, down_cols = column_major(out_proj, down_proj)
    shard = jnp.concatenate([in_proj.reshape(depth, -1), out_cols, up_proj, down_cols], axis=1).astype(jnp.bfloat16)
    gathered = lax.all_gather(shard, ("dp", "tensor"), axis=0)
    gathered = gathered.reshape(dp_size, tensor_size, depth, shard.shape[1])
    gathered = jnp.moveaxis(gathered, 1, 2).reshape(D, tensor_size, shard.shape[1])
    edge0 = heads_here * 192
    edge1 = edge0 + heads_here * HEAD_DIM
    edge2 = edge1 + ff_here
    in_mat = gathered[:, :, :edge0].reshape(D, PAIRS, 2, 3, HEAD_DIM).transpose(0, 1, 3, 2, 4).reshape(D, 3 * D)
    out_mat = gathered[:, :, edge0:edge1].reshape(D, D)
    up_mat = gathered[:, :, edge1:edge2].reshape(D, FF)
    down_mat = gathered[:, :, edge2:].reshape(D, FF)

    cosine, sine = turn_tables(lengths)
    qkv, mixed, totals, enter1 = attention_forward(lengths, x, small_params, cosine, sine, in_mat)
    block_out, act, grad_up, grad_mlp, enter2, grad_y_first, grad_branch, grad_mixed, sums = mlp_both(
        lengths, x, cot, mixed, small_params, out_mat, up_mat, down_mat
    )

    def weight_grad(left, right):
        return dot(left.reshape(-1, left.shape[-1]), right.reshape(-1, right.shape[-1]), TN).astype(jnp.bfloat16)

    grad_down = weight_grad(grad_mlp, act)
    grad_upw = weight_grad(enter2, grad_up)
    grad_out = weight_grad(grad_branch, mixed)
    grad_proj = attention_backward(lengths, qkv, mixed, grad_mixed, totals, cosine, sine)
    grad_in = weight_grad(enter1, grad_proj)
    grad_in = grad_in.reshape(D, PAIRS, 3, 2, HEAD_DIM).transpose(0, 1, 3, 2, 4)

    def by_owner(mat):
        return jnp.moveaxis(mat.reshape(dp_size, depth, tensor_size, -1), 2, 1)

    stacked = jnp.concatenate([by_owner(grad_in), by_owner(grad_out), by_owner(grad_upw), by_owner(grad_down)], axis=-1)
    owned = lax.psum_scatter(
        stacked.reshape(dp_size * tensor_size, depth, -1), ("dp", "tensor"), scatter_dimension=0, tiled=False
    ).astype(jnp.float32)

    grad_enter1 = dot(grad_proj.reshape(-1, 3 * D), in_mat, NT).reshape(count, LEN, D)
    normal1, inverse1 = norm_parts(x.astype(jnp.float32))
    input_grad = (grad_y_first + norm_back(grad_enter1 * small_params[0], normal1, inverse1)).astype(jnp.bfloat16)
    late = jnp.sum(sums, axis=1)
    small_terms = jnp.stack(
        [jnp.sum(grad_enter1 * normal1, (0, 1)), jnp.sum(grad_enter1, (0, 1)), late[0], late[1], late[2], late[3]]
    )

    grads = (
        owned[:, :edge0].reshape(in_proj.shape),
        owned[:, edge0:edge1].T.reshape(out_proj.shape),
        owned[:, edge1:edge2],
        owned[:, edge2:].T,
    )
    weights_in = (in_proj, out_proj, up_proj, down_proj)
    firsts = (in_first, out_first, up_first, down_first)
    seconds = (in_second, out_second, up_second, down_second)
    own_squares = jnp.stack([jnp.sum(weight * weight) for weight in weights_in])
    small_grad, weight_squares = lax.psum((small_terms, own_squares), ("dp", "tensor"))
    new_firsts = []
    new_seconds = []
    updates = []
    for weight, gradient, first, second in zip(weights_in, grads, firsts, seconds):
        first = beta_first * first + (1.0 - beta_first) * gradient
        second = beta_second * second + (1.0 - beta_second) * gradient * gradient
        update = (
            first / (1.0 - beta_first**STEP) / (jnp.sqrt(second / (1.0 - beta_second**STEP)) + adam_eps)
            + decay_rate * weight
        )
        new_firsts.append(first)
        new_seconds.append(second)
        updates.append(update)
    update_squares = lax.psum(jnp.stack([jnp.sum(update * update) for update in updates]), ("dp", "tensor"))
    trust_ratio = jnp.sqrt(weight_squares) * lax.rsqrt(update_squares + 1e-12)
    new_weights = [weights_in[index] - learn_rate * trust_ratio[index] * updates[index] for index in range(4)]
    small_first_new = beta_first * small_first + (1.0 - beta_first) * small_grad
    small_second_new = beta_second * small_second + (1.0 - beta_second) * small_grad * small_grad
    small_update = (
        small_first_new / (1.0 - beta_first**STEP) / (jnp.sqrt(small_second_new / (1.0 - beta_second**STEP)) + adam_eps)
        + decay_rate * small_params
    )
    small_weight_sq = jnp.sum(small_params * small_params, axis=1, keepdims=True)
    small_update_sq = jnp.sum(small_update * small_update, axis=1, keepdims=True)
    small_new = small_params - learn_rate * jnp.sqrt(small_weight_sq) * lax.rsqrt(small_update_sq + 1e-12) * small_update
    norms = jnp.stack(
        [
            jnp.concatenate([jnp.sqrt(weight_squares), jnp.sqrt(small_weight_sq).reshape(-1)]),
            jnp.concatenate([jnp.sqrt(update_squares), jnp.sqrt(small_update_sq).reshape(-1)]),
        ]
    )
    outputs = [block_out.reshape(frames.shape), input_grad.reshape(frames.shape)]
    for new, first, second in zip(new_weights, new_firsts, new_seconds):
        outputs += [new, first, second, new.astype(jnp.bfloat16)]
    return tuple(outputs + [small_grad, small_new, small_first_new, small_second_new, norms])


def solution(mesh):
    rows = P(None, ("dp", "tensor"), None)
    in_spec = P("dp", "tensor", None)
    out_spec = P("tensor", None, "dp")
    up_spec = P("dp", "tensor")
    down_spec = P("tensor", "dp")
    return jax.shard_map(
        on_device,
        mesh=mesh,
        in_specs=(
            rows, rows, P(None, "dp", None), in_spec, out_spec, up_spec, down_spec, P(),
            in_spec, in_spec, out_spec, out_spec, up_spec, up_spec, down_spec, down_spec, P(), P(),
        ),
        out_specs=(rows, rows) + (in_spec,) * 4 + (out_spec,) * 4 + (up_spec,) * 4 + (down_spec,) * 4 + (P(),) * 5,
        check_vma=False,
    )
```

time: 1480 us -> 462 us (0.31)
  waiting for transfers between devices: 565 us -> 163 us
  matrix products: 269 us -> 36.7 us
  local copies, waits for them, and re-layouts: 228 us -> 45.7 us
  other arithmetic: 216 us -> 46.7 us
  blocking collectives: 167 us -> 39.9 us
  Pallas kernels: 0 us -> 103 us
    reduce_scatter x11 -> x1, waiting for transfers between devices: 433 us -> 102 us  [on_device(): lax.psum_scatter(stacked.reshape(dp_size * tensor_size, depth, -1), ('dp'...]
    dot_general x136 -> x5, matrix products: 269 us -> 36.7 us  [dot(): return lax.dot_general(a, b, dims, preferred_element_type=jnp.float32)]
    all_gather x4 -> x0, blocking collectives: 127 us -> none  [the longest x1 32.6 us: on_device(): lax.all_gather(copies[1], 'dp', axis=2, tiled=True)]
    pallas_call x0 -> x3, Pallas kernels: none -> 103 us  [the longest x1 36.4 us: attention_backward(): pl.pallas_call(backward_kernel, grid=(count,), in_specs=[SCALARS, per_buc...]
    another operation x100 -> x0, local copies, waits for them, and re-layouts: 42.2 us -> none
    reduce_sum x92 -> x3, other arithmetic: 43 us -> 1.4 us  [the longest x1 1.01 us: norm_parts(): inverse = lax.rsqrt(jnp.mean(centred * centred, -1, keepdims=True) + 1e-05)]
    dynamic_update_slice x32 -> x0, other arithmetic: 39.8 us -> none  [the longest x16 27.1 us: on_device(): lax.map(attend_forward, (head_items, item_sizes))]
    squeeze x48 -> x0, local copies, waits for them, and re-layouts: 39.3 us -> none  [the longest x32 20 us: rotate(): paired = values_in.reshape(values_in.shape[:-1] + (half_dim, 2))]
  transfers between devices with their start and end apart: 20 -> 2, of which waited for: 13 -> 2; matrix products, arithmetic and copies ran while one was open for 34% -> 5% of each run, Pallas kernels for 0% -> 0%
where the time goes in v1:
time: 462 us; the launch traced here: 453 us
  waiting for transfers between devices  163 us (35%)
  Pallas kernels  103 us (22%)
  other arithmetic  46.7 us (10%)
  local copies, waits for them, and re-layouts  45.7 us (10%)
  blocking collectives  39.9 us (9%)
  matrix products  36.7 us (8%)
  between operations  17.5 us (4%)
    reduce_scatter x1, waiting for transfers between devices, on_device(): lax.psum_scatter(stacked.reshape(dp_size * tensor_size, depth, -1), ('dp'...  102 us
    all_gather x1, waiting for transfers between devices, on_device(): gathered = lax.all_gather(shard, ('dp', 'tensor'), axis=0)  61.3 us
    psum x1, blocking collectives, on_device(): lax.psum(jnp.stack([jnp.sum(update * update) for update in updates]), ('d...  39.9 us
    dot_general x5, matrix products, dot(): return lax.dot_general(a, b, dims, preferred_element_type=jnp.float32)  36.7 us
    pallas_call x1, Pallas kernels, attention_backward(): pl.pallas_call(backward_kernel, grid=(count,), in_specs=[SCALARS, per_buc...  36.4 us
    pallas_call x1, Pallas kernels, mlp_both(): pl.pallas_call(mlp_kernel, grid=(count, LEN // MLP_ROWS), in_specs=[SCALA...  33.7 us
    pallas_call x1, Pallas kernels, attention_forward(): pl.pallas_call(forward_kernel, grid=(count,), in_specs=[SCALARS, per_buck...  32.6 us
    reshape x4, local copies, waits for them, and re-layouts, by_owner(): return jnp.moveaxis(mat.reshape(dp_size, depth, tensor_size, -1), 2, 1)  11.7 us
  transfers between devices with their start and end apart: 2, of which 2 were waited for; matrix products, arithmetic and copies ran while one was open for 5% of the time, Pallas kernels for 0%

profile of v1, /device:TPU:0, one launch (start us, length us, event | category | flops | bytes accessed | tf_op | source)
XLA Modules:
  0.0 452.6 jit_solution(10912562273204149854)
XLA Ops:
  7.3 1.7 multiply_reduce_fusion.6
  9.1 0.9 convert_bitcast_fusion
  10.0 0.9 convert_bitcast_fusion.1
  10.9 0.8 convert.21
  13.1 3.8 fusion.20
  17.5 3.5 multiply_cosine_fusion
  21.5 1.9 pad_maximum_fusion.1
  23.5 61.3 %all-gather.2.cloned.1.call-done = bf16[32,64,1536]{2,1,0:T(8,128)(2,1)} async-done(((bf16[1,64,1536]{2,1,0:T(8,128)(2,1)}), bf16[32,64,1536]{2,1,0:T(8,128)(2,1)}) %all-gather.2.cloned.1.call-update) | async-done | bytes 6291472 | tf_op jit(solution)/shard_map/all_gather | solution.py:369
  84.7 3.5 copy.143
  88.2 1.3 slice.62
  89.5 1.8 slice_bitcast_fusion
  91.3 0.9 copy_bitcast_fusion.out_ref
  92.1 2.6 copy.144
  94.7 2.7 copy.145
  97.4 2.6 copy.146.in_ref
  100.0 3.2 copy.167
  103.3 1.6 copy.168
  104.9 32.6 %attention_forward.1 = (bf16[2,1024,1536]{2,1,0:T(8,128)(2,1)}, bf16[2,1024,512]{2,1,0:T(8,128)(2,1)}, f32[2,1024,512]{2,1,0:T(8,128)}, bf16[2,1024,512]{2,1,0:T(8,128)(2,1)}) custom-call(s32[2,4]{1,0:T(2,128)} %bitcast.123, bf16[2,1024,512]{2,1,0:T(8,128)(2,1)} %x_ref.3, f32[6,512]{1,0:T(8,128)} %small_ref.3, f32[2,1024,128]{2,1,0:T(8,128)} %get-tuple-element.101.cos_ref, ...), custom_call_target="tpu_custom_call" | custom-call | tf_op jit(solution)/shard_map/attention_forward/pallas_call | solution.py:301
  137.4 33.7 %mlp_both.1 = (bf16[2,1024,512]{2,1,0:T(8,128)(2,1)}, bf16[2,1024,2048]{2,1,0:T(8,128)(2,1)}, bf16[2,1024,2048]{2,1,0:T(8,128)(2,1)}, bf16[2,1024,512]{2,1,0:T(8...) custom-call(s32[2,4]{1,0:T(2,128)} %bitcast.124, ...), custom_call_target="tpu_custom_call" | custom-call | tf_op jit(solution)/shard_map/mlp_both/pallas_call | solution.py:318
  171.1 36.4 %attention_backward.1 = bf16[2,1024,1536]{2,1,0:T(8,128)(2,1)} custom-call(s32[2,4]{1,0:T(2,128)} %bitcast.125, bf16[2,1024,1536]{2,1,0:T(8,128)(2,1)} %get-tuple-element.39.qkv_ref, bf16[2,1024,512]{2,1,0:T(8,128)(2,1)} %get-tuple-element.36.mixed_ref, bf16[2,1024,512]{2,1,0:T(8,128)(2,1)} %get-tuple-element.40.gmixed_ref, ...), custom_call_target="tpu_custom_call" | custom-call | tf_op jit(solution)/shard_map/attention_backward/pallas_call | solution.py:334
  207.5 6.9 %fusion.12 = bf16[512,1536]{1,0:T(8,128)(2,1)S(1)} fusion(bf16[2,1024,512]{2,1,0:T(8,128)(2,1)} %get-tuple-element.42, bf16[2,1024,1536]{2,1,0:T(8,128)(2,1)} %attention_backward.1), kind=kOutput, calls=%fused_computation.19 | convolution fusion | flops 3222011904 | bytes 9961472 | tf_op jit(solution)/shard_map/dot_general | solution.py:38
  215.1 1.3 copy.152
  216.4 3.9 reshape.263
  220.3 3.3 copy.156
  223.6 8.6 %bitcast_convert_fusion.1 = bf16[512,2048]{1,0:T(8,128)(2,1)S(1)} fusion(bf16[2,1024,512]{2,1,0:T(8,128)(2,1)} %get-tuple-element.44, bf16[2,1024,2048]{2,1,0:T(8,128)(2,1)} %get-tuple-element.45), kind=kOutput, calls=%fused_computation.16 | convolution fusion | flops 4296015872 | bytes 12582912 | tf_op jit(solution)/shard_map/dot_general | solution.py:38
  232.2 3.0 reshape.265
  235.2 9.9 %bitcast_convert_fusion = bf16[512,2048]{1,0:T(8,128)(2,1)} fusion(bf16[2,1024,512]{2,1,0:T(8,128)(2,1)} %get-tuple-element.46, bf16[2,1024,2048]{2,1,0:T(8,128)(2,1)} %get-tuple-element.47), kind=kOutput, calls=%fused_computation.15 | convolution fusion | flops 4296015872 | bytes 12582912 | tf_op jit(solution)/shard_map/dot_general | solution.py:38
  245.1 4.7 %reshape.266 = bf16[8,64,4,512]{3,2,1,0:T(4,128)(2,1)} reshape(bf16[512,2048]{1,0:T(8,128)(2,1)} %bitcast_convert_fusion) | data formatting | bytes 4194304 | tf_op jit(solution)/shard_map/reshape | solution.py:397
  249.8 2.9 fusion.13
  252.8 6.0 %pad_maximum_fusion = bf16[8,4,64,1536]{3,1,2,0:T(4,128)(2,1)S(1)} fusion(bf16[8,4,64,512]{3,1,2,0:T(4,128)(2,1)} %bitcast.110, bf16[8,4,64,512]{3,1,2,0:T(4,128)(2,1)} %bitcast.109, bf16[8,4,64,128]{3,1,2,0:T(4,128)(2,1)S(1)} %bitcast.116, bf16[8,4,64,384]{3,1,2,0:T(4,128)(2,1)} %copy.156), kind=kLoop, calls=%fused_computation | loop fusion | flops 25165824 | bytes 12582912 | tf_op jit(solution)/shard_map/concatenate | solution.py:399
  258.8 4.2 copy.157
  263.7 0.9 copy-done.2
  265.0 1.0 fusion.11
  266.1 8.5 %fusion.10 = (f32[512]{0:T(512)S(1)}, f32[2,1024]{1,0:T(2,128)S(1)}, f32[2,1024]{1,0:T(2,128)S(1)}, f32[512]{0:T(512)S(1)}, f32[2,1024,512]{2,1,0:T(8,128)}) fusion(bf16[2,1024,512]{2,1,0:T(8,128)(2,1)S(1)} %copy-done.2, f32[2,1024]{1,0:T(2,128)S(1)} %add_rsqrt_fusion, f32[2,1024]{1,0:T(2,128)S(1)} %broadcast_multiply_fusion.2, f32[512]{0:T(512)S(1)} %bitcast.126, ...), kind=kOutput, calls=%fused_computation.13 | convolution fusion | flops 3231706112 | bytes 14194688 | tf_op jit(solution)/shard_map/dot_general | solution.py:38
  274.7 102.1 %reduce-scatter.2.cloned.1.call-done = bf16[1,64,1536]{2,1,0:T(8,128)(2,1)} async-done(((bf16[32,64,1536]{2,1,0:T(8,128)(2,1)}), bf16[1,64,1536]{2,1,0:T(8,128)(2,1)}) %reduce-scatter.2.cloned.1.call-update) | async-done | bytes 196624 | tf_op jit(solution)/shard_map/reduce_scatter | solution.py:400
  376.7 1.0 bitcast_convert_fusion.2
  377.7 0.7 copy.165
  378.6 1.6 multiply_reduce_fusion.5
  380.3 2.4 multiply_reduce_fusion.4
  382.7 1.6 multiply_reduce_fusion.8
  384.3 2.7 multiply_reduce_fusion.3
  387.0 2.7 pad_maximum_fusion.7
  389.7 2.7 pad_maximum_fusion.8
  392.4 5.2 %fusion.9 = bf16[2,1024,512]{2,1,0:T(8,128)(2,1)} fusion(f32[2,1024,512]{2,1,0:T(8,128)} %get-tuple-element.38, bf16[2,1024,512]{2,1,0:T(8,128)(2,1)S(1)} %copy-done.2, f32[2,1024,512]{2,1,0:T(8,128)} %get-tuple-element.100, f32[2,1024]{1,0:T(2,128)S(1)} %broadcast_multiply_fusion, f32[2,1024]{1,0:T(2,128)S(1)} %broadcast_multiply_fusion.1, ...), kind=kLoop, calls=%fused_computation.12 | loop fusion | flops 10485760 | bytes 12617728 | tf_op jit(solution)/shard_map/convert_element_type | solution.py:406
  397.6 39.9 %all-reduce = (f32[4]{0:T(128)S(1)}, f32[4]{0:T(128)S(1)}, f32[6,512]{1,0:T(8,128)S(1)}) all-reduce(f32[4]{0:T(128)S(1)} %pad_maximum_fusion.8, f32[4]{0:T(128)S(1)} %pad_maximum_fusion.7, f32[6,512]{1,0:T(8,128)S(1)} %pad_maximum_fusion.5), channel_id=1, replica_groups=mesh['dp'=8,'tensor'=4] {'dp','tensor'}, use_global_device_ids=true, to_apply=%region_16.17 | all-reduce | flops 3080 | bytes 24640 | tf_op jit(solution)/shard_map/psum | solution.py:436
  441.7 0.8 fusion.25
  443.1 0.8 fusion.22
  443.9 0.8 fusion.23
  (84 shorter events, 7.6 us)
Async XLA Ops:
  7.2 5.5 %copy-start = (s32[2,4,4]{2,1,0:T(4,128)S(1)}, s32[2,4,4]{2,1,0:T(4,128)}, u32[]{:S(2)}) copy-start(s32[2,4,4]{2,1,0:T(4,128)} %param.20) | copy-start | bytes 388
  7.2 77.5 %all-gather.2.cloned.1.call-start = ((), (), s32[]{:S(2)}) async-start(), calls=%async_computation.1 | async-start | bytes 6488064 | tf_op jit(solution)/shard_map/all_gather | solution.py:369
  12.6 364.2 %reduce-scatter.2.cloned.1.call-start = ((), (), s32[]{:S(2)}) async-start(), calls=%async_computation.2 | async-start | bytes 6488064 | tf_op jit(solution)/shard_map/reduce_scatter | solution.py:400
  12.7 10.8 %copy-start.19 = (s32[2,1,4]{2,1,0:T(1,128)}, s32[2,1,4]{2,1,0:T(1,128)S(1)}, u32[]{:S(2)}) copy-start(s32[2,1,4]{2,1,0:T(1,128)S(1)} %constant_dynamic-slice_fusion) | copy-start | bytes 100
  245.1 4.7 %copy-start.3 = (bf16[2,1024,512]{2,1,0:T(8,128)(2,1)S(1)}, bf16[2,1024,512]{2,1,0:T(8,128)(2,1)}, u32[]{:S(2)}) copy-start(bf16[2,1024,512]{2,1,0:T(8,128)(2,1)} %get-tuple-element.36.mixed_ref) | copy-start | bytes 6291460
  263.0 0.7 copy-start.12
  263.0 1.6 copy-start.2
  263.0 3.0 copy-start.16
  266.1 112.5 %copy-start.6 = (f32[64,512]{1,0:T(8,128)S(1)}, f32[64,512]{1,0:T(8,128)}, u32[]{:S(2)}) copy-start(f32[64,512]{1,0:T(8,128)} %param.23) | copy-start | bytes 393220
  266.1 112.5 %copy-start.15 = (f32[64,512]{1,0:T(8,128)S(1)}, f32[64,512]{1,0:T(8,128)}, u32[]{:S(2)}) copy-start(f32[64,512]{1,0:T(8,128)} %param.30) | copy-start | bytes 393220
  266.1 114.2 %copy-start.5 = (f32[512,64]{0,1:T(8,128)S(1)}, f32[512,64]{0,1:T(8,128)}, u32[]{:S(2)}) copy-start(f32[512,64]{0,1:T(8,128)} %param.24) | copy-start | bytes 393220
  266.1 116.6 %copy-start.7 = (f32[2,64,64]{2,1,0:T(8,128)S(1)}, f32[2,64,64]{2,1,0:T(8,128)}, u32[]{:S(2)}) copy-start(f32[2,64,64]{2,1,0:T(8,128)} %param.22) | copy-start | bytes 98308
  266.1 118.2 %copy-start.4 = (f32[64,2,192]{2,1,0:T(2,128)S(1)}, f32[64,2,192]{2,1,0:T(2,128)}, u32[]{:S(2)}) copy-start(f32[64,2,192]{2,1,0:T(2,128)} %param.21) | copy-start | bytes 294916
  380.3 63.6 %copy-start.8 = (f32[64,512]{1,0:T(8,128)}, f32[64,512]{1,0:T(8,128)S(1)}, u32[]{:S(2)}) copy-start(f32[64,512]{1,0:T(8,128)S(1)} %get-tuple-element.80) | copy-start | bytes 393220
  380.3 63.6 %copy-start.9 = (f32[64,512]{1,0:T(8,128)}, f32[64,512]{1,0:T(8,128)S(1)}, u32[]{:S(2)}) copy-start(f32[64,512]{1,0:T(8,128)S(1)} %get-tuple-element.81) | copy-start | bytes 393220
  382.7 60.4 %copy-start.10 = (f32[512,64]{0,1:T(8,128)}, f32[512,64]{0,1:T(8,128)S(1)}, u32[]{:S(2)}) copy-start(f32[512,64]{0,1:T(8,128)S(1)} %get-tuple-element.82) | copy-start | bytes 393220
  384.3 60.3 %copy-start.13 = (f32[2,64,64]{2,1,0:T(8,128)}, f32[2,64,64]{2,1,0:T(8,128)S(1)}, u32[]{:S(2)}) copy-start(f32[2,64,64]{2,1,0:T(8,128)S(1)} %get-tuple-element.78) | copy-start | bytes 98308
  384.3 60.3 %copy-start.14 = (f32[2,64,64]{2,1,0:T(8,128)}, f32[2,64,64]{2,1,0:T(8,128)S(1)}, u32[]{:S(2)}) copy-start(f32[2,64,64]{2,1,0:T(8,128)S(1)} %get-tuple-element.79) | copy-start | bytes 98308
  392.3 48.4 %copy-start.20 = (f32[6,512]{1,0:T(8,128)S(1)}, f32[6,512]{1,0:T(8,128)}, u32[]{:S(2)}) copy-start(f32[6,512]{1,0:T(8,128)} %param.34) | copy-start | bytes 36868
  392.3 48.4 %copy-start.21 = (f32[6,512]{1,0:T(8,128)S(1)}, f32[6,512]{1,0:T(8,128)}, u32[]{:S(2)}) copy-start(f32[6,512]{1,0:T(8,128)} %param.35) | copy-start | bytes 36868
  392.3 50.8 %copy-start.11 = (f32[512,64]{0,1:T(8,128)S(1)}, f32[512,64]{0,1:T(8,128)}, u32[]{:S(2)}) copy-start(f32[512,64]{0,1:T(8,128)} %get-tuple-element.83) | copy-start | bytes 393220
  392.3 53.0 %copy-start.1 = (s32[2,4,4]{2,1,0:T(4,128)S(1)}, s32[2,4,4]{2,1,0:T(4,128)}, u32[]{:S(2)}) copy-start(s32[2,4,4]{2,1,0:T(4,128)} %param.20) | copy-start | bytes 388
  437.5 7.8 %copy-start.22 = (f32[6,512]{1,0:T(8,128)}, f32[6,512]{1,0:T(8,128)S(1)}, u32[]{:S(2)}) copy-start(f32[6,512]{1,0:T(8,128)S(1)} %get-tuple-element.63) | copy-start | bytes 36868
  440.9 4.4 copy-start.17
  440.9 4.4 copy-start.18
Sparse Core Ops, SparseCore 0:
  12.7 71.9 all-gather.1
  263.2 113.5 reduce-scatter.1

commit v2 on v1

v2 whole, which is shorter than its diff:
```python
import functools
import math

import jax
import jax.numpy as jnp
from jax import lax
from jax.experimental import pallas as pl
from jax.experimental.pallas import tpu as pltpu
from jax.sharding import PartitionSpec as P

D = 512
HEADS = 8
HEAD_DIM = 64
FF = 2048
PAIRS = HEADS // 2
WINDOW = 250
LEN = 1024
CLIPS = 4
MICRO = 2
STEP = 3

BQ = 256
MLP_ROWS = 256
VMEM_LIMIT = 62 * 1024 * 1024

beta_first = 0.5
beta_second = 0.5
adam_eps = 1e-06
decay_rate = 0.01
learn_rate = 0.3

NT = (((1,), (1,)), ((), ()))
NN = (((1,), (0,)), ((), ()))
TN = (((0,), (0,)), ((), ()))


def dot(a, b, dims=NN):
    return lax.dot_general(a, b, dims, preferred_element_type=jnp.float32)


def norm_parts(rows):
    mean = jnp.mean(rows, -1, keepdims=True)
    centred = rows - mean
    inverse = lax.rsqrt(jnp.mean(centred * centred, -1, keepdims=True) + 1e-05)
    return centred * inverse, inverse


def norm_back(scaled, normal, inverse):
    return inverse * (
        scaled
        - jnp.mean(scaled, -1, keepdims=True)
        - normal * jnp.mean(scaled * normal, -1, keepdims=True)
    )


def lane_ids(shape):
    return lax.broadcasted_iota(jnp.int32, shape, len(shape) - 1)


def swap_pairs(rows):
    even = (lane_ids(rows.shape) & 1) == 0
    return jnp.where(even, pltpu.roll(rows, 127, 1), pltpu.roll(rows, 1, 1))


def run_starts(lengths_ref, bucket, position):
    end0 = lengths_ref[bucket, 0]
    end1 = end0 + lengths_ref[bucket, 1]
    end2 = end1 + lengths_ref[bucket, 2]
    start = jnp.where(position >= end0, end0, 0)
    start = jnp.where(position >= end1, end1, start)
    return jnp.where(position >= end2, end2, start), position < end2


def block_bias(lengths_ref, bucket, first_row, first_key, keys):
    position = first_row + lax.broadcasted_iota(jnp.int32, (BQ, 1), 0)
    start, _ = run_starts(lengths_ref, bucket, position)
    lowest = jnp.maximum(start, position - (WINDOW - 1))
    key = first_key + lax.broadcasted_iota(jnp.int32, (BQ, keys), 1)
    return jnp.where((key >= lowest) & (key <= position), 0.0, -1e30)


def head_lanes(tile, head):
    return jnp.where((lane_ids(tile.shape) // HEAD_DIM) == head, tile, jnp.zeros_like(tile))


MESH = pl.DeviceIdType.MESH
HERE_DP = 8
HERE_TENSOR = 4
IN_W, OUT_W, FF_W = 384, 128, 512
SHARD_W = IN_W + OUT_W + 2 * FF_W
CORE, ALONG_Y, ALONG_X = "core", "y", "x"

GATHERED = (
    (0, 0, 32, IN_W, 0, "xy"),
    (0, 32, 32, IN_W, 0, "yx"),
    (1, 0, 64, OUT_W, IN_W, "xy"),
    (2, 0, 64, FF_W, IN_W + OUT_W, "xy"),
    (3, 0, 64, FF_W, IN_W + OUT_W + FF_W, "yx"),
)
SUMMED = (
    (1, 0, 64, OUT_W, "yx"),
    (2, 0, 64, FF_W, "yx"),
    (3, 0, 64, FF_W, "xy"),
    (0, 0, 32, IN_W, "xy"),
    (0, 32, 32, IN_W, "yx"),
)


class Place:
    def __init__(self):
        dp = lax.axis_index("dp")
        tensor = lax.axis_index("tensor")
        self.z, self.x = dp // 2, dp % 2
        self.y, self.c = tensor // 2, tensor % 2

    def device(self, dz=0, x=None, y=None, c=None):
        x = self.x if x is None else x
        y = self.y if y is None else y
        c = self.c if c is None else c
        return {"dp": (self.z + dz) % 4 * 2 + x, "tensor": y * 2 + c}

    def peers(self):
        return {
            CORE: self.device(c=1 - self.c),
            ALONG_Y: self.device(y=1 - self.y),
            ALONG_X: self.device(x=1 - self.x),
            1: self.device(dz=1),
            2: self.device(dz=2),
            3: self.device(dz=3),
        }


def tile_cols(tensor, width):
    return pl.ds(pl.multiple_of(tensor * width, 128), width)


def remote(source, target, send, recv, device):
    return pltpu.make_async_remote_copy(
        src_ref=source, dst_ref=target, send_sem=send, recv_sem=recv, device_id=device, device_id_type=MESH
    )


def meet(place):
    barrier = pltpu.get_barrier_semaphore()
    peers = place.peers()
    for device in peers.values():
        pl.semaphore_signal(barrier, inc=1, device_id=device, device_id_type=MESH)
    pl.semaphore_wait(barrier, len(peers))


def start_all(copies):
    for copy in copies:
        copy.start()


def arrive_all(copies):
    for copy in copies:
        copy.wait_recv()


def sent_all(copies):
    for copy in copies:
        copy.wait_send()


def gather_copies(index, stage, place, shard, weights, send, recv):
    weight, row, count, width, offset, order = GATHERED[index]
    full = weights[weight]
    rows = pl.ds(row, count)
    peers = place.peers()

    def copy(source, target, slot, peer):
        return remote(source, target, send.at[index, slot], recv.at[index, slot], peers[peer])

    def cols(y):
        return tile_cols(y * 2 + place.c, width)

    mine = cols(place.y)
    if stage == 0:
        return [
            copy(shard.at[rows, offset : offset + width], full.at[place.z, place.x, rows, mine], step - 1, step)
            for step in (1, 2, 3)
        ]
    if stage == 3:
        parts = [full.at[:, :, rows, cols(y)] for y in range(2)]
        return [copy(part, part, 6 + y, CORE) for y, part in enumerate(parts)]
    if stage == 1:
        part = full.at[:, place.x, rows, mine]
        return [copy(part, part, 3, ALONG_X if order == "xy" else ALONG_Y)]
    if order == "xy":
        part = full.at[:, :, rows, mine]
        return [copy(part, part, 4, ALONG_Y)]
    parts = [full.at[:, place.x, rows, cols(y)] for y in range(2)]
    return [copy(part, part, 4 + y, ALONG_X) for y, part in enumerate(parts)]


def project_rows(rows, enter, cosine, sine, weight, qkv_ref):
    for pair in range(PAIRS):
        part = dot(enter, weight(pair))
        for which in range(2):
            piece = part[:, which * 128 : which * 128 + 128]
            turned = piece * cosine + swap_pairs(piece) * sine
            if which == 0:
                turned = turned * (HEAD_DIM**-0.5)
            qkv_ref[0, rows, pair * 384 + which * 128 : pair * 384 + which * 128 + 128] = turned.astype(jnp.bfloat16)
        qkv_ref[0, rows, pair * 384 + 256 : pair * 384 + 384] = part[:, 256:].astype(jnp.bfloat16)


def attend_forward(lengths_ref, bucket, first_row, first_key, keys, qkv_ref, mixed_ref, total_ref):
    rows = pl.ds(first_row, BQ)
    key_rows = pl.ds(first_key, keys)
    bias = block_bias(lengths_ref, bucket, first_row, first_key, keys)
    for pair in range(PAIRS):
        base = pair * 384
        queries = qkv_ref[0, rows, base : base + 128]
        keys_rot = qkv_ref[0, key_rows, base + 128 : base + 256]
        values = qkv_ref[0, key_rows, base + 256 : base + 384]
        outs = []
        totals = []
        for head in range(2):
            scores = dot(head_lanes(queries, head), keys_rot, NT) + bias
            top = jnp.max(scores, -1, keepdims=True)
            powers = jnp.exp(scores - top)
            total = jnp.sum(powers, -1, keepdims=True)
            outs.append(dot(powers.astype(jnp.bfloat16), values) / total)
            totals.append(jnp.broadcast_to(top + jnp.log(total), (BQ, 128)))
        low = lane_ids((BQ, 128)) < HEAD_DIM
        mixed_ref[0, rows, pair * 128 : pair * 128 + 128] = jnp.where(low, outs[0], outs[1]).astype(jnp.bfloat16)
        total_ref[0, rows, pair * 128 : pair * 128 + 128] = jnp.where(low, totals[0], totals[1])


def enter_rows(x_ref, small_ref, rows, bucket=0):
    normal, _ = norm_parts(x_ref[bucket, rows, :].astype(jnp.float32))
    return (normal * small_ref[0:1, :] + small_ref[1:2, :]).astype(jnp.bfloat16)


def chunk_rows(chunk):
    return pl.ds(pl.multiple_of(chunk * BQ, BQ), BQ)


def forward_kernel(
    lengths_ref, x_ref, small_ref, cos_ref, sin_ref, *refs, alone
):
    bucket = pl.program_id(0)
    if alone:
        in_ref, qkv_ref, mixed_ref, total_ref, enter_ref = refs
    else:
        shard_ref, qkv_ref, mixed_ref, total_ref = refs[:4]
        kept = refs[4:8]
        full = refs[8:12]
        enter_ref, send, recv, own_sem, keep_sem = refs[12:]
        place = Place()

        def copies(which, stage):
            found = []
            for index in which:
                found += gather_copies(index, stage, place, shard_ref, full, send, recv)
            return found

        def own_tiles():
            tiles = []
            for weight, width, offset in ((0, IN_W, 0), (1, OUT_W, IN_W), (2, FF_W, IN_W + OUT_W), (3, FF_W, IN_W + OUT_W + FF_W)):
                target = full[weight].at[place.z, place.x, :, tile_cols(place.y * 2 + place.c, width)]
                tiles.append(pltpu.make_async_copy(shard_ref.at[:, offset : offset + width], target, own_sem.at[weight]))
            return tiles

        def keeps():
            return [pltpu.make_async_copy(full[weight], kept[weight], keep_sem.at[weight]) for weight in range(4)]

        early, late = (0, 1), (2, 3, 4)

        @pl.when(bucket == 0)
        def _():
            meet(place)
            start_all(copies(early, 0))
            start_all(own_tiles())
            start_all(copies(late, 0))

    def normalise(chunk, carry):
        rows = chunk_rows(chunk)
        enter_ref[0, rows, :] = enter_rows(x_ref, small_ref, rows)
        return carry

    lax.fori_loop(0, LEN // BQ, normalise, 0)

    if not alone:

        @pl.when(bucket == 0)
        def _():
            for tile in own_tiles():
                tile.wait()
            for stage in range(3):
                arrive_all(copies(early, stage))
                start_all(copies(early, stage + 1))
            arrive_all(copies(early, 3))
            arrive_all(copies(late, 0))
            start_all(copies(late, 1))

        @pl.when(bucket == 1)
        def _():
            arrive_all(copies(late, 3))
            start_all(keeps())

    def weight(pair):
        cols = slice(pair * 384, pair * 384 + 384)
        return in_ref[:, cols] if alone else full[0][:, :, :, cols].reshape(D, 384)

    def project(chunk, carry):
        rows = chunk_rows(chunk)
        project_rows(rows, enter_ref[0, rows, :], cos_ref[0, rows, :], sin_ref[0, rows, :], weight, qkv_ref)
        return carry

    lax.fori_loop(0, LEN // BQ, project, 0)
    attend_forward(lengths_ref, bucket, 0, 0, BQ, qkv_ref, mixed_ref, total_ref)

    def later(step, carry):
        if not alone:

            @pl.when((bucket == 0) & (step == 1))
            def _():
                arrive_all(copies(late, 1))
                start_all(copies(late, 2))

            @pl.when((bucket == 0) & (step == 3))
            def _():
                arrive_all(copies(late, 2))
                start_all(copies(late, 3))

        first_row = pl.multiple_of(step * BQ, BQ)
        attend_forward(lengths_ref, bucket, first_row, pl.multiple_of(first_row - BQ, BQ), 2 * BQ, qkv_ref, mixed_ref, total_ref)
        return carry

    lax.fori_loop(1, LEN // BQ, later, 0)

    if not alone:

        @pl.when(bucket == 1)
        def _():
            for keep in keeps():
                keep.wait()
            for stage in range(4):
                sent_all(copies(early + late, stage))


def mlp_kernel(
    lengths_ref, x_ref, cot_ref, mixed_ref, small_ref, out_ref, up_ref, down_ref,
    block_ref, gy1_ref, gmixed_ref, sums_ref, gout_ref, gup_out_ref, gdown_ref,
    act_ref, gup_ref, keep_ref, enter_t, gmlp_t, gbranch_t,
):
    bucket = pl.program_id(0)
    chunk = pl.program_id(1)
    buckets = pl.num_programs(0)
    chunks = pl.num_programs(1)

    @pl.when((bucket == 0) & (chunk == 0))
    def _():
        sums_ref[...] = jnp.zeros_like(sums_ref)

    index = bucket * chunks + chunk
    rows = pl.ds(pl.multiple_of(index * MLP_ROWS, MLP_ROWS), MLP_ROWS)
    small = [small_ref[row : row + 1, :] for row in range(6)]
    x = x_ref[0].astype(jnp.float32)
    mixed = mixed_ref[0]
    keep_ref[rows, :] = mixed
    branch = dot(mixed, out_ref[...], NT)
    y_first = x + small[4] * branch
    normal, inverse = norm_parts(y_first)
    enter = (normal * small[2] + small[3]).astype(jnp.bfloat16)
    enter_t[:, rows] = enter.T
    position = chunk * MLP_ROWS + lax.broadcasted_iota(jnp.int32, (MLP_ROWS, 1), 0)
    _, valid = run_starts(lengths_ref, bucket, position)
    grad_y = jnp.where(valid, cot_ref[0].astype(jnp.float32), 0.0)
    grad_mlp = (small[5] * grad_y).astype(jnp.bfloat16)
    gmlp_t[:, rows] = grad_mlp.T
    mlp = jnp.zeros((MLP_ROWS, D), jnp.float32)
    grad_enter = jnp.zeros((MLP_ROWS, D), jnp.float32)
    for part in range(FF // 512):
        cols = slice(part * 512, part * 512 + 512)
        upval = dot(enter, up_ref[:, cols])
        grad_act = dot(grad_mlp, down_ref[:, cols])
        cumulative = 0.5 + 0.5 * lax.erf(upval * (1.0 / math.sqrt(2.0)))
        act = (upval * cumulative).astype(jnp.bfloat16)
        act_ref[rows, cols] = act
        density = jnp.exp(-0.5 * upval * upval) * (1.0 / math.sqrt(2.0 * math.pi))
        grad_up = (grad_act * (cumulative + upval * density)).astype(jnp.bfloat16)
        gup_ref[rows, cols] = grad_up
        mlp = mlp + dot(act, down_ref[:, cols], NT)
        grad_enter = grad_enter + dot(grad_up, up_ref[:, cols], NT)
    block_ref[0] = (y_first + small[5] * mlp).astype(jnp.bfloat16)
    grad_y_first = grad_y + norm_back(grad_enter * small[2], normal, inverse)
    gy1_ref[0] = grad_y_first
    grad_branch = (small[4] * grad_y_first).astype(jnp.bfloat16)
    gbranch_t[:, rows] = grad_branch.T
    gmixed_ref[0] = dot(grad_branch, out_ref[...]).astype(jnp.bfloat16)

    def fold(terms):
        return jnp.sum(terms.reshape(MLP_ROWS // 8, 8, D), 0)

    sums_ref[0] += fold(grad_enter * normal)
    sums_ref[1] += fold(grad_enter)
    sums_ref[2] += fold(grad_y_first * branch)
    sums_ref[3] += fold(grad_y * mlp)

    @pl.when(index == buckets * chunks - 1)
    def _():
        gout_ref[...] = dot(gbranch_t[...], keep_ref[...]).astype(jnp.bfloat16)

        def weight_grads(part, carry):
            cols = pl.ds(pl.multiple_of(part * 256, 256), 256)
            gup_out_ref[:, cols] = dot(enter_t[...], gup_ref[:, cols]).astype(jnp.bfloat16)
            gdown_ref[:, cols] = dot(gmlp_t[...], act_ref[:, cols]).astype(jnp.bfloat16)
            return carry

        lax.fori_loop(0, FF // 256, weight_grads, 0)


def attend_backward(
    lengths_ref, bucket, slot, first_row, first_key, keys, qkv_ref, mixed_ref, gmixed_ref, total_ref, cos_ref, sin_ref, gproj_ref, dk_ref, dv_ref
):
    rows = pl.ds(first_row, BQ)
    key_rows = pl.ds(first_key, keys)
    bias = block_bias(lengths_ref, bucket, first_row, first_key, keys)
    low = lane_ids((BQ, 128)) < HEAD_DIM
    for pair in range(PAIRS):
        base = pair * 384
        queries = qkv_ref[0, rows, base : base + 128]
        keys_rot = qkv_ref[0, key_rows, base + 128 : base + 256]
        values = qkv_ref[0, key_rows, base + 256 : base + 384]
        grad = gmixed_ref[0, rows, pair * 128 : pair * 128 + 128]
        totals = total_ref[0, rows, pair * 128 : pair * 128 + 128]
        product = grad.astype(jnp.float32) * mixed_ref[0, rows, pair * 128 : pair * 128 + 128].astype(jnp.float32)
        grad_q = jnp.zeros((BQ, 128), jnp.float32)
        grad_k = jnp.zeros((keys, 128), jnp.float32)
        grad_v = jnp.zeros((keys, 128), jnp.float32)
        for head in range(2):
            query = head_lanes(queries, head)
            grad_head = head_lanes(grad, head)
            inner = jnp.sum(jnp.where(low == (head == 0), product, 0.0), -1, keepdims=True)
            total = totals[:, head * HEAD_DIM : head * HEAD_DIM + 1]
            attn = jnp.exp(dot(query, keys_rot, NT) + bias - total)
            grad_attn = dot(grad_head, values, NT)
            grad_scores = (attn * (grad_attn - inner)).astype(jnp.bfloat16)
            grad_v = grad_v + dot(attn.astype(jnp.bfloat16), grad_head, TN)
            grad_k = grad_k + dot(grad_scores, query, TN)
            grad_q = grad_q + dot(grad_scores, head_lanes(keys_rot, head))
        cosine = cos_ref[0, rows, :]
        sine = sin_ref[0, rows, :]
        grad_q = grad_q * (HEAD_DIM**-0.5)
        gproj_ref[slot, rows, base : base + 128] = (grad_q * cosine - swap_pairs(grad_q) * sine).astype(jnp.bfloat16)
        lanes = slice(pair * 128, pair * 128 + 128)
        if keys > BQ:
            before = pl.ds(first_key, BQ)
            dk_ref[before, lanes] += grad_k[:BQ]
            dv_ref[before, lanes] += grad_v[:BQ]
            dk_ref[rows, lanes] = grad_k[BQ:]
            dv_ref[rows, lanes] = grad_v[BQ:]
        else:
            dk_ref[rows, lanes] = grad_k
            dv_ref[rows, lanes] = grad_v


def finish_keys(slot, cos_ref, sin_ref, gproj_ref, dk_ref, dv_ref):
    def finish(chunk, carry):
        rows = chunk_rows(chunk)
        cosine = cos_ref[0, rows, :]
        sine = sin_ref[0, rows, :]
        for pair in range(PAIRS):
            grad_k = dk_ref[rows, pair * 128 : pair * 128 + 128]
            turned = grad_k * cosine - swap_pairs(grad_k) * sine
            gproj_ref[slot, rows, pair * 384 + 128 : pair * 384 + 256] = turned.astype(jnp.bfloat16)
            gproj_ref[slot, rows, pair * 384 + 256 : pair * 384 + 384] = dv_ref[rows, pair * 128 : pair * 128 + 128].astype(jnp.bfloat16)
        return carry

    lax.fori_loop(0, LEN // BQ, finish, 0)


def backward_kernel(lengths_ref, qkv_ref, mixed_ref, gmixed_ref, total_ref, cos_ref, sin_ref, gproj_ref, dk_ref, dv_ref):
    bucket = pl.program_id(0)
    shared = (qkv_ref, mixed_ref, gmixed_ref, total_ref, cos_ref, sin_ref, gproj_ref, dk_ref, dv_ref)
    attend_backward(lengths_ref, bucket, 0, 0, 0, BQ, *shared)

    def later(step, carry):
        first_row = pl.multiple_of(step * BQ, BQ)
        attend_backward(lengths_ref, bucket, 0, first_row, pl.multiple_of(first_row - BQ, BQ), 2 * BQ, *shared)
        return carry

    lax.fori_loop(1, LEN // BQ, later, 0)
    finish_keys(0, cos_ref, sin_ref, gproj_ref, dk_ref, dv_ref)


def moments(weight, gradient, first, second):
    first = beta_first * first + (1.0 - beta_first) * gradient
    second = beta_second * second + (1.0 - beta_second) * gradient * gradient
    update = (
        first / (1.0 - beta_first**STEP) / (jnp.sqrt(second / (1.0 - beta_second**STEP)) + adam_eps)
        + decay_rate * weight
    )
    return first, second, update


def planes(which):
    if which == 0:
        return [(slice(None), head, slice(None)) for head in range(2)]
    if which == 1:
        return [(head, slice(None), slice(None)) for head in range(2)]
    return [(slice(None), slice(None))]


def total_of(values_in):
    return jnp.sum(jnp.sum(values_in, 1, keepdims=True), 0, keepdims=True)


def sums_of_squares(tables):
    lanes = lane_ids((1, 512))
    row = jnp.zeros((1, 512), jnp.float32)
    for which, squares in enumerate(tables):
        amount = sum((total_of(plane) for plane in squares[1:]), total_of(squares[0]))
        row = row + jnp.where(lanes == which, amount, 0.0)
    return row


class Everywhere:
    def __init__(self, place, held, got, last, send, recv):
        self.place, self.held, self.got, self.last = place, held, got, last
        self.send, self.recv = send, recv

    def copies(self, stage):
        peers = self.place.peers()
        if stage < 3:
            peer = (CORE, ALONG_Y, ALONG_X)[stage]
            return [remote(self.held.at[stage], self.got.at[stage], self.send.at[stage], self.recv.at[stage], peers[peer])]
        return [
            remote(self.held.at[3], self.last.at[self.place.z], self.send.at[2 + step], self.recv.at[2 + step], peers[step])
            for step in (1, 2, 3)
        ]

    def start(self, stage):
        start_all(self.copies(stage))

    def step(self, stage):
        arrive_all(self.copies(stage))
        if stage == 3:
            return
        total = self.held[stage] + self.got[stage]
        self.held[stage + 1] = total
        if stage == 2:
            self.last[self.place.z] = total
        self.start(stage + 1)

    def total(self):
        return (self.last[0] + self.last[1]) + (self.last[2] + self.last[3])

    def sent(self):
        for stage in range(4):
            sent_all(self.copies(stage))


class Summing:
    def __init__(self, index, place, away, held, got, middle, near, last, send, recv):
        self.weight, self.row, self.count, self.width, self.order = SUMMED[index]
        self.index, self.place = index, place
        self.away, self.held, self.got = away, held, got
        self.middle, self.near, self.last = middle, near, last
        self.send, self.recv = send, recv
        self.rows = pl.ds(self.row, self.count)

    def copies(self, stage):
        place = self.place
        peers = place.peers()

        def copy(source, target, slot, peer):
            return remote(source, target, self.send.at[self.index, slot], self.recv.at[self.index, slot], peers[peer])

        held, rows = self.held, self.rows
        if stage == 0:
            return [copy(self.away(y, rows), self.got.at[y, :, :, rows, :], y, CORE) for y in range(2)]
        if stage == 1:
            if self.order == "yx":
                return [copy(held.at[1 - place.y, :, :, rows, :], self.middle, 2, ALONG_Y)]
            return [copy(held.at[:, :, 1 - place.x, rows, :], self.middle, 2, ALONG_X)]
        if stage == 2:
            if self.order == "yx":
                return [copy(held.at[place.y, :, 1 - place.x, rows, :], self.near, 3, ALONG_X)]
            return [copy(held.at[1 - place.y, :, place.x, rows, :], self.near, 3, ALONG_Y)]
        return [
            copy(held.at[place.y, (place.z + step) % 4, place.x, rows, :], self.last.at[step - 1], 3 + step, step)
            for step in (1, 2, 3)
        ]

    def start(self, stage):
        start_all(self.copies(stage))

    def add(self, where, more):
        held = self.held
        held[where] = (held[where].astype(jnp.float32) + more.astype(jnp.float32)).astype(jnp.bfloat16)

    def arrive(self, stage):
        arrive_all(self.copies(stage))
        place, rows = self.place, self.rows

        def block(z, carry):
            if stage == 0:
                for y in range(2):
                    for x in range(2):
                        self.add((y, z, x, rows, slice(None)), self.got[y, z, x, rows, :])
            elif stage == 1:
                for other in range(2):
                    if self.order == "yx":
                        self.add((place.y, z, other, rows, slice(None)), self.middle[z, other])
                    else:
                        self.add((other, z, place.x, rows, slice(None)), self.middle[other, z])
            else:
                self.add((place.y, z, place.x, rows, slice(None)), self.near[z])
            return carry

        lax.fori_loop(0, 4, block, 0)

    def result(self):
        arrive_all(self.copies(3))
        place = self.place
        own = self.held[place.y, place.z, place.x, self.rows, :].astype(jnp.float32)
        for step in range(3):
            own = own + self.last[step].astype(jnp.float32)
        return own

    def sent(self):
        for stage in range(4):
            sent_all(self.copies(stage))


def middle_shape(index):
    _, _, count, width, order = SUMMED[index]
    return (4, 2, count, width) if order == "yx" else (2, 4, count, width)


def tail_kernel(
    lengths_ref, qkv_ref, mixed_ref, gmixed_ref, total_ref, cos_ref, sin_ref, x_ref, small_ref, gy1_ref, sums_ref, in_ref,
    gout_hbm, gup_hbm, gdown_hbm, *refs,
):
    state, refs = refs[:12], refs[12:]
    grad_refs, (xgrad_ref, all_ref, norm_ref), refs = refs[:4], refs[4:7], refs[7:]
    gproj_ref, dk_ref, dv_ref, enter_t, away_in, small_acc, refs = *refs[:6], refs[6:]
    held, got, refs = refs[:4], refs[4:8], refs[8:]
    middle, near, last, refs = refs[:5], refs[5:10], refs[10:15], refs[15:]
    small_held, small_got, small_last, norm_held, norm_got, norm_last, refs = *refs[:6], refs[6:]
    send, recv, small_send, small_recv, norm_send, norm_recv, load_sem = refs
    bucket = pl.program_id(0)
    place = Place()
    sources = (None, gout_hbm, gup_hbm, gdown_hbm)

    def away(weight, width):
        if weight == 0:
            return lambda y, rows: away_in.at[y, :, :, rows, :]
        return lambda y, rows: sources[weight].at[:, :, rows, tile_cols(y * 2 + (1 - place.c), width)]

    def summing(which):
        return [
            Summing(
                index, place, away(SUMMED[index][0], SUMMED[index][3]), held[SUMMED[index][0]], got[SUMMED[index][0]],
                middle[index], near[index], last[index], send, recv,
            )
            for index in which
        ]

    early, late = summing((0, 1, 2)), summing((3, 4))
    small_sum = Everywhere(place, small_held, small_got, small_last, small_send, small_recv)
    norm_sum = Everywhere(place, norm_held, norm_got, norm_last, norm_send, norm_recv)

    def loads():
        found = []
        for weight, width in ((1, OUT_W), (2, FF_W), (3, FF_W)):
            for y in range(2):
                source = sources[weight].at[:, :, :, tile_cols(y * 2 + place.c, width)]
                found.append(pltpu.make_async_copy(source, held[weight].at[y], load_sem.at[weight - 1, y]))
        return found

    @pl.when(bucket == 0)
    def _():
        meet(place)
        for item in early:
            item.start(0)
        start_all(loads())
        for index in range(MICRO):

            def normalise(chunk, carry):
                rows = chunk_rows(chunk)
                cols = pl.ds(pl.multiple_of(index * LEN + chunk * BQ, BQ), BQ)
                enter_t[:, cols] = enter_rows(x_ref, small_ref, rows, index).T
                return carry

            lax.fori_loop(0, LEN // BQ, normalise, 0)

    @pl.when(bucket == 1)
    def _():
        for item in early:
            item.arrive(1)
        for item in early:
            item.start(2)

    shared = (qkv_ref, mixed_ref, gmixed_ref, total_ref, cos_ref, sin_ref, gproj_ref, dk_ref, dv_ref)
    attend_backward(lengths_ref, bucket, bucket, 0, 0, BQ, *shared)

    def later(step, carry):
        @pl.when((bucket == 0) & (step == 2))
        def _():
            for load in loads():
                load.wait()
            for item in early:
                item.arrive(0)
            for item in early:
                item.start(1)

        @pl.when((bucket == 1) & (step == 2))
        def _():
            for item in early:
                item.arrive(2)
            for item in early:
                item.start(3)

        first_row = pl.multiple_of(step * BQ, BQ)
        attend_backward(lengths_ref, bucket, bucket, first_row, pl.multiple_of(first_row - BQ, BQ), 2 * BQ, *shared)
        return carry

    lax.fori_loop(1, LEN // BQ, later, 0)
    finish_keys(bucket, cos_ref, sin_ref, gproj_ref, dk_ref, dv_ref)

    @pl.when(bucket == 1)
    def _():
        def grad_tile(tensor):
            right = gproj_ref[:, :, tile_cols(tensor, IN_W)].reshape(MICRO * LEN, IN_W)
            return dot(enter_t[...], right).astype(jnp.bfloat16).reshape(4, 2, 64, IN_W)

        def tiles(step, carry):
            @pl.when(step < 2)
            def _():
                away_in[step] = grad_tile(step * 2 + 1 - place.c)

            @pl.when(step == 1)
            def _():
                for item in late:
                    item.start(0)

            @pl.when(step >= 2)
            def _():
                held[0][step - 2] = grad_tile((step - 2) * 2 + place.c)

            return carry

        lax.fori_loop(0, 4, tiles, 0)
        small_acc[...] = jnp.zeros_like(small_acc)
        in_full = in_ref[...]

        def data_grad(step, carry):
            for stage, moment in ((0, 1), (1, 4), (2, 7)):

                @pl.when(step == moment)
                def _():
                    for item in late:
                        item.arrive(stage)
                    for item in late:
                        item.start(stage + 1)

            index = step // (LEN // BQ)
            rows = chunk_rows(step % (LEN // BQ))
            grad_enter = dot(gproj_ref[index, rows, :], in_full, NT)
            normal, inverse = norm_parts(x_ref[index, rows, :].astype(jnp.float32))
            back = norm_back(grad_enter * small_ref[0:1, :], normal, inverse)
            xgrad_ref[index, rows, :] = (gy1_ref[index, rows, :] + back).astype(jnp.bfloat16)
            small_acc[0] += jnp.sum((grad_enter * normal).reshape(BQ // 8, 8, D), 0)
            small_acc[1] += jnp.sum(grad_enter.reshape(BQ // 8, 8, D), 0)
            return carry

        lax.fori_loop(0, MICRO * LEN // BQ, data_grad, 0)

        rows = [jnp.sum(small_acc[row], 0, keepdims=True) for row in range(2)]
        rows += [jnp.sum(sums_ref[row], 0, keepdims=True) for row in range(4)]
        weights_sq = []
        for which in range(4):
            weights_sq.append([state[3 * which][plane] * state[3 * which][plane] for plane in planes(which)])
        rows.append(sums_of_squares(weights_sq))
        rows.append(jnp.zeros((1, D), jnp.float32))
        small_held[0] = jnp.concatenate(rows, 0)
        small_sum.start(0)

        grads = [None, early[0].result().T, early[1].result(), early[2].result().T]
        grad_refs[1][0] = grads[1][:HEAD_DIM]
        grad_refs[1][1] = grads[1][HEAD_DIM:]
        grad_refs[2][...] = grads[2]
        grad_refs[3][...] = grads[3]
        small_sum.step(0)
        parts = [item.result() for item in late]
        part = jnp.concatenate(parts, 0)
        for head in range(2):
            pieces = [part[:, which * 128 + head * HEAD_DIM : which * 128 + head * HEAD_DIM + HEAD_DIM] for which in range(3)]
            grad_refs[0][:, head, :] = jnp.concatenate(pieces, 1)
        updates_sq = []
        for which in range(4):
            squares = []
            for plane in planes(which):
                weight, first, second = (state[3 * which + kind][plane] for kind in range(3))
                update = moments(weight, grad_refs[which][plane], first, second)[2]
                squares.append(update * update)
            updates_sq.append(squares)
        norm_held[0] = jnp.broadcast_to(sums_of_squares(updates_sq)[:, :128], (8, 128))
        norm_sum.start(0)
        small_sum.step(1)
        norm_sum.step(0)
        small_sum.step(2)
        norm_sum.step(1)
        small_sum.step(3)
        norm_sum.step(2)
        norm_sum.step(3)
        all_ref[...] = small_sum.total()
        norm_ref[...] = norm_sum.total()
        for item in early + late:
            item.sent()
        small_sum.sent()
        norm_sum.sent()


def lamb_kernel(*refs):
    state, grads, refs = refs[:12], refs[12:16], refs[16:]
    small_ref, small_first_ref, small_second_ref, all_ref, norm_ref, refs = *refs[:5], refs[5:]
    outs, (grad_ref, new_ref, first_ref, second_ref, norms_ref) = refs[:16], refs[16:]
    weight_norm = jnp.sqrt(all_ref[6:7, 0:128])
    update_sq = norm_ref[0:1, :]
    ratio = learn_rate * weight_norm * lax.rsqrt(update_sq + 1e-12)
    for which in range(4):
        scale = ratio[:, which : which + 1]
        for plane in planes(which):
            weight, first, second = (state[3 * which + kind][plane] for kind in range(3))
            first, second, update = moments(weight, grads[which][plane], first, second)
            new = weight - scale * update
            outs[4 * which][plane] = new
            outs[4 * which + 1][plane] = first
            outs[4 * which + 2][plane] = second
            outs[4 * which + 3][plane] = new.astype(jnp.bfloat16)
    small = small_ref[...]
    small_grad = all_ref[0:6, :]
    grad_ref[...] = small_grad
    first, second, update = moments(small, small_grad, small_first_ref[...], small_second_ref[...])
    small_sq = jnp.sum(small * small, 1, keepdims=True)
    change_sq = jnp.sum(update * update, 1, keepdims=True)
    new_ref[...] = small - learn_rate * jnp.sqrt(small_sq) * lax.rsqrt(change_sq + 1e-12) * update
    first_ref[...] = first
    second_ref[...] = second
    lanes = lane_ids((1, 128))
    top = jnp.where(lanes < 4, weight_norm, 0.0)
    bottom = jnp.where(lanes < 4, jnp.sqrt(update_sq), 0.0)
    for row in range(6):
        top = top + jnp.where(lanes == 4 + row, jnp.sqrt(small_sq[row : row + 1]), 0.0)
        bottom = bottom + jnp.where(lanes == 4 + row, jnp.sqrt(change_sq[row : row + 1]), 0.0)
    norms_ref[0:1, :] = top[:, :10]
    norms_ref[1:2, :] = bottom[:, :10]


def whole(shape):
    return pl.BlockSpec(shape, lambda *ids: (0,) * len(shape), pipeline_mode=pl.Buffered(1))


def per_bucket(*shape):
    return pl.BlockSpec((1,) + shape, lambda b: (b, 0, 0))


def bf16(*shape):
    return jax.ShapeDtypeStruct(shape, jnp.bfloat16)


def f32(*shape):
    return jax.ShapeDtypeStruct(shape, jnp.float32)


def vmem16(*shape):
    return pltpu.VMEM(shape, jnp.bfloat16)


def vmem32(*shape):
    return pltpu.VMEM(shape, jnp.float32)


SCALARS = pl.BlockSpec(memory_space=pltpu.SMEM)
ANYWHERE = pl.BlockSpec(memory_space=pl.ANY)


def params(count, collective=None):
    more = {} if collective is None else dict(collective_id=collective, has_side_effects=True)
    return pltpu.CompilerParams(dimension_semantics=("arbitrary",) * count, vmem_limit_bytes=VMEM_LIMIT, **more)


def turn_tables(lengths):
    ends = jnp.cumsum(lengths, axis=1)
    position = jnp.arange(LEN, dtype=jnp.int32)
    passed = position[None, :, None] >= ends[:, None, : CLIPS - 1]
    start = jnp.max(jnp.where(passed, ends[:, None, : CLIPS - 1], 0), axis=2)
    offset = (position[None, :] - start).astype(jnp.float32)
    frequency = jnp.exp(jnp.arange(HEAD_DIM // 2, dtype=jnp.float32) * (-2.0 * math.log(10000.0) / HEAD_DIM))
    angles = offset[:, :, None] * frequency
    cosine = jnp.repeat(jnp.cos(angles), 2, axis=-1)
    sine = jnp.sin(angles)
    sine = jnp.stack([-sine, sine], axis=-1).reshape(cosine.shape)
    return jnp.concatenate([cosine, cosine], -1), jnp.concatenate([sine, sine], -1)


def attention_forward(lengths, x, small, cosine, sine, in_mat):
    count = x.shape[0]
    return pl.pallas_call(
        functools.partial(forward_kernel, alone=True),
        grid=(count,),
        in_specs=[SCALARS, per_bucket(LEN, D), whole((6, D)), per_bucket(LEN, 128), per_bucket(LEN, 128), whole((D, 3 * D))],
        out_specs=[per_bucket(LEN, 3 * D), per_bucket(LEN, D), per_bucket(LEN, D), per_bucket(LEN, D)],
        out_shape=[bf16(count, LEN, 3 * D), bf16(count, LEN, D), f32(count, LEN, D), bf16(count, LEN, D)],
        compiler_params=params(1),
        name="attention_forward",
    )(lengths, x, small, cosine, sine, in_mat)


def gather_forward(lengths, x, small, cosine, sine, shard):
    shapes = [(4, 2, 64, 4 * width) for width in (IN_W, OUT_W, FF_W, FF_W)]
    return pl.pallas_call(
        functools.partial(forward_kernel, alone=False),
        grid=(MICRO,),
        in_specs=[
            SCALARS, per_bucket(LEN, D), whole((6, D)), per_bucket(LEN, 128), per_bucket(LEN, 128), whole((64, SHARD_W)),
        ],
        out_specs=[per_bucket(LEN, 3 * D), per_bucket(LEN, D), per_bucket(LEN, D)] + [ANYWHERE] * 4,
        out_shape=[bf16(MICRO, LEN, 3 * D), bf16(MICRO, LEN, D), f32(MICRO, LEN, D)] + [bf16(*shape) for shape in shapes],
        scratch_shapes=[vmem16(*shape) for shape in shapes]
        + [
            vmem16(1, LEN, D),
            pltpu.SemaphoreType.DMA((5, 8)),
            pltpu.SemaphoreType.DMA((5, 8)),
            pltpu.SemaphoreType.DMA((4,)),
            pltpu.SemaphoreType.DMA((4,)),
        ],
        compiler_params=params(1, 1),
        name="gather_forward",
    )(lengths, x, small, cosine, sine, shard)


def mlp_both(lengths, x, cot, mixed, small, out_mat, up_mat, down_mat):
    count = x.shape[0]
    rows = count * LEN

    def chunked(width):
        return pl.BlockSpec((1, MLP_ROWS, width), lambda b, i: (b, i, 0))

    return pl.pallas_call(
        mlp_kernel,
        grid=(count, LEN // MLP_ROWS),
        in_specs=[SCALARS, chunked(D), chunked(D), chunked(D), whole((6, D)), whole((D, D)), whole((D, FF)), whole((D, FF))],
        out_specs=[chunked(D), chunked(D), chunked(D), whole((4, 8, D)), whole((D, D)), whole((D, FF)), whole((D, FF))],
        out_shape=[
            bf16(count, LEN, D), f32(count, LEN, D), bf16(count, LEN, D), f32(4, 8, D), bf16(D, D), bf16(D, FF), bf16(D, FF),
        ],
        scratch_shapes=[
            vmem16(rows, FF), vmem16(rows, FF), vmem16(rows, D), vmem16(D, rows), vmem16(D, rows), vmem16(D, rows),
        ],
        compiler_params=params(2),
        name="mlp_both",
    )(lengths, x, cot, mixed, small, out_mat, up_mat, down_mat)


def attention_backward(lengths, qkv, mixed, gmixed, totals, cosine, sine):
    count = qkv.shape[0]
    return pl.pallas_call(
        backward_kernel,
        grid=(count,),
        in_specs=[SCALARS, per_bucket(LEN, 3 * D), per_bucket(LEN, D), per_bucket(LEN, D), per_bucket(LEN, D), per_bucket(LEN, 128), per_bucket(LEN, 128)],
        out_specs=per_bucket(LEN, 3 * D),
        out_shape=bf16(count, LEN, 3 * D),
        scratch_shapes=[vmem32(LEN, D), vmem32(LEN, D)],
        compiler_params=params(1),
        name="attention_backward",
    )(lengths, qkv, mixed, gmixed, totals, cosine, sine)


def backward_tail(lengths, qkv, mixed, gmixed, totals, cosine, sine, x, small, gy1, sums, in_mat, gout, gup, gdown, state):
    widths = (IN_W, OUT_W, FF_W, FF_W)
    dma = pltpu.SemaphoreType.DMA
    grad_shapes = [f32(*state[3 * which].shape) for which in range(4)]
    return pl.pallas_call(
        tail_kernel,
        grid=(MICRO,),
        in_specs=[
            SCALARS, per_bucket(LEN, 3 * D), per_bucket(LEN, D), per_bucket(LEN, D), per_bucket(LEN, D),
            per_bucket(LEN, 128), per_bucket(LEN, 128), whole((MICRO, LEN, D)), whole((6, D)), whole((MICRO, LEN, D)),
            whole((4, 8, D)), whole((D, 3 * D)), ANYWHERE, ANYWHERE, ANYWHERE,
        ]
        + [whole(item.shape) for item in state],
        out_specs=[whole(item.shape) for item in grad_shapes] + [whole((MICRO, LEN, D)), whole((8, D)), whole((8, 128))],
        out_shape=grad_shapes + [bf16(MICRO, LEN, D), f32(8, D), f32(8, 128)],
        scratch_shapes=[
            vmem16(MICRO, LEN, 3 * D), vmem32(LEN, D), vmem32(LEN, D), vmem16(D, MICRO * LEN), vmem16(2, 4, 2, 64, IN_W), vmem32(2, 8, D),
        ]
        + [vmem16(2, 4, 2, 64, width) for width in widths]
        + [vmem16(2, 4, 2, 64, width) for width in widths]
        + [vmem16(*middle_shape(index)) for index in range(5)]
        + [vmem16(4, SUMMED[index][2], SUMMED[index][3]) for index in range(5)]
        + [vmem16(3, SUMMED[index][2], SUMMED[index][3]) for index in range(5)]
        + [vmem32(4, 8, D), vmem32(3, 8, D), vmem32(4, 8, D), vmem32(4, 8, 128), vmem32(3, 8, 128), vmem32(4, 8, 128)]
        + [dma((5, 7)), dma((5, 7)), dma((6,)), dma((6,)), dma((6,)), dma((6,)), dma((3, 2))],
        compiler_params=params(1, 2),
        name="backward_tail",
    )(lengths, qkv, mixed, gmixed, totals, cosine, sine, x, small, gy1, sums, in_mat, gout, gup, gdown, *state)


def lamb_all(state, grads, small, small_first, small_second, everything, norm_squares):
    outs = []
    for which in range(4):
        shape = state[3 * which].shape
        outs += [f32(*shape)] * 3 + [bf16(*shape)]
    outs += [f32(6, D)] * 4 + [f32(2, 10)]
    return pl.pallas_call(
        lamb_kernel,
        out_shape=outs,
        compiler_params=pltpu.CompilerParams(vmem_limit_bytes=VMEM_LIMIT),
        name="lamb_all",
    )(*state, *grads, small, small_first, small_second, everything, norm_squares)


def tile_shard(in_proj, out_proj, up_proj, down_proj, paired):
    depth, heads_here, _ = in_proj.shape
    in_cols = in_proj.reshape(depth, heads_here, 3, HEAD_DIM)
    if paired:
        in_cols = in_cols.transpose(0, 2, 1, 3)
    out_cols = out_proj.reshape(heads_here * HEAD_DIM, depth).T
    parts = [in_cols.reshape(depth, -1), out_cols, up_proj, down_proj.T]
    return jnp.concatenate(parts, axis=1).astype(jnp.bfloat16)


def on_device(
    frames, cotangent, clip_lengths, in_proj, out_proj, up_proj, down_proj, small_params,
    in_first, in_second, out_first, out_second, up_first, up_second, down_first, down_second,
    small_first, small_second,
):
    lengths = lax.dynamic_slice_in_dim(clip_lengths, lax.axis_index("tensor"), 1, 1).reshape(MICRO, CLIPS)
    cosine, sine = turn_tables(lengths)
    shard = tile_shard(in_proj, out_proj, up_proj, down_proj, True)
    qkv, mixed, totals, in_full, out_full, up_full, down_full = gather_forward(lengths, frames, small_params, cosine, sine, shard)
    block_out, gy1, gmixed, sums, gout, gup, gdown = mlp_both(
        lengths, frames, cotangent, mixed, small_params, out_full.reshape(D, D), up_full.reshape(D, FF), down_full.reshape(D, FF)
    )
    state = (
        in_proj, in_first, in_second, out_proj, out_first, out_second, up_proj, up_first, up_second, down_proj, down_first, down_second,
    )
    *grads, input_grad, everything, norm_squares = backward_tail(
        lengths, qkv, mixed, gmixed, totals, cosine, sine, frames, small_params, gy1, sums, in_full.reshape(D, 3 * D),
        gout.reshape(4, 2, 64, D), gup.reshape(4, 2, 64, FF), gdown.reshape(4, 2, 64, FF), state,
    )
    outs = lamb_all(state, grads, small_params, small_first, small_second, everything, norm_squares)
    return (block_out, input_grad, *outs)


def on_any_mesh(
    frames, cotangent, clip_lengths, in_proj, out_proj, up_proj, down_proj, small_params,
    in_first, in_second, out_first, out_second, up_first, up_second, down_first, down_second,
    small_first, small_second,
):
    rows_here = frames.shape[1]
    own_buckets = rows_here // LEN
    first_bucket = lax.axis_index("tensor") * own_buckets
    lengths = lax.dynamic_slice_in_dim(clip_lengths, first_bucket, own_buckets, 1).reshape(-1, CLIPS)
    count = MICRO * own_buckets
    x = frames.reshape(count, LEN, D)
    cot = cotangent.reshape(count, LEN, D)
    tensor_size = lax.axis_size("tensor")
    dp_size = lax.axis_size("dp")
    depth = in_proj.shape[0]
    heads_here = in_proj.shape[1]
    ff_here = up_proj.shape[1]

    shard = tile_shard(in_proj, out_proj, up_proj, down_proj, False)
    gathered = lax.all_gather(shard, ("dp", "tensor"), axis=0)
    gathered = gathered.reshape(dp_size, tensor_size, depth, shard.shape[1])
    gathered = jnp.moveaxis(gathered, 1, 2).reshape(D, tensor_size, shard.shape[1])
    edge0 = heads_here * 192
    edge1 = edge0 + heads_here * HEAD_DIM
    edge2 = edge1 + ff_here
    in_mat = gathered[:, :, :edge0].reshape(D, PAIRS, 2, 3, HEAD_DIM).transpose(0, 1, 3, 2, 4).reshape(D, 3 * D)
    out_mat = gathered[:, :, edge0:edge1].reshape(D, D)
    up_mat = gathered[:, :, edge1:edge2].reshape(D, FF)
    down_mat = gathered[:, :, edge2:].reshape(D, FF)

    cosine, sine = turn_tables(lengths)
    qkv, mixed, totals, enter1 = attention_forward(lengths, x, small_params, cosine, sine, in_mat)
    block_out, grad_y_first, grad_mixed, sums, grad_out, grad_upw, grad_down = mlp_both(
        lengths, x, cot, mixed, small_params, out_mat, up_mat, down_mat
    )

    def weight_grad(left, right):
        return dot(left.reshape(-1, left.shape[-1]), right.reshape(-1, right.shape[-1]), TN).astype(jnp.bfloat16)

    grad_proj = attention_backward(lengths, qkv, mixed, grad_mixed, totals, cosine, sine)
    grad_in = weight_grad(enter1, grad_proj)
    grad_in = grad_in.reshape(D, PAIRS, 3, 2, HEAD_DIM).transpose(0, 1, 3, 2, 4)

    def by_owner(mat):
        return jnp.moveaxis(mat.reshape(dp_size, depth, tensor_size, -1), 2, 1)

    stacked = jnp.concatenate([by_owner(grad_in), by_owner(grad_out), by_owner(grad_upw), by_owner(grad_down)], axis=-1)
    owned = lax.psum_scatter(
        stacked.reshape(dp_size * tensor_size, depth, -1), ("dp", "tensor"), scatter_dimension=0, tiled=False
    ).astype(jnp.float32)

    grad_enter1 = dot(grad_proj.reshape(-1, 3 * D), in_mat, NT).reshape(count, LEN, D)
    normal1, inverse1 = norm_parts(x.astype(jnp.float32))
    input_grad = (grad_y_first + norm_back(grad_enter1 * small_params[0], normal1, inverse1)).astype(jnp.bfloat16)
    late = jnp.sum(sums, axis=1)
    small_terms = jnp.stack(
        [jnp.sum(grad_enter1 * normal1, (0, 1)), jnp.sum(grad_enter1, (0, 1)), late[0], late[1], late[2], late[3]]
    )

    grads = (
        owned[:, :edge0].reshape(in_proj.shape),
        owned[:, edge0:edge1].T.reshape(out_proj.shape),
        owned[:, edge1:edge2],
        owned[:, edge2:].T,
    )
    weights_in = (in_proj, out_proj, up_proj, down_proj)
    firsts = (in_first, out_first, up_first, down_first)
    seconds = (in_second, out_second, up_second, down_second)
    own_squares = jnp.stack([jnp.sum(weight * weight) for weight in weights_in])
    small_grad, weight_squares = lax.psum((small_terms, own_squares), ("dp", "tensor"))
    new_firsts = []
    new_seconds = []
    updates = []
    for weight, gradient, first, second in zip(weights_in, grads, firsts, seconds):
        first = beta_first * first + (1.0 - beta_first) * gradient
        second = beta_second * second + (1.0 - beta_second) * gradient * gradient
        update = (
            first / (1.0 - beta_first**STEP) / (jnp.sqrt(second / (1.0 - beta_second**STEP)) + adam_eps)
            + decay_rate * weight
        )
        new_firsts.append(first)
        new_seconds.append(second)
        updates.append(update)
    update_squares = lax.psum(jnp.stack([jnp.sum(update * update) for update in updates]), ("dp", "tensor"))
    trust_ratio = jnp.sqrt(weight_squares) * lax.rsqrt(update_squares + 1e-12)
    new_weights = [weights_in[index] - learn_rate * trust_ratio[index] * updates[index] for index in range(4)]
    small_first_new = beta_first * small_first + (1.0 - beta_first) * small_grad
    small_second_new = beta_second * small_second + (1.0 - beta_second) * small_grad * small_grad
    small_update = (
        small_first_new / (1.0 - beta_first**STEP) / (jnp.sqrt(small_second_new / (1.0 - beta_second**STEP)) + adam_eps)
        + decay_rate * small_params
    )
    small_weight_sq = jnp.sum(small_params * small_params, axis=1, keepdims=True)
    small_update_sq = jnp.sum(small_update * small_update, axis=1, keepdims=True)
    small_new = small_params - learn_rate * jnp.sqrt(small_weight_sq) * lax.rsqrt(small_update_sq + 1e-12) * small_update
    norms = jnp.stack(
        [
            jnp.concatenate([jnp.sqrt(weight_squares), jnp.sqrt(small_weight_sq).reshape(-1)]),
            jnp.concatenate([jnp.sqrt(update_squares), jnp.sqrt(small_update_sq).reshape(-1)]),
        ]
    )
    outputs = [block_out.reshape(frames.shape), input_grad.reshape(frames.shape)]
    for new, first, second in zip(new_weights, new_firsts, new_seconds):
        outputs += [new, first, second, new.astype(jnp.bfloat16)]
    return tuple(outputs + [small_grad, small_new, small_first_new, small_second_new, norms])


def solution(mesh):
    rows = P(None, ("dp", "tensor"), None)
    in_spec = P("dp", "tensor", None)
    out_spec = P("tensor", None, "dp")
    up_spec = P("dp", "tensor")
    down_spec = P("tensor", "dp")
    shape = dict(mesh.shape)
    small_slice = shape["dp"] == HERE_DP and shape["tensor"] == HERE_TENSOR
    return jax.shard_map(
        on_device if small_slice else on_any_mesh,
        mesh=mesh,
        in_specs=(
            rows, rows, P(None, "dp", None), in_spec, out_spec, up_spec, down_spec, P(),
            in_spec, in_spec, out_spec, out_spec, up_spec, up_spec, down_spec, down_spec, P(), P(),
        ),
        out_specs=(rows, rows) + (in_spec,) * 4 + (out_spec,) * 4 + (up_spec,) * 4 + (down_spec,) * 4 + (P(),) * 5,
        check_vma=False,
    )
```

time: 462 us -> 235 us (0.51); the launches traced: 453 us -> 234 us
  waiting for transfers between devices: 163 us -> 0 us
  Pallas kernels: 103 us -> 209 us
  blocking collectives: 39.9 us -> 0 us
  matrix products: 36.7 us -> 0 us
  other arithmetic: 46.7 us -> 10.5 us
  local copies, waits for them, and re-layouts: 45.7 us -> 14.5 us
  between operations: 17.5 us -> 0.88 us
    reduce_scatter x1 -> x0, waiting for transfers between devices: 102 us -> none  [on_device(): lax.psum_scatter(stacked.reshape(dp_size * tensor_size, depth, -1), ('dp'...]
    pallas_call x2 -> x3, Pallas kernels: 68.9 us -> 162 us  [the longest x1 87.2 us: backward_tail(): pl.pallas_call(tail_kernel, grid=(MICRO,), in_specs=[SCALARS, per_bucket(...]
    all_gather x1 -> x0, waiting for transfers between devices: 61.3 us -> none  [on_device(): gathered = lax.all_gather(shard, ('dp', 'tensor'), axis=0)]
    psum x1 -> x0, blocking collectives: 39.9 us -> none  [on_device(): lax.psum(jnp.stack([jnp.sum(update * update) for update in updates]), ('d...]
    dot_general x5 -> x0, matrix products: 36.7 us -> none  [dot(): return lax.dot_general(a, b, dims, preferred_element_type=jnp.float32)]
    reshape x11 -> x2, local copies, waits for them, and re-layouts: 21 us -> 0.21 us  [the longest x1 0.13 us: tile_shard(): parts = [in_cols.reshape(depth, -1), out_cols, up_proj, down_proj.T]]
    pallas_call x1, Pallas kernels: 33.7 us -> 46.7 us  [mlp_both(): pl.pallas_call(mlp_kernel, grid=(count, LEN // MLP_ROWS), in_specs=[SCALA...]
    reduce_sum x9 -> x0, other arithmetic: 11.6 us -> none  [the longest x4 7.38 us: on_device(): own_squares = jnp.stack([jnp.sum(weight * weight) for weight in weights_in])]
  transfers between devices with their start and end apart: 2 -> 0, of which waited for: 2 -> 0; matrix products, arithmetic and copies ran while one was open for 5% -> 0% of each run, Pallas kernels for 0% -> 0%
where the time goes in v2:
time: 235 us; the launch traced here: 234 us
  Pallas kernels  209 us (89%)
  local copies, waits for them, and re-layouts  14.5 us (6%)
  other arithmetic  10.5 us (4%)
    pallas_call x1, Pallas kernels, backward_tail(): pl.pallas_call(tail_kernel, grid=(MICRO,), in_specs=[SCALARS, per_bucket(...  87.2 us
    pallas_call x1, Pallas kernels, gather_forward(): pl.pallas_call(functools.partial(forward_kernel, alone=False), grid=(MICR...  70.3 us
    pallas_call x1, Pallas kernels, mlp_both(): pl.pallas_call(mlp_kernel, grid=(count, LEN // MLP_ROWS), in_specs=[SCALA...  46.7 us
    unnamed x25, local copies, waits for them, and re-layouts  13.2 us

profile of v2, /device:TPU:0, one launch (start us, length us, event | category | flops | bytes accessed | tf_op | source)
XLA Modules:
  0.0 234.4 jit_solution(3966651448683820537)
XLA Ops:
  0.7 0.0 copy-start
  0.7 0.7 copy-done
  1.4 0.0 copy-start.7
  1.4 0.2 reduce_window_sum.11
  1.5 0.1 copy.70
  1.6 0.1 fusion
  1.8 3.8 %fusion.1 = (f32[2,1024,32,1]{1,0,3,2:T(2,128)S(1)}, f32[2,1024,32,1]{1,0,3,2:T(2,128)S(1)}) fusion(f32[32]{0:T(128)S(1)} %multiply_exponential_fusion, f32[2,1024]{1,0:T(2,128)S(1)} %subtract_convert_fusion), kind=kLoop, calls=%fused_computation.12 | loop fusion | flops 131072 | bytes 532608 | tf_op jit(solution)/shard_map/neg | solution.py:900
  5.5 0.2 pad_maximum_fusion.2
  5.8 0.4 copy.73
  6.1 3.5 %multiply_cosine_fusion = f32[2,1024,32]{1,0,2:T(2,128)S(1)} fusion(f32[2,1024]{1,0:T(2,128)S(1)} %subtract_convert_fusion, f32[32]{0:T(128)S(1)} %multiply_exponential_fusion), kind=kLoop, calls=%fused_computation.4 | loop fusion | flops 65536 | bytes 270464 | tf_op jit(solution)/shard_map/cos | solution.py:898
  9.7 0.2 broadcast_in_dim.13
  9.8 0.0 copy-done.7
  9.8 0.4 copy.71
  10.2 0.0 copy-start.1
  10.2 0.0 copy-start.2
  10.2 0.0 copy-start.4
  10.2 0.0 copy-start.3
  10.3 1.9 pad_maximum_fusion
  12.2 0.0 copy-done.1
  12.2 0.1 copy.75
  12.3 0.1 copy.76
  12.5 0.1 reshape.116
  12.6 0.0 copy-done.2
  12.6 0.0 copy-done.4
  12.6 0.0 copy-done.3
  12.7 0.1 copy.88
  12.8 0.7 pad_maximum_fusion.3.refs_0_
  13.5 70.3 %gather_forward.1 = (bf16[2,1024,1536]{2,1,0:T(8,128)(2,1)}, bf16[2,1024,512]{2,1,0:T(8,128)(2,1)}, f32[2,1024,512]{2,1,0:T(8,128)}, bf16[4,2,64,1536]{3,2,1,0:T...) custom-call(s32[2,4]{1,0:T(2,128)} %bitcast.31, ...), custom_call_target="tpu_custom_call" | custom-call | tf_op jit(solution)/shard_map/gather_forward/pallas_call | solution.py:919
  83.7 0.0 copy-start.5
  83.7 0.0 copy-start.6
  83.8 46.7 %mlp_both.1 = (bf16[2,1024,512]{2,1,0:T(8,128)(2,1)}, f32[2,1024,512]{2,1,0:T(8,128)}, bf16[2,1024,512]{2,1,0:T(8,128)(2,1)}, f32[4,8,512]{2,1,0:T(8,128)}, bf16...) custom-call(s32[2,4]{1,0:T(2,128)} %bitcast.32, bf16[2,1024,512]{2,1,0:T(8,128)(2,1)} %x_ref.5, ...), custom_call_target="tpu_custom_call" | custom-call | tf_op jit(solution)/shard_map/mlp_both/pallas_call | solution.py:947
  130.5 0.8 copy.78.refs_9_
  131.3 0.0 copy-done.5
  131.3 0.8 copy.79.refs_10_
  132.1 0.0 copy-done.6
  132.1 0.8 copy.80.refs_11_
  133.0 87.2 %backward_tail.1 = (f32[64,2,192]{2,1,0:T(2,128)}, f32[2,64,64]{2,1,0:T(8,128)}, f32[64,512]{1,0:T(8,128)}, f32[512,64]{1,0:T(8,128)}, bf16[2,1024,512]{2,1,0:T(...) custom-call(s32[2,4]{1,0:T(2,128)} %bitcast.33, bf16[2,1024,1536]{2,1,0:T(8,128)(2,1)} %get-tuple-element.70.qkv_ref, ...), custom_call_target="tpu_custom_call" | custom-call | tf_op jit(solution)/shard_map/backward_tail/pallas_call | solution.py:981
  220.2 4.3 %lamb_all.1 = (f32[64,2,192]{2,1,0:T(2,128)}, f32[64,2,192]{2,1,0:T(2,128)}, f32[64,2,192]{2,1,0:T(2,128)}, bf16[64,2,192]{2,1,0:T(2,128)(2,1)}, f32[2,64,64]{2,...) custom-call(f32[64,2,192]{2,1,0:T(2,128)} %refs_0_.3, ...), custom_call_target="tpu_custom_call" | custom-call | tf_op jit(solution)/shard_map/lamb_all/pallas_call | solution.py:1013
  224.5 1.7 copy.84
  226.3 1.7 copy.85
  228.0 1.7 copy.86
  229.7 1.6 copy.87
  231.3 3.0 %copy.90 = bf16[2,1024,512]{2,1,0:T(8,128)(2,1)} copy(bf16[2,1024,512]{2,1,0:T(8,128)(2,1)} %get-tuple-element.204) | data formatting | bytes 4194304
  (6 shorter events, 0.1 us)
Async XLA Ops:
  0.7 0.7 copy-start
  1.4 8.5 %copy-start.7 = (s32[2,1,4]{2,1,0:T(1,128)}, s32[2,1,4]{2,1,0:T(1,128)S(1)}, u32[]{:S(2)}) copy-start(s32[2,1,4]{2,1,0:T(1,128)S(1)} %constant_dynamic-slice_fusion) | copy-start | bytes 100
  10.2 2.0 copy-start.1
  10.2 2.4 %copy-start.2 = (f32[64,512]{1,0:T(8,128)S(1)}, f32[64,512]{1,0:T(8,128)}, u32[]{:S(2)}) copy-start(f32[64,512]{1,0:T(8,128)} %refs_6_.3) | copy-start | bytes 393220
  10.2 2.4 %copy-start.4 = (f32[512,64]{0,1:T(8,128)S(1)}, f32[512,64]{0,1:T(8,128)}, u32[]{:S(2)}) copy-start(f32[512,64]{0,1:T(8,128)} %param.24) | copy-start | bytes 393220
  10.2 2.4 %copy-start.3 = (f32[2,64,64]{2,1,0:T(8,128)S(1)}, f32[2,64,64]{2,1,0:T(8,128)}, u32[]{:S(2)}) copy-start(f32[2,64,64]{2,1,0:T(8,128)} %refs_3_.3) | copy-start | bytes 98308
  83.7 47.6 %copy-start.5 = (f32[512,64]{0,1:T(8,128)S(1)}, f32[512,64]{0,1:T(8,128)}, u32[]{:S(2)}) copy-start(f32[512,64]{0,1:T(8,128)} %param.32) | copy-start | bytes 393220
  83.7 48.4 %copy-start.6 = (f32[512,64]{0,1:T(8,128)S(1)}, f32[512,64]{0,1:T(8,128)}, u32[]{:S(2)}) copy-start(f32[512,64]{0,1:T(8,128)} %param.33) | copy-start | bytes 393220

commit v3 on v2

--- a/solution.py
+++ b/solution.py
@@ -3,6 +3,7 @@
 
 import jax
 import jax.numpy as jnp
+import numpy as np
 from jax import lax
 from jax.experimental import pallas as pl
 from jax.experimental.pallas import tpu as pltpu
@@ -229,6 +230,46 @@
         total_ref[0, rows, pair * 128 : pair * 128 + 128] = jnp.where(low, totals[0], totals[1])
 
 
+def turn_tables_here(lengths_ref, steps_ref, cos_ref, sin_ref):
+    lanes = lane_ids((8, 128))
+    frequency = jnp.exp(((lanes & (HEAD_DIM - 1)) // 2).astype(jnp.float32) * (-2.0 * math.log(10000.0) / HEAD_DIM))
+    sign = jnp.where((lane_ids((1, 128)) & 1) == 0, -1.0, 1.0)
+    fine_cos, fine_sin = steps_ref[2:3], steps_ref[3:4]
+    for bucket in range(MICRO):
+        end0 = lengths_ref[bucket, 0]
+        end1 = end0 + lengths_ref[bucket, 1]
+        end2 = end1 + lengths_ref[bucket, 2]
+        row = lax.broadcasted_iota(jnp.int32, (8, 128), 0)
+        start = jnp.where(row == 0, 0, jnp.where(row == 1, end0, jnp.where(row == 2, end1, end2)))
+        angle = start.astype(jnp.float32) * frequency
+        run_cos, run_sin = jnp.cos(angle), jnp.sin(angle)
+
+        def chunk_tables(chunk, carry):
+            coarse = pl.ds(pl.multiple_of(chunk * 8, 8), 8)
+            coarse_cos, coarse_sin = steps_ref[0, coarse, :][:, None, :], steps_ref[1, coarse, :][:, None, :]
+            at_cos = (coarse_cos * fine_cos - coarse_sin * fine_sin).reshape(BQ, 128)
+            at_sin = (coarse_sin * fine_cos + coarse_cos * fine_sin).reshape(BQ, 128)
+            position = chunk * BQ + lax.broadcasted_iota(jnp.int32, (BQ, 128), 0)
+            first_cos, first_sin = run_cos[0:1], run_sin[0:1]
+            for run, end in enumerate((end0, end1, end2)):
+                first_cos = jnp.where(position >= end, run_cos[run + 1 : run + 2], first_cos)
+                first_sin = jnp.where(position >= end, run_sin[run + 1 : run + 2], first_sin)
+            rows = chunk_rows(chunk)
+            cos_ref[bucket, rows, :] = at_cos * first_cos + at_sin * first_sin
+            sin_ref[bucket, rows, :] = (at_sin * first_cos - at_cos * first_sin) * sign
+            return carry
+
+        lax.fori_loop(0, LEN // BQ, chunk_tables, 0)
+
+
+def position_steps():
+    lane = np.arange(128) % HEAD_DIM // 2
+    frequency = np.exp(lane.astype(np.float32) * np.float32(-2.0 * math.log(10000.0) / HEAD_DIM)).astype(np.float64)
+    step = np.arange(32)[:, None]
+    coarse, fine = step * 32 * frequency, step * frequency
+    return jnp.asarray(np.stack([np.cos(coarse), np.sin(coarse), np.cos(fine), np.sin(fine)]).astype(np.float32))
+
+
 def enter_rows(x_ref, small_ref, rows, bucket=0):
     normal, _ = norm_parts(x_ref[bucket, rows, :].astype(jnp.float32))
     return (normal * small_ref[0:1, :] + small_ref[1:2, :]).astype(jnp.bfloat16)
@@ -238,17 +279,16 @@
     return pl.ds(pl.multiple_of(chunk * BQ, BQ), BQ)
 
 
-def forward_kernel(
-    lengths_ref, x_ref, small_ref, cos_ref, sin_ref, *refs, alone
-):
+def forward_kernel(lengths_ref, x_ref, small_ref, *refs, alone):
     bucket = pl.program_id(0)
+    table = 0 if alone else bucket
     if alone:
-        in_ref, qkv_ref, mixed_ref, total_ref, enter_ref = refs
+        cos_ref, sin_ref, in_ref, qkv_ref, mixed_ref, total_ref, enter_ref = refs
     else:
-        shard_ref, qkv_ref, mixed_ref, total_ref = refs[:4]
-        kept = refs[4:8]
-        full = refs[8:12]
-        enter_ref, send, recv, own_sem, keep_sem = refs[12:]
+        steps_ref, shard_ref, qkv_ref, mixed_ref, total_ref, cos_ref, sin_ref = refs[:7]
+        kept = refs[7:11]
+        full = refs[11:15]
+        enter_ref, send, recv, own_sem, keep_sem = refs[15:]
         place = Place()
 
         def copies(which, stage):
@@ -275,6 +315,7 @@
             start_all(copies(early, 0))
             start_all(own_tiles())
             start_all(copies(late, 0))
+            turn_tables_here(lengths_ref, steps_ref, cos_ref, sin_ref)
 
     def normalise(chunk, carry):
         rows = chunk_rows(chunk)
@@ -296,18 +337,13 @@
             arrive_all(copies(late, 0))
             start_all(copies(late, 1))
 
-        @pl.when(bucket == 1)
-        def _():
-            arrive_all(copies(late, 3))
-            start_all(keeps())
-
     def weight(pair):
         cols = slice(pair * 384, pair * 384 + 384)
         return in_ref[:, cols] if alone else full[0][:, :, :, cols].reshape(D, 384)
 
     def project(chunk, carry):
         rows = chunk_rows(chunk)
-        project_rows(rows, enter_ref[0, rows, :], cos_ref[0, rows, :], sin_ref[0, rows, :], weight, qkv_ref)
+        project_rows(rows, enter_ref[0, rows, :], cos_ref[table, rows, :], sin_ref[table, rows, :], weight, qkv_ref)
         return carry
 
     lax.fori_loop(0, LEN // BQ, project, 0)
@@ -316,15 +352,20 @@
     def later(step, carry):
         if not alone:
 
-            @pl.when((bucket == 0) & (step == 1))
+            @pl.when((bucket == 0) & (step == 2))
             def _():
                 arrive_all(copies(late, 1))
                 start_all(copies(late, 2))
 
-            @pl.when((bucket == 0) & (step == 3))
+            @pl.when((bucket == 1) & (step == 1))
             def _():
                 arrive_all(copies(late, 2))
                 start_all(copies(late, 3))
+
+            @pl.when((bucket == 1) & (step == 3))
+            def _():
+                arrive_all(copies(late, 3))
+                start_all(keeps())
 
         first_row = pl.multiple_of(step * BQ, BQ)
         attend_forward(lengths_ref, bucket, first_row, pl.multiple_of(first_row - BQ, BQ), 2 * BQ, qkv_ref, mixed_ref, total_ref)
@@ -690,13 +731,6 @@
 
             lax.fori_loop(0, LEN // BQ, normalise, 0)
 
-    @pl.when(bucket == 1)
-    def _():
-        for item in early:
-            item.arrive(1)
-        for item in early:
-            item.start(2)
-
     shared = (qkv_ref, mixed_ref, gmixed_ref, total_ref, cos_ref, sin_ref, gproj_ref, dk_ref, dv_ref)
     attend_backward(lengths_ref, bucket, bucket, 0, 0, BQ, *shared)
 
@@ -710,7 +744,14 @@
             for item in early:
                 item.start(1)
 
-        @pl.when((bucket == 1) & (step == 2))
+        @pl.when((bucket == 1) & (step == 1))
+        def _():
+            for item in early:
+                item.arrive(1)
+            for item in early:
+                item.start(2)
+
+        @pl.when((bucket == 1) & (step == 3))
         def _():
             for item in early:
                 item.arrive(2)
@@ -782,7 +823,7 @@
         small_held[0] = jnp.concatenate(rows, 0)
         small_sum.start(0)
 
-        grads = [None, early[0].result().T, early[1].result(), early[2].result().T]
+        grads = [None, early[0].result().T, early[1].result(), early[2].result()]
         grad_refs[1][0] = grads[1][:HEAD_DIM]
         grad_refs[1][1] = grads[1][HEAD_DIM:]
         grad_refs[2][...] = grads[2]
@@ -914,16 +955,18 @@
     )(lengths, x, small, cosine, sine, in_mat)
 
 
-def gather_forward(lengths, x, small, cosine, sine, shard):
+def gather_forward(lengths, x, small, shard):
     shapes = [(4, 2, 64, 4 * width) for width in (IN_W, OUT_W, FF_W, FF_W)]
     return pl.pallas_call(
         functools.partial(forward_kernel, alone=False),
         grid=(MICRO,),
-        in_specs=[
-            SCALARS, per_bucket(LEN, D), whole((6, D)), per_bucket(LEN, 128), per_bucket(LEN, 128), whole((64, SHARD_W)),
-        ],
-        out_specs=[per_bucket(LEN, 3 * D), per_bucket(LEN, D), per_bucket(LEN, D)] + [ANYWHERE] * 4,
-        out_shape=[bf16(MICRO, LEN, 3 * D), bf16(MICRO, LEN, D), f32(MICRO, LEN, D)] + [bf16(*shape) for shape in shapes],
+        in_specs=[SCALARS, per_bucket(LEN, D), whole((6, D)), whole((4, 32, 128)), whole((64, SHARD_W))],
+        out_specs=[per_bucket(LEN, 3 * D), per_bucket(LEN, D), per_bucket(LEN, D)]
+        + [whole((MICRO, LEN, 128))] * 2
+        + [ANYWHERE] * 4,
+        out_shape=[bf16(MICRO, LEN, 3 * D), bf16(MICRO, LEN, D), f32(MICRO, LEN, D)]
+        + [f32(MICRO, LEN, 128)] * 2
+        + [bf16(*shape) for shape in shapes],
         scratch_shapes=[vmem16(*shape) for shape in shapes]
         + [
             vmem16(1, LEN, D),
@@ -934,7 +977,7 @@
         ],
         compiler_params=params(1, 1),
         name="gather_forward",
-    )(lengths, x, small, cosine, sine, shard)
+    )(lengths, x, small, position_steps(), shard)
 
 
 def mlp_both(lengths, x, cot, mixed, small, out_mat, up_mat, down_mat):
@@ -1034,20 +1077,20 @@
     small_first, small_second,
 ):
     lengths = lax.dynamic_slice_in_dim(clip_lengths, lax.axis_index("tensor"), 1, 1).reshape(MICRO, CLIPS)
-    cosine, sine = turn_tables(lengths)
     shard = tile_shard(in_proj, out_proj, up_proj, down_proj, True)
-    qkv, mixed, totals, in_full, out_full, up_full, down_full = gather_forward(lengths, frames, small_params, cosine, sine, shard)
+    qkv, mixed, totals, cosine, sine, in_full, out_full, up_full, down_full = gather_forward(lengths, frames, small_params, shard)
     block_out, gy1, gmixed, sums, gout, gup, gdown = mlp_both(
         lengths, frames, cotangent, mixed, small_params, out_full.reshape(D, D), up_full.reshape(D, FF), down_full.reshape(D, FF)
     )
     state = (
-        in_proj, in_first, in_second, out_proj, out_first, out_second, up_proj, up_first, up_second, down_proj, down_first, down_second,
+        in_proj, in_first, in_second, out_proj, out_first, out_second, up_proj, up_first, up_second, down_proj.T, down_first.T, down_second.T,
     )
     *grads, input_grad, everything, norm_squares = backward_tail(
         lengths, qkv, mixed, gmixed, totals, cosine, sine, frames, small_params, gy1, sums, in_full.reshape(D, 3 * D),
         gout.reshape(4, 2, 64, D), gup.reshape(4, 2, 64, FF), gdown.reshape(4, 2, 64, FF), state,
     )
-    outs = lamb_all(state, grads, small_params, small_first, small_second, everything, norm_squares)
+    outs = list(lamb_all(state, grads, small_params, small_first, small_second, everything, norm_squares))
+    outs[12:16] = [item.T for item in outs[12:16]]
     return (block_out, input_grad, *outs)
 
 

time: 235 us -> 205 us (0.87)
  Pallas kernels: 209 us -> 195 us
  local copies, waits for them, and re-layouts: 14.5 us -> 5.65 us
  other arithmetic: 10.5 us -> 3.38 us
    unnamed x25 -> x4, local copies, waits for them, and re-layouts: 13.2 us -> 4.75 us
    pallas_call x1, Pallas kernels: 70.3 us -> 62.9 us  [gather_forward(): pl.pallas_call(functools.partial(forward_kernel, alone=False), grid=(MICR...]
    pallas_call x1, Pallas kernels: 87.2 us -> 81.8 us  [backward_tail(): pl.pallas_call(tail_kernel, grid=(MICRO,), in_specs=[SCALARS, per_bucket(...]
    neg x1 -> x0, other arithmetic: 3.77 us -> none  [turn_tables(): sine = jnp.stack([-sine, sine], axis=-1).reshape(cosine.shape)]
    cos x1 -> x0, other arithmetic: 3.52 us -> none  [turn_tables(): cosine = jnp.repeat(jnp.cos(angles), 2, axis=-1)]
where the time goes in v3:
time: 205 us
  Pallas kernels  195 us (95%)
  local copies, waits for them, and re-layouts  5.65 us (3%)
  other arithmetic  3.38 us (2%)
    pallas_call x1, Pallas kernels, backward_tail(): pl.pallas_call(tail_kernel, grid=(MICRO,), in_specs=[SCALARS, per_bucket(...  81.8 us
    pallas_call x1, Pallas kernels, gather_forward(): pl.pallas_call(functools.partial(forward_kernel, alone=False), grid=(MICR...  62.9 us
    pallas_call x1, Pallas kernels, mlp_both(): pl.pallas_call(mlp_kernel, grid=(count, LEN // MLP_ROWS), in_specs=[SCALA...  46.5 us
    unnamed x4, local copies, waits for them, and re-layouts  4.75 us

profile of v3, /device:TPU:0, one launch (start us, length us, event | category | flops | bytes accessed | tf_op | source)
XLA Modules:
  0.0 204.9 jit_solution(9344604946960943793)
XLA Ops:
  0.7 0.0 copy-start
  0.7 0.7 copy-done
  1.4 0.6 constant_dynamic-slice_fusion
  1.9 0.8 convert.18
  2.8 0.1 copy.47
  2.9 0.9 bitcast_convert_fusion
  3.8 0.9 convert.19
  4.7 1.0 copy.44
  5.7 0.1 copy.45
  5.9 0.1 reshape.84
  6.0 0.7 pad_maximum_fusion.refs_1_
  6.7 62.9 %gather_forward.1 = (bf16[2,1024,1536]{2,1,0:T(8,128)(2,1)}, bf16[2,1024,512]{2,1,0:T(8,128)(2,1)}, f32[2,1024,512]{2,1,0:T(8,128)}, f32[2,1024,128]{2,1,0:T(8,1...) custom-call(s32[2,4]{1,0:T(2,128)} %bitcast.37, ...), custom_call_target="tpu_custom_call" | custom-call | tf_op jit(solution)/shard_map/gather_forward/pallas_call | solution.py:960
  69.6 46.5 %mlp_both.1 = (bf16[2,1024,512]{2,1,0:T(8,128)(2,1)}, f32[2,1024,512]{2,1,0:T(8,128)}, bf16[2,1024,512]{2,1,0:T(8,128)(2,1)}, f32[4,8,512]{2,1,0:T(8,128)}, bf16...) custom-call(s32[2,4]{1,0:T(2,128)} %bitcast.38, bf16[2,1024,512]{2,1,0:T(8,128)(2,1)} %x_ref.5, ...), custom_call_target="tpu_custom_call" | custom-call | tf_op jit(solution)/shard_map/mlp_both/pallas_call | solution.py:990
  116.1 81.8 %backward_tail.1 = (f32[64,2,192]{2,1,0:T(2,128)}, f32[2,64,64]{2,1,0:T(8,128)}, f32[64,512]{1,0:T(8,128)}, f32[64,512]{1,0:T(8,128)}, bf16[2,1024,512]{2,1,0:T(...) custom-call(s32[2,4]{1,0:T(2,128)} %bitcast.39, bf16[2,1024,1536]{2,1,0:T(8,128)(2,1)} %get-tuple-element.72.qkv_ref, ...), custom_call_target="tpu_custom_call" | custom-call | tf_op jit(solution)/shard_map/backward_tail/pallas_call | solution.py:1024
  197.9 3.9 %lamb_all.1 = (f32[64,2,192]{2,1,0:T(2,128)}, f32[64,2,192]{2,1,0:T(2,128)}, f32[64,2,192]{2,1,0:T(2,128)}, bf16[64,2,192]{2,1,0:T(2,128)(2,1)}, f32[2,64,64]{2,...) custom-call(f32[64,2,192]{2,1,0:T(2,128)} %refs_0_.4, ...), custom_call_target="tpu_custom_call" | custom-call | tf_op jit(solution)/shard_map/lamb_all/pallas_call | solution.py:1056
  201.8 3.0 %copy.49 = bf16[2,1024,512]{2,1,0:T(8,128)(2,1)} copy(bf16[2,1024,512]{2,1,0:T(8,128)(2,1)} %get-tuple-element.135) | data formatting | bytes 4194304
Async XLA Ops:
  0.7 0.7 copy-start

commit v4 on v3

--- a/solution.py
+++ b/solution.py
@@ -21,6 +21,9 @@
 STEP = 3
 
 BQ = 256
+BH = 128
+BLOCKS = LEN // BH
+KEYS = 3 * BH
 MLP_ROWS = 256
 VMEM_LIMIT = 62 * 1024 * 1024
 
@@ -92,12 +95,14 @@
 CORE, ALONG_Y, ALONG_X = "core", "y", "x"
 
 GATHERED = (
-    (0, 0, 32, IN_W, 0, "xy"),
-    (0, 32, 32, IN_W, 0, "yx"),
-    (1, 0, 64, OUT_W, IN_W, "xy"),
-    (2, 0, 64, FF_W, IN_W + OUT_W, "xy"),
-    (3, 0, 64, FF_W, IN_W + OUT_W + FF_W, "yx"),
+    (0, 0, 64, IN_W, 0, "xy"),
+    (1, 0, 64, OUT_W, IN_W, "yx"),
+    (2, 0, 32, FF_W, IN_W + OUT_W, "xy"),
+    (3, 0, 32, FF_W, IN_W + OUT_W + FF_W, "yx"),
+    (2, 32, 32, FF_W, IN_W + OUT_W, "xy"),
+    (3, 32, 32, FF_W, IN_W + OUT_W + FF_W, "yx"),
 )
+IN, OUT, UP_A, DOWN_A, UP_B, DOWN_B = range(6)
 SUMMED = (
     (1, 0, 64, OUT_W, "yx"),
     (2, 0, 64, FF_W, "yx"),
@@ -131,8 +136,8 @@
         }
 
 
-def tile_cols(tensor, width):
-    return pl.ds(pl.multiple_of(tensor * width, 128), width)
+def tile_cols(slot, width):
+    return pl.ds(pl.multiple_of(slot * width, 128), width)
 
 
 def remote(source, target, send, recv, device):
@@ -173,38 +178,37 @@
     def copy(source, target, slot, peer):
         return remote(source, target, send.at[index, slot], recv.at[index, slot], peers[peer])
 
-    def cols(y):
-        return tile_cols(y * 2 + place.c, width)
-
-    mine = cols(place.y)
+    def cols(slot):
+        return slice(slot * width, slot * width + width)
+
     if stage == 0:
         return [
-            copy(shard.at[rows, offset : offset + width], full.at[place.z, place.x, rows, mine], step - 1, step)
+            copy(shard.at[rows, offset : offset + width], full.at[place.z, place.x, rows, cols(0)], step - 1, step)
             for step in (1, 2, 3)
         ]
-    if stage == 3:
-        parts = [full.at[:, :, rows, cols(y)] for y in range(2)]
-        return [copy(part, part, 6 + y, CORE) for y, part in enumerate(parts)]
     if stage == 1:
-        part = full.at[:, place.x, rows, mine]
-        return [copy(part, part, 3, ALONG_X if order == "xy" else ALONG_Y)]
-    if order == "xy":
-        part = full.at[:, :, rows, mine]
-        return [copy(part, part, 4, ALONG_Y)]
-    parts = [full.at[:, place.x, rows, cols(y)] for y in range(2)]
-    return [copy(part, part, 4 + y, ALONG_X) for y, part in enumerate(parts)]
-
-
-def project_rows(rows, enter, cosine, sine, weight, qkv_ref):
-    for pair in range(PAIRS):
-        part = dot(enter, weight(pair))
-        for which in range(2):
-            piece = part[:, which * 128 : which * 128 + 128]
-            turned = piece * cosine + swap_pairs(piece) * sine
-            if which == 0:
-                turned = turned * (HEAD_DIM**-0.5)
-            qkv_ref[0, rows, pair * 384 + which * 128 : pair * 384 + which * 128 + 128] = turned.astype(jnp.bfloat16)
-        qkv_ref[0, rows, pair * 384 + 256 : pair * 384 + 384] = part[:, 256:].astype(jnp.bfloat16)
+        part = full.at[:, place.x, rows, cols(0)]
+        if order == "xy":
+            return [copy(part, part, 3, ALONG_X)]
+        return [copy(part, full.at[:, place.x, rows, cols(2)], 3, ALONG_Y)]
+    if stage == 2:
+        if order == "xy":
+            return [copy(full.at[:, :, rows, cols(0)], full.at[:, :, rows, cols(2)], 4, ALONG_Y)]
+        parts = [full.at[:, place.x, rows, cols(slot)] for slot in (0, 2)]
+        return [copy(part, part, 4 + index, ALONG_X) for index, part in enumerate(parts)]
+    slot = stage * 2 - 6
+    return [copy(full.at[:, :, rows, cols(slot)], full.at[:, :, rows, cols(slot + 1)], stage + 3, CORE)]
+
+
+def project_rows(rows, enter, cosine, sine, weight, qkv_ref, base):
+    part = dot(enter, weight)
+    for which in range(2):
+        piece = part[:, which * 128 : which * 128 + 128]
+        turned = piece * cosine + swap_pairs(piece) * sine
+        if which == 0:
+            turned = turned * (HEAD_DIM**-0.5)
+        qkv_ref[0, rows, base + which * 128 : base + which * 128 + 128] = turned.astype(jnp.bfloat16)
+    qkv_ref[0, rows, base + 256 : base + 384] = part[:, 256:].astype(jnp.bfloat16)
 
 
 def attend_forward(lengths_ref, bucket, first_row, first_key, keys, qkv_ref, mixed_ref, total_ref):
@@ -279,108 +283,227 @@
     return pl.ds(pl.multiple_of(chunk * BQ, BQ), BQ)
 
 
-def forward_kernel(lengths_ref, x_ref, small_ref, *refs, alone):
+def forward_kernel(lengths_ref, x_ref, small_ref, cos_ref, sin_ref, in_ref, qkv_ref, mixed_ref, total_ref, enter_ref):
     bucket = pl.program_id(0)
-    table = 0 if alone else bucket
-    if alone:
-        cos_ref, sin_ref, in_ref, qkv_ref, mixed_ref, total_ref, enter_ref = refs
-    else:
-        steps_ref, shard_ref, qkv_ref, mixed_ref, total_ref, cos_ref, sin_ref = refs[:7]
-        kept = refs[7:11]
-        full = refs[11:15]
-        enter_ref, send, recv, own_sem, keep_sem = refs[15:]
-        place = Place()
-
-        def copies(which, stage):
-            found = []
-            for index in which:
-                found += gather_copies(index, stage, place, shard_ref, full, send, recv)
-            return found
-
-        def own_tiles():
-            tiles = []
-            for weight, width, offset in ((0, IN_W, 0), (1, OUT_W, IN_W), (2, FF_W, IN_W + OUT_W), (3, FF_W, IN_W + OUT_W + FF_W)):
-                target = full[weight].at[place.z, place.x, :, tile_cols(place.y * 2 + place.c, width)]
-                tiles.append(pltpu.make_async_copy(shard_ref.at[:, offset : offset + width], target, own_sem.at[weight]))
-            return tiles
-
-        def keeps():
-            return [pltpu.make_async_copy(full[weight], kept[weight], keep_sem.at[weight]) for weight in range(4)]
-
-        early, late = (0, 1), (2, 3, 4)
-
-        @pl.when(bucket == 0)
-        def _():
-            meet(place)
-            start_all(copies(early, 0))
-            start_all(own_tiles())
-            start_all(copies(late, 0))
-            turn_tables_here(lengths_ref, steps_ref, cos_ref, sin_ref)
-
-    def normalise(chunk, carry):
+
+    def project(chunk, carry):
         rows = chunk_rows(chunk)
         enter_ref[0, rows, :] = enter_rows(x_ref, small_ref, rows)
-        return carry
-
-    lax.fori_loop(0, LEN // BQ, normalise, 0)
-
-    if not alone:
-
-        @pl.when(bucket == 0)
-        def _():
-            for tile in own_tiles():
-                tile.wait()
-            for stage in range(3):
-                arrive_all(copies(early, stage))
-                start_all(copies(early, stage + 1))
-            arrive_all(copies(early, 3))
-            arrive_all(copies(late, 0))
-            start_all(copies(late, 1))
-
-    def weight(pair):
-        cols = slice(pair * 384, pair * 384 + 384)
-        return in_ref[:, cols] if alone else full[0][:, :, :, cols].reshape(D, 384)
-
-    def project(chunk, carry):
-        rows = chunk_rows(chunk)
-        project_rows(rows, enter_ref[0, rows, :], cos_ref[table, rows, :], sin_ref[table, rows, :], weight, qkv_ref)
+        for pair in range(PAIRS):
+            weight = in_ref[:, pair * 384 : pair * 384 + 384]
+            project_rows(rows, enter_ref[0, rows, :], cos_ref[0, rows, :], sin_ref[0, rows, :], weight, qkv_ref, pair * 384)
         return carry
 
     lax.fori_loop(0, LEN // BQ, project, 0)
     attend_forward(lengths_ref, bucket, 0, 0, BQ, qkv_ref, mixed_ref, total_ref)
 
     def later(step, carry):
-        if not alone:
-
-            @pl.when((bucket == 0) & (step == 2))
-            def _():
-                arrive_all(copies(late, 1))
-                start_all(copies(late, 2))
-
-            @pl.when((bucket == 1) & (step == 1))
-            def _():
-                arrive_all(copies(late, 2))
-                start_all(copies(late, 3))
-
-            @pl.when((bucket == 1) & (step == 3))
-            def _():
-                arrive_all(copies(late, 3))
-                start_all(keeps())
-
         first_row = pl.multiple_of(step * BQ, BQ)
         attend_forward(lengths_ref, bucket, first_row, pl.multiple_of(first_row - BQ, BQ), 2 * BQ, qkv_ref, mixed_ref, total_ref)
         return carry
 
     lax.fori_loop(1, LEN // BQ, later, 0)
 
-    if not alone:
-
-        @pl.when(bucket == 1)
-        def _():
-            for keep in keeps():
-                keep.wait()
-            for stage in range(4):
-                sent_all(copies(early + late, stage))
+
+class RunLengths:
+    def __init__(self, ref):
+        self.ref, self.own = ref, lax.axis_index("tensor")
+
+    def __getitem__(self, where):
+        bucket, run = where
+        return self.ref[bucket, self.own, run]
+
+
+def band_biases(lengths, bias_ref):
+    def fill(index, carry):
+        bucket, block = index // BLOCKS, index % BLOCKS
+        position = block * BH + lax.broadcasted_iota(jnp.int32, (BH, 1), 0)
+        start, _ = run_starts(lengths, bucket, position)
+        lowest = jnp.maximum(start, position - (WINDOW - 1))
+        key = jnp.maximum(block - 2, 0) * BH + lax.broadcasted_iota(jnp.int32, (BH, KEYS), 1)
+        bias_ref[bucket, block] = jnp.where((key >= lowest) & (key <= position), 0.0, -1e30)
+        return carry
+
+    lax.fori_loop(0, MICRO * BLOCKS, fill, 0)
+
+
+def block_span(block):
+    first = max(block - 2, 0)
+    return slice(block * BH, block * BH + BH), slice(first * BH, block * BH + BH), (block + 1 - first) * BH
+
+
+def both_heads(tile):
+    return jnp.concatenate([head_lanes(tile, 0), head_lanes(tile, 1)], 0)
+
+
+def each_head(rows):
+    return jnp.where(lane_ids((BH, 128)) < HEAD_DIM, rows[:BH], rows[BH:])
+
+
+def attend_pair(bias_ref, bucket, block, qkv_ref, mixed_ref, total_ref):
+    rows, key_rows, keys = block_span(block)
+    bias = bias_ref[bucket, block, :, :keys]
+    scores = dot(both_heads(qkv_ref[0, rows, :128]), qkv_ref[0, key_rows, 128:256], NT)
+    scores = scores + jnp.concatenate([bias, bias], 0)
+    top = jnp.max(scores, -1, keepdims=True)
+    powers = jnp.exp(scores - top)
+    total = jnp.sum(powers, -1, keepdims=True)
+    out = dot(powers.astype(jnp.bfloat16), qkv_ref[0, key_rows, 256:384]) / total
+    mixed_ref[0, rows, :] = each_head(out).astype(jnp.bfloat16)
+    total_ref[0, rows, :] = each_head(jnp.broadcast_to(top + jnp.log(total), (2 * BH, 128)))
+
+
+def gather_kernel(
+    lengths_ref, x_ref, small_ref, steps_ref, in_ref, out_ref, up_ref, down_ref,
+    qkv_ref, mixed_ref, total_ref, cos_ref, sin_ref, *refs,
+):
+    kept, full, refs = refs[:4], refs[4:8], refs[8:]
+    shard_ref, enter_ref, bias_ref, send, recv, own_sem, keep_sem = refs
+    bucket = pl.program_id(1)
+    step = pl.program_id(0) * MICRO + bucket
+    place = Place()
+
+    def copies(stage, which):
+        found = []
+        for index in which:
+            found += gather_copies(index, stage, place, shard_ref, full, send, recv)
+        return found
+
+    def start(stage, *which):
+        start_all(copies(stage, which))
+
+    def arrive(stage, *which):
+        arrive_all(copies(stage, which))
+
+    def own_tiles():
+        tiles = []
+        for weight, width, offset in ((0, IN_W, 0), (1, OUT_W, IN_W), (2, FF_W, IN_W + OUT_W), (3, FF_W, IN_W + OUT_W + FF_W)):
+            target = full[weight].at[place.z, place.x, :, 0:width]
+            tiles.append(pltpu.make_async_copy(shard_ref.at[:, offset : offset + width], target, own_sem.at[weight]))
+        return tiles
+
+    def keep(index):
+        weight, row, count = GATHERED[index][:3]
+        rows = pl.ds(row, count)
+        return pltpu.make_async_copy(full[weight].at[:, :, rows, :], kept[weight].at[:, :, rows, :], keep_sem.at[index])
+
+    def finish(*which):
+        arrive(3, *which)
+        arrive(4, *which)
+        for index in which:
+            keep(index).start()
+
+    def begin():
+        lengths = RunLengths(lengths_ref)
+        heads = [in_ref[:, head, :] for head in range(2)]
+        pieces = [heads[head][:, part * HEAD_DIM : part * HEAD_DIM + HEAD_DIM] for part in range(3) for head in range(2)]
+        shard_ref[:, :IN_W] = jnp.concatenate(pieces, 1).astype(jnp.bfloat16)
+        shard_ref[:, IN_W : IN_W + OUT_W] = jnp.concatenate([out_ref[0].T, out_ref[1].T], 1).astype(jnp.bfloat16)
+        shard_ref[:, IN_W + OUT_W : IN_W + OUT_W + FF_W] = up_ref[...].astype(jnp.bfloat16)
+        shard_ref[:, IN_W + OUT_W + FF_W :] = down_ref[...].astype(jnp.bfloat16)
+        meet(place)
+        start(0, IN)
+        start(0, OUT, UP_A, DOWN_A, UP_B, DOWN_B)
+        start_all(own_tiles())
+        turn_tables_here(lengths, steps_ref, cos_ref, sin_ref)
+
+        def normalise(index, carry):
+            rows = chunk_rows(index % (LEN // BQ))
+            enter_ref[index // (LEN // BQ), rows, :] = enter_rows(x_ref, small_ref, rows, index // (LEN // BQ))
+            return carry
+
+        lax.fori_loop(0, MICRO * LEN // BQ, normalise, 0)
+        for tile in own_tiles():
+            tile.wait()
+        arrive(0, IN)
+        start(1, IN)
+        arrive(0, OUT)
+        start(1, OUT)
+        band_biases(lengths, bias_ref)
+        arrive(1, IN)
+
+    def at_0_1():
+        arrive(0, UP_A, DOWN_A)
+        start(1, DOWN_A, UP_A)
+        start(2, IN)
+        start(3, IN)
+        arrive(1, OUT)
+        start(2, OUT)
+
+    def at_2_0():
+        arrive(3, IN)
+
+    def at_2_1():
+        arrive(0, UP_B, DOWN_B)
+        start(1, DOWN_B, UP_B)
+
+    def at_2_2():
+        arrive(1, DOWN_A, UP_A)
+        start(2, DOWN_A, UP_A)
+        start(3, UP_A)
+
+    def at_4_0():
+        arrive(2, IN)
+        start(4, IN)
+
+    def at_5_2():
+        arrive(1, DOWN_B, UP_B)
+        start(2, DOWN_B, UP_B)
+        start(3, UP_B)
+
+    def at_6_0():
+        arrive(4, IN)
+        keep(IN).start()
+
+    def at_6_1():
+        arrive(2, OUT, DOWN_A)
+        start(3, OUT, DOWN_A)
+        start(4, OUT, DOWN_A)
+
+    def at_7_1():
+        arrive(2, UP_A)
+        start(4, UP_A)
+
+    def at_7_3():
+        finish(OUT, DOWN_A)
+
+    events = {
+        (0, 0): begin, (0, 1): at_0_1, (2, 0): at_2_0, (2, 1): at_2_1, (2, 2): at_2_2, (4, 0): at_4_0,
+        (5, 2): at_5_2, (6, 0): at_6_0, (6, 1): at_6_1, (7, 1): at_7_1, (7, 3): at_7_3,
+    }
+
+    def progress(point):
+        for (moment, where), event in events.items():
+            if where == point:
+                pl.when(step == moment)(event)
+
+    progress(0)
+    weight = full[0][:, :, :, tile_cols(pl.program_id(0), IN_W)].reshape(D, IN_W)
+
+    def project(chunk, carry):
+        rows = chunk_rows(chunk)
+        project_rows(rows, enter_ref[bucket, rows, :], cos_ref[bucket, rows, :], sin_ref[bucket, rows, :], weight, qkv_ref, 0)
+        return carry
+
+    lax.fori_loop(0, LEN // BQ, project, 0)
+    for point, blocks in enumerate(((0, 1, 2), (3, 4, 5), (6, 7))):
+        progress(point + 1)
+        for block in blocks:
+            attend_pair(bias_ref, bucket, block, qkv_ref, mixed_ref, total_ref)
+
+    @pl.when(step == PAIRS * MICRO - 1)
+    def _():
+        arrive(2, DOWN_B)
+        start(3, DOWN_B)
+        start(4, DOWN_B)
+        arrive(2, UP_B)
+        start(4, UP_B)
+        finish(UP_A)
+        finish(DOWN_B, UP_B)
+        for index in range(len(GATHERED)):
+            keep(index).wait()
+        for stage in range(5):
+            sent_all(copies(stage, range(len(GATHERED))))
 
 
 def mlp_kernel(
@@ -388,6 +511,7 @@
     block_ref, gy1_ref, gmixed_ref, sums_ref, gout_ref, gup_out_ref, gdown_ref,
     act_ref, gup_ref, keep_ref, enter_t, gmlp_t, gbranch_t,
 ):
+    lengths = RunLengths(lengths_ref) if len(lengths_ref.shape) == 3 else lengths_ref
     bucket = pl.program_id(0)
     chunk = pl.program_id(1)
     buckets = pl.num_programs(0)
@@ -409,7 +533,7 @@
     enter = (normal * small[2] + small[3]).astype(jnp.bfloat16)
     enter_t[:, rows] = enter.T
     position = chunk * MLP_ROWS + lax.broadcasted_iota(jnp.int32, (MLP_ROWS, 1), 0)
-    _, valid = run_starts(lengths_ref, bucket, position)
+    _, valid = run_starts(lengths, bucket, position)
     grad_y = jnp.where(valid, cot_ref[0].astype(jnp.float32), 0.0)
     grad_mlp = (small[5] * grad_y).astype(jnp.bfloat16)
     gmlp_t[:, rows] = grad_mlp.T
@@ -617,14 +741,14 @@
             return [copy(self.away(y, rows), self.got.at[y, :, :, rows, :], y, CORE) for y in range(2)]
         if stage == 1:
             if self.order == "yx":
-                return [copy(held.at[1 - place.y, :, :, rows, :], self.middle, 2, ALONG_Y)]
+                return [copy(held.at[1, :, :, rows, :], self.middle, 2, ALONG_Y)]
             return [copy(held.at[:, :, 1 - place.x, rows, :], self.middle, 2, ALONG_X)]
         if stage == 2:
             if self.order == "yx":
-                return [copy(held.at[place.y, :, 1 - place.x, rows, :], self.near, 3, ALONG_X)]
-            return [copy(held.at[1 - place.y, :, place.x, rows, :], self.near, 3, ALONG_Y)]
+                return [copy(held.at[0, :, 1 - place.x, rows, :], self.near, 3, ALONG_X)]
+            return [copy(held.at[1, :, place.x, rows, :], self.near, 3, ALONG_Y)]
         return [
-            copy(held.at[place.y, (place.z + step) % 4, place.x, rows, :], self.last.at[step - 1], 3 + step, step)
+            copy(held.at[0, (place.z + step) % 4, place.x, rows, :], self.last.at[step - 1], 3 + step, step)
             for step in (1, 2, 3)
         ]
 
@@ -647,11 +771,11 @@
             elif stage == 1:
                 for other in range(2):
                     if self.order == "yx":
-                        self.add((place.y, z, other, rows, slice(None)), self.middle[z, other])
+                        self.add((0, z, other, rows, slice(None)), self.middle[z, other])
                     else:
                         self.add((other, z, place.x, rows, slice(None)), self.middle[other, z])
             else:
-                self.add((place.y, z, place.x, rows, slice(None)), self.near[z])
+                self.add((0, z, place.x, rows, slice(None)), self.near[z])
             return carry
 
         lax.fori_loop(0, 4, block, 0)
@@ -659,7 +783,7 @@
     def result(self):
         arrive_all(self.copies(3))
         place = self.place
-        own = self.held[place.y, place.z, place.x, self.rows, :].astype(jnp.float32)
+        own = self.held[0, place.z, place.x, self.rows, :].astype(jnp.float32)
         for step in range(3):
             own = own + self.last[step].astype(jnp.float32)
         return own
@@ -685,6 +809,7 @@
     middle, near, last, refs = refs[:5], refs[5:10], refs[10:15], refs[15:]
     small_held, small_got, small_last, norm_held, norm_got, norm_last, refs = *refs[:6], refs[6:]
     send, recv, small_send, small_recv, norm_send, norm_recv, load_sem = refs
+    lengths = RunLengths(lengths_ref)
     bucket = pl.program_id(0)
     place = Place()
     sources = (None, gout_hbm, gup_hbm, gdown_hbm)
@@ -692,7 +817,7 @@
     def away(weight, width):
         if weight == 0:
             return lambda y, rows: away_in.at[y, :, :, rows, :]
-        return lambda y, rows: sources[weight].at[:, :, rows, tile_cols(y * 2 + (1 - place.c), width)]
+        return lambda y, rows: sources[weight].at[:, :, rows, tile_cols(y * 2 + 1, width)]
 
     def summing(which):
         return [
@@ -711,7 +836,7 @@
         found = []
         for weight, width in ((1, OUT_W), (2, FF_W), (3, FF_W)):
             for y in range(2):
-                source = sources[weight].at[:, :, :, tile_cols(y * 2 + place.c, width)]
+                source = sources[weight].at[:, :, :, tile_cols(y * 2, width)]
                 found.append(pltpu.make_async_copy(source, held[weight].at[y], load_sem.at[weight - 1, y]))
         return found
 
@@ -732,7 +857,7 @@
             lax.fori_loop(0, LEN // BQ, normalise, 0)
 
     shared = (qkv_ref, mixed_ref, gmixed_ref, total_ref, cos_ref, sin_ref, gproj_ref, dk_ref, dv_ref)
-    attend_backward(lengths_ref, bucket, bucket, 0, 0, BQ, *shared)
+    attend_backward(lengths, bucket, bucket, 0, 0, BQ, *shared)
 
     def later(step, carry):
         @pl.when((bucket == 0) & (step == 2))
@@ -759,7 +884,7 @@
                 item.start(3)
 
         first_row = pl.multiple_of(step * BQ, BQ)
-        attend_backward(lengths_ref, bucket, bucket, first_row, pl.multiple_of(first_row - BQ, BQ), 2 * BQ, *shared)
+        attend_backward(lengths, bucket, bucket, first_row, pl.multiple_of(first_row - BQ, BQ), 2 * BQ, *shared)
         return carry
 
     lax.fori_loop(1, LEN // BQ, later, 0)
@@ -774,7 +899,7 @@
         def tiles(step, carry):
             @pl.when(step < 2)
             def _():
-                away_in[step] = grad_tile(step * 2 + 1 - place.c)
+                away_in[step] = grad_tile(step * 2 + 1)
 
             @pl.when(step == 1)
             def _():
@@ -783,7 +908,7 @@
 
             @pl.when(step >= 2)
             def _():
-                held[0][step - 2] = grad_tile((step - 2) * 2 + place.c)
+                held[0][step - 2] = grad_tile((step - 2) * 2)
 
             return carry
 
@@ -945,7 +1070,7 @@
 def attention_forward(lengths, x, small, cosine, sine, in_mat):
     count = x.shape[0]
     return pl.pallas_call(
-        functools.partial(forward_kernel, alone=True),
+        forward_kernel,
         grid=(count,),
         in_specs=[SCALARS, per_bucket(LEN, D), whole((6, D)), per_bucket(LEN, 128), per_bucket(LEN, 128), whole((D, 3 * D))],
         out_specs=[per_bucket(LEN, 3 * D), per_bucket(LEN, D), per_bucket(LEN, D), per_bucket(LEN, D)],
@@ -955,29 +1080,33 @@
     )(lengths, x, small, cosine, sine, in_mat)
 
 
-def gather_forward(lengths, x, small, shard):
+def gather_forward(lengths, x, small, weights):
     shapes = [(4, 2, 64, 4 * width) for width in (IN_W, OUT_W, FF_W, FF_W)]
+
+    def per_pair(width):
+        return pl.BlockSpec((1, LEN, width), lambda pair, bucket: (bucket, 0, pair))
+
     return pl.pallas_call(
-        functools.partial(forward_kernel, alone=False),
-        grid=(MICRO,),
-        in_specs=[SCALARS, per_bucket(LEN, D), whole((6, D)), whole((4, 32, 128)), whole((64, SHARD_W))],
-        out_specs=[per_bucket(LEN, 3 * D), per_bucket(LEN, D), per_bucket(LEN, D)]
-        + [whole((MICRO, LEN, 128))] * 2
-        + [ANYWHERE] * 4,
+        gather_kernel,
+        grid=(PAIRS, MICRO),
+        in_specs=[SCALARS, whole((MICRO, LEN, D)), whole((6, D)), whole((4, 32, 128))] + [whole(item.shape) for item in weights],
+        out_specs=[per_pair(IN_W), per_pair(128), per_pair(128)] + [whole((MICRO, LEN, 128))] * 2 + [ANYWHERE] * 4,
         out_shape=[bf16(MICRO, LEN, 3 * D), bf16(MICRO, LEN, D), f32(MICRO, LEN, D)]
         + [f32(MICRO, LEN, 128)] * 2
         + [bf16(*shape) for shape in shapes],
         scratch_shapes=[vmem16(*shape) for shape in shapes]
         + [
-            vmem16(1, LEN, D),
-            pltpu.SemaphoreType.DMA((5, 8)),
-            pltpu.SemaphoreType.DMA((5, 8)),
+            vmem16(64, SHARD_W),
+            vmem16(MICRO, LEN, D),
+            vmem32(MICRO, BLOCKS, BH, KEYS),
+            pltpu.SemaphoreType.DMA((6, 8)),
+            pltpu.SemaphoreType.DMA((6, 8)),
             pltpu.SemaphoreType.DMA((4,)),
-            pltpu.SemaphoreType.DMA((4,)),
+            pltpu.SemaphoreType.DMA((6,)),
         ],
-        compiler_params=params(1, 1),
+        compiler_params=params(2, 1),
         name="gather_forward",
-    )(lengths, x, small, position_steps(), shard)
+    )(lengths, x, small, position_steps(), *weights)
 
 
 def mlp_both(lengths, x, cot, mixed, small, out_mat, up_mat, down_mat):
@@ -1061,13 +1190,10 @@
     )(*state, *grads, small, small_first, small_second, everything, norm_squares)
 
 
-def tile_shard(in_proj, out_proj, up_proj, down_proj, paired):
+def tile_shard(in_proj, out_proj, up_proj, down_proj):
     depth, heads_here, _ = in_proj.shape
-    in_cols = in_proj.reshape(depth, heads_here, 3, HEAD_DIM)
-    if paired:
-        in_cols = in_cols.transpose(0, 2, 1, 3)
     out_cols = out_proj.reshape(heads_here * HEAD_DIM, depth).T
-    parts = [in_cols.reshape(depth, -1), out_cols, up_proj, down_proj.T]
+    parts = [in_proj.reshape(depth, -1), out_cols, up_proj, down_proj.T]
     return jnp.concatenate(parts, axis=1).astype(jnp.bfloat16)
 
 
@@ -1076,9 +1202,10 @@
     in_first, in_second, out_first, out_second, up_first, up_second, down_first, down_second,
     small_first, small_second,
 ):
-    lengths = lax.dynamic_slice_in_dim(clip_lengths, lax.axis_index("tensor"), 1, 1).reshape(MICRO, CLIPS)
-    shard = tile_shard(in_proj, out_proj, up_proj, down_proj, True)
-    qkv, mixed, totals, cosine, sine, in_full, out_full, up_full, down_full = gather_forward(lengths, frames, small_params, shard)
+    lengths = clip_lengths
+    qkv, mixed, totals, cosine, sine, in_full, out_full, up_full, down_full = gather_forward(
+        lengths, frames, small_params, (in_proj, out_proj, up_proj, down_proj.T)
+    )
     block_out, gy1, gmixed, sums, gout, gup, gdown = mlp_both(
         lengths, frames, cotangent, mixed, small_params, out_full.reshape(D, D), up_full.reshape(D, FF), down_full.reshape(D, FF)
     )
@@ -1112,7 +1239,7 @@
     heads_here = in_proj.shape[1]
     ff_here = up_proj.shape[1]
 
-    shard = tile_shard(in_proj, out_proj, up_proj, down_proj, False)
+    shard = tile_shard(in_proj, out_proj, up_proj, down_proj)
     gathered = lax.all_gather(shard, ("dp", "tensor"), axis=0)
     gathered = gathered.reshape(dp_size, tensor_size, depth, shard.shape[1])
     gathered = jnp.moveaxis(gathered, 1, 2).reshape(D, tensor_size, shard.shape[1])

time: 205 us -> 204 us (level)
  Pallas kernels: 195 us -> 200 us
  other arithmetic: 3.38 us -> 0 us
  local copies, waits for them, and re-layouts: 5.65 us -> 3.05 us
    pallas_call x1, Pallas kernels: 81.8 us -> 85.7 us  [backward_tail(): pl.pallas_call(tail_kernel, grid=(MICRO,), in_specs=[SCALARS, per_bucket(...]
    another operation x3 -> x0, other arithmetic: 2.69 us -> none
    unnamed x4 -> x1, local copies, waits for them, and re-layouts: 4.75 us -> 3.05 us
where the time goes in v4:
time: 204 us
  Pallas kernels  200 us (98%)
  local copies, waits for them, and re-layouts  3.05 us (1%)
    pallas_call x1, Pallas kernels, backward_tail(): pl.pallas_call(tail_kernel, grid=(MICRO,), in_specs=[SCALARS, per_bucket(...  85.7 us
    pallas_call x1, Pallas kernels, gather_forward(): pl.pallas_call(gather_kernel, grid=(PAIRS, MICRO), in_specs=[SCALARS, who...  63.7 us
    pallas_call x1, Pallas kernels, mlp_both(): pl.pallas_call(mlp_kernel, grid=(count, LEN // MLP_ROWS), in_specs=[SCALA...  46.6 us

profile of v4, /device:TPU:0, one launch (start us, length us, event | category | flops | bytes accessed | tf_op | source)
XLA Modules:
  0.0 203.6 jit_solution(845017960526497431)
XLA Ops:
  0.7 63.7 %gather_forward.1 = (bf16[2,1024,1536]{2,1,0:T(8,128)(2,1)}, bf16[2,1024,512]{2,1,0:T(8,128)(2,1)}, f32[2,1024,512]{2,1,0:T(8,128)}, f32[2,1024,128]{2,1,0:T(8,1...) custom-call(s32[2,4,4]{2,1,0:T(4,128)} %lengths_ref.5, ...), custom_call_target="tpu_custom_call" | custom-call | tf_op jit(solution)/shard_map/gather_forward/pallas_call | solution.py:1089
  64.4 46.6 %mlp_both.1 = (bf16[2,1024,512]{2,1,0:T(8,128)(2,1)}, f32[2,1024,512]{2,1,0:T(8,128)}, bf16[2,1024,512]{2,1,0:T(8,128)(2,1)}, f32[4,8,512]{2,1,0:T(8,128)}, bf16...) custom-call(s32[2,4,4]{2,1,0:T(4,128)} %lengths_ref.5, bf16[2,1024,512]{2,1,0:T(8,128)(2,1)} %x_ref.5, ...), custom_call_target="tpu_custom_call" | custom-call | tf_op jit(solution)/shard_map/mlp_both/pallas_call | solution.py:1119
  111.0 85.7 %backward_tail.1 = (f32[64,2,192]{2,1,0:T(2,128)}, f32[2,64,64]{2,1,0:T(8,128)}, f32[64,512]{1,0:T(8,128)}, f32[64,512]{1,0:T(8,128)}, bf16[2,1024,512]{2,1,0:T(...) custom-call(s32[2,4,4]{2,1,0:T(4,128)} %lengths_ref.5, bf16[2,1024,1536]{2,1,0:T(8,128)(2,1)} %get-tuple-element.72.qkv_ref, ...), custom_call_target="tpu_custom_call" | custom-call | tf_op jit(solution)/shard_map/backward_tail/pallas_call | solution.py:1153
  196.7 3.9 %lamb_all.1 = (f32[64,2,192]{2,1,0:T(2,128)}, f32[64,2,192]{2,1,0:T(2,128)}, f32[64,2,192]{2,1,0:T(2,128)}, bf16[64,2,192]{2,1,0:T(2,128)(2,1)}, f32[2,64,64]{2,...) custom-call(f32[64,2,192]{2,1,0:T(2,128)} %refs_0_.3, ...), custom_call_target="tpu_custom_call" | custom-call | tf_op jit(solution)/shard_map/lamb_all/pallas_call | solution.py:1185
  200.6 3.0 %copy.43 = bf16[2,1024,512]{2,1,0:T(8,128)(2,1)} copy(bf16[2,1024,512]{2,1,0:T(8,128)(2,1)} %get-tuple-element.135) | data formatting | bytes 4194304

commit v5 on v4

--- a/solution.py
+++ b/solution.py
@@ -24,7 +24,8 @@
 BH = 128
 BLOCKS = LEN // BH
 KEYS = 3 * BH
-MLP_ROWS = 256
+MLP_ROWS = 512
+LAST_ROWS = 512
 VMEM_LIMIT = 62 * 1024 * 1024
 
 beta_first = 0.5
@@ -105,9 +106,11 @@
 IN, OUT, UP_A, DOWN_A, UP_B, DOWN_B = range(6)
 SUMMED = (
     (1, 0, 64, OUT_W, "yx"),
-    (2, 0, 64, FF_W, "yx"),
-    (3, 0, 64, FF_W, "xy"),
-    (0, 0, 32, IN_W, "xy"),
+    (2, 0, 32, FF_W, "yx"),
+    (3, 0, 32, FF_W, "xy"),
+    (2, 32, 32, FF_W, "yx"),
+    (3, 32, 32, FF_W, "xy"),
+    (0, 0, 32, IN_W, "yx"),
     (0, 32, 32, IN_W, "yx"),
 )
 
@@ -480,12 +483,7 @@
     progress(0)
     weight = full[0][:, :, :, tile_cols(pl.program_id(0), IN_W)].reshape(D, IN_W)
 
-    def project(chunk, carry):
-        rows = chunk_rows(chunk)
-        project_rows(rows, enter_ref[bucket, rows, :], cos_ref[bucket, rows, :], sin_ref[bucket, rows, :], weight, qkv_ref, 0)
-        return carry
-
-    lax.fori_loop(0, LEN // BQ, project, 0)
+    project_rows(slice(None), enter_ref[bucket], cos_ref[bucket], sin_ref[bucket], weight, qkv_ref, 0)
     for point, blocks in enumerate(((0, 1, 2), (3, 4, 5), (6, 7))):
         progress(point + 1)
         for block in blocks:
@@ -729,7 +727,7 @@
         self.send, self.recv = send, recv
         self.rows = pl.ds(self.row, self.count)
 
-    def copies(self, stage):
+    def copies(self, stage, which=(0, 1)):
         place = self.place
         peers = place.peers()
 
@@ -738,7 +736,7 @@
 
         held, rows = self.held, self.rows
         if stage == 0:
-            return [copy(self.away(y, rows), self.got.at[y, :, :, rows, :], y, CORE) for y in range(2)]
+            return [copy(self.away(y, rows), self.got.at[y, :, :, rows, :], y, CORE) for y in which]
         if stage == 1:
             if self.order == "yx":
                 return [copy(held.at[1, :, :, rows, :], self.middle, 2, ALONG_Y)]
@@ -752,20 +750,20 @@
             for step in (1, 2, 3)
         ]
 
-    def start(self, stage):
-        start_all(self.copies(stage))
+    def start(self, stage, which=(0, 1)):
+        start_all(self.copies(stage, which))
 
     def add(self, where, more):
         held = self.held
         held[where] = (held[where].astype(jnp.float32) + more.astype(jnp.float32)).astype(jnp.bfloat16)
 
-    def arrive(self, stage):
-        arrive_all(self.copies(stage))
+    def arrive(self, stage, which=(0, 1)):
+        arrive_all(self.copies(stage, which))
         place, rows = self.place, self.rows
 
         def block(z, carry):
             if stage == 0:
-                for y in range(2):
+                for y in which:
                     for x in range(2):
                         self.add((y, z, x, rows, slice(None)), self.got[y, z, x, rows, :])
             elif stage == 1:
@@ -798,19 +796,65 @@
     return (4, 2, count, width) if order == "yx" else (2, 4, count, width)
 
 
+def back_pair(bias_ref, bucket, slot, block, qkv_ref, mixed_ref, gmixed_ref, total_ref, cos_ref, sin_ref, gproj_ref, dk_ref, dv_ref):
+    rows, key_rows, keys = block_span(block)
+    bias = bias_ref[bucket, block, :, :keys]
+    keys_rot = qkv_ref[0, key_rows, 128:256]
+    query = both_heads(qkv_ref[0, rows, :128])
+    grad = gmixed_ref[0, rows, :]
+    product = grad.astype(jnp.float32) * mixed_ref[0, rows, :].astype(jnp.float32)
+    inner = jnp.sum(both_heads(product), -1, keepdims=True)
+    grad = both_heads(grad)
+    totals = total_ref[0, rows, :]
+    total = jnp.concatenate([totals[:, 0:1], totals[:, HEAD_DIM : HEAD_DIM + 1]], 0)
+    attn = jnp.exp(dot(query, keys_rot, NT) + jnp.concatenate([bias, bias], 0) - total)
+    grad_attn = dot(grad, qkv_ref[0, key_rows, 256:384], NT)
+    grad_scores = (attn * (grad_attn - inner)).astype(jnp.bfloat16)
+    grad_v = dot(attn.astype(jnp.bfloat16), grad, TN)
+    grad_k = dot(grad_scores, query, TN)
+    grad_q = each_head(dot(grad_scores, keys_rot)) * (HEAD_DIM**-0.5)
+    turned = grad_q * cos_ref[0, rows, :] - swap_pairs(grad_q) * sin_ref[0, rows, :]
+    gproj_ref[bucket, rows, pair_cols(slot, 0)] = turned.astype(jnp.bfloat16)
+    old = keys - BH
+    if old:
+        before = slice(key_rows.start, key_rows.start + old)
+        dk_ref[before, :] += grad_k[:old]
+        dv_ref[before, :] += grad_v[:old]
+    dk_ref[rows, :] = grad_k[old:]
+    dv_ref[rows, :] = grad_v[old:]
+
+
+def pair_cols(slot, which):
+    return pl.ds(pl.multiple_of(slot * IN_W + which * 128, 128), 128)
+
+
+def finish_pair(bucket, slot, cos_ref, sin_ref, gproj_ref, dk_ref, dv_ref):
+    def finish(chunk, carry):
+        rows = chunk_rows(chunk)
+        grad_k = dk_ref[rows, :]
+        turned = grad_k * cos_ref[0, rows, :] - swap_pairs(grad_k) * sin_ref[0, rows, :]
+        gproj_ref[bucket, rows, pair_cols(slot, 1)] = turned.astype(jnp.bfloat16)
+        gproj_ref[bucket, rows, pair_cols(slot, 2)] = dv_ref[rows, :].astype(jnp.bfloat16)
+        return carry
+
+    lax.fori_loop(0, LEN // BQ, finish, 0)
+
+
 def tail_kernel(
-    lengths_ref, qkv_ref, mixed_ref, gmixed_ref, total_ref, cos_ref, sin_ref, x_ref, small_ref, gy1_ref, sums_ref, in_ref,
-    gout_hbm, gup_hbm, gdown_hbm, *refs,
+    lengths_ref, qkv_ref, mixed_ref, gmixed_ref, total_ref, cos_ref, sin_ref, x_ref, small_ref, sums_ref,
+    gy1_hbm, in_hbm, gout_hbm, gup_hbm, gdown_hbm, *refs,
 ):
+    count = len(SUMMED)
     state, refs = refs[:12], refs[12:]
     grad_refs, (xgrad_ref, all_ref, norm_ref), refs = refs[:4], refs[4:7], refs[7:]
-    gproj_ref, dk_ref, dv_ref, enter_t, away_in, small_acc, refs = *refs[:6], refs[6:]
+    gproj_ref, dk_ref, dv_ref, enter_t, bias_ref, gy1_ref, in_ref, away_in, small_acc, refs = *refs[:9], refs[9:]
     held, got, refs = refs[:4], refs[4:8], refs[8:]
-    middle, near, last, refs = refs[:5], refs[5:10], refs[10:15], refs[15:]
+    middle, near, last, refs = refs[:count], refs[count : 2 * count], refs[2 * count : 3 * count], refs[3 * count :]
     small_held, small_got, small_last, norm_held, norm_got, norm_last, refs = *refs[:6], refs[6:]
-    send, recv, small_send, small_recv, norm_send, norm_recv, load_sem = refs
-    lengths = RunLengths(lengths_ref)
-    bucket = pl.program_id(0)
+    send, recv, small_send, small_recv, norm_send, norm_recv, load_sem, late_sem = refs
+    bucket = pl.program_id(1)
+    slot = PAIRS - 1 - pl.program_id(0)
+    step = pl.program_id(0) * MICRO + bucket
     place = Place()
     sources = (None, gout_hbm, gup_hbm, gdown_hbm)
 
@@ -819,16 +863,14 @@
             return lambda y, rows: away_in.at[y, :, :, rows, :]
         return lambda y, rows: sources[weight].at[:, :, rows, tile_cols(y * 2 + 1, width)]
 
-    def summing(which):
-        return [
-            Summing(
-                index, place, away(SUMMED[index][0], SUMMED[index][3]), held[SUMMED[index][0]], got[SUMMED[index][0]],
-                middle[index], near[index], last[index], send, recv,
-            )
-            for index in which
-        ]
-
-    early, late = summing((0, 1, 2)), summing((3, 4))
+    items = [
+        Summing(
+            index, place, away(item[0], item[3]), held[item[0]], got[item[0]], middle[index], near[index], last[index], send, recv
+        )
+        for index, item in enumerate(SUMMED)
+    ]
+    out_sum, up_a, down_a, up_b, down_b = items[:5]
+    early, late = items[:5], items[5:]
     small_sum = Everywhere(place, small_held, small_got, small_last, small_send, small_recv)
     norm_sum = Everywhere(place, norm_held, norm_got, norm_last, norm_send, norm_recv)
 
@@ -840,103 +882,111 @@
                 found.append(pltpu.make_async_copy(source, held[weight].at[y], load_sem.at[weight - 1, y]))
         return found
 
-    @pl.when(bucket == 0)
-    def _():
+    def late_loads():
+        return [pltpu.make_async_copy(gy1_hbm, gy1_ref, late_sem.at[0]), pltpu.make_async_copy(in_hbm, in_ref, late_sem.at[1])]
+
+    def advance(stage, *which):
+        for item in which:
+            item.arrive(stage)
+            item.start(stage + 1)
+
+    def begin():
+        lengths = RunLengths(lengths_ref)
         meet(place)
         for item in early:
             item.start(0)
         start_all(loads())
-        for index in range(MICRO):
-
-            def normalise(chunk, carry):
-                rows = chunk_rows(chunk)
-                cols = pl.ds(pl.multiple_of(index * LEN + chunk * BQ, BQ), BQ)
-                enter_t[:, cols] = enter_rows(x_ref, small_ref, rows, index).T
-                return carry
-
-            lax.fori_loop(0, LEN // BQ, normalise, 0)
+        start_all(late_loads())
+        band_biases(lengths, bias_ref)
+
+        def normalise(index, carry):
+            half, chunk = index // (LEN // BQ), index % (LEN // BQ)
+            cols = pl.ds(pl.multiple_of(index * BQ, BQ), BQ)
+            enter_t[:, cols] = enter_rows(x_ref, small_ref, chunk_rows(chunk), half).T
+            return carry
+
+        lax.fori_loop(0, MICRO * LEN // BQ, normalise, 0)
+
+    def at_0_1():
+        for load in loads():
+            load.wait()
+        advance(0, out_sum, up_a, down_a)
+
+    events = {
+        (0, 0): begin,
+        (0, 1): at_0_1,
+        (0, 2): lambda: advance(0, up_b, down_b),
+        (2, 1): lambda: advance(1, out_sum),
+        (2, 2): lambda: advance(1, down_a),
+        (3, 1): lambda: advance(1, up_a),
+        (4, 0): lambda: advance(1, down_b),
+        (4, 1): lambda: advance(2, out_sum),
+        (5, 0): lambda: advance(1, up_b),
+        (5, 1): lambda: advance(2, up_a),
+        (6, 0): lambda: advance(2, up_b, down_a),
+    }
+
+    def progress(point):
+        for (moment, where), event in events.items():
+            if where == point:
+                pl.when(step == moment)(event)
 
     shared = (qkv_ref, mixed_ref, gmixed_ref, total_ref, cos_ref, sin_ref, gproj_ref, dk_ref, dv_ref)
-    attend_backward(lengths, bucket, bucket, 0, 0, BQ, *shared)
-
-    def later(step, carry):
-        @pl.when((bucket == 0) & (step == 2))
+    for point, blocks in enumerate(((0, 1, 2), (3, 4, 5), (6, 7))):
+        progress(point)
+        for block in blocks:
+            back_pair(bias_ref, bucket, slot, block, *shared)
+    finish_pair(bucket, slot, cos_ref, sin_ref, gproj_ref, dk_ref, dv_ref)
+
+    def grad_tile():
+        right = gproj_ref[:, :, tile_cols(slot, IN_W)].reshape(MICRO * LEN, IN_W)
+        return dot(enter_t[...], right).astype(jnp.bfloat16).reshape(4, 2, 64, IN_W)
+
+    @pl.when((bucket == 1) & (slot % 2 == 1))
+    def _():
+        away_in[slot // 2] = grad_tile()
+
+    @pl.when((bucket == 1) & (slot % 2 == 0))
+    def _():
+        held[0][slot // 2] = grad_tile()
+
+    for which in range(2):
+
+        @pl.when((bucket == 1) & (slot == which * 2 + 1))
         def _():
-            for load in loads():
-                load.wait()
-            for item in early:
-                item.arrive(0)
-            for item in early:
-                item.start(1)
-
-        @pl.when((bucket == 1) & (step == 1))
-        def _():
-            for item in early:
-                item.arrive(1)
-            for item in early:
-                item.start(2)
-
-        @pl.when((bucket == 1) & (step == 3))
-        def _():
-            for item in early:
-                item.arrive(2)
-            for item in early:
-                item.start(3)
-
-        first_row = pl.multiple_of(step * BQ, BQ)
-        attend_backward(lengths, bucket, bucket, first_row, pl.multiple_of(first_row - BQ, BQ), 2 * BQ, *shared)
-        return carry
-
-    lax.fori_loop(1, LEN // BQ, later, 0)
-    finish_keys(bucket, cos_ref, sin_ref, gproj_ref, dk_ref, dv_ref)
-
-    @pl.when(bucket == 1)
+            for item in late:
+                item.start(0, (which,))
+
+    @pl.when((bucket == 1) & (slot == 2))
     def _():
-        def grad_tile(tensor):
-            right = gproj_ref[:, :, tile_cols(tensor, IN_W)].reshape(MICRO * LEN, IN_W)
-            return dot(enter_t[...], right).astype(jnp.bfloat16).reshape(4, 2, 64, IN_W)
-
-        def tiles(step, carry):
-            @pl.when(step < 2)
-            def _():
-                away_in[step] = grad_tile(step * 2 + 1)
-
-            @pl.when(step == 1)
-            def _():
-                for item in late:
-                    item.start(0)
-
-            @pl.when(step >= 2)
-            def _():
-                held[0][step - 2] = grad_tile((step - 2) * 2)
-
-            return carry
-
-        lax.fori_loop(0, 4, tiles, 0)
+        for item in late:
+            item.arrive(0, (1,))
+            item.start(1)
+
+    @pl.when((bucket == 1) & (slot == 0))
+    def _():
+        for item in late:
+            item.arrive(0, (0,))
+            item.arrive(1)
+            item.start(2)
         small_acc[...] = jnp.zeros_like(small_acc)
-        in_full = in_ref[...]
+        for load in late_loads():
+            load.wait()
 
         def data_grad(step, carry):
-            for stage, moment in ((0, 1), (1, 4), (2, 7)):
-
-                @pl.when(step == moment)
-                def _():
-                    for item in late:
-                        item.arrive(stage)
-                    for item in late:
-                        item.start(stage + 1)
-
-            index = step // (LEN // BQ)
-            rows = chunk_rows(step % (LEN // BQ))
-            grad_enter = dot(gproj_ref[index, rows, :], in_full, NT)
+            for stage, item, moment in ((2, down_b, 1), (2, late[0], 2), (2, late[1], 3)):
+                pl.when(step == moment)(lambda: advance(stage, item))
+            index = step // (LEN // LAST_ROWS)
+            rows = pl.ds(pl.multiple_of(step % (LEN // LAST_ROWS) * LAST_ROWS, LAST_ROWS), LAST_ROWS)
+            grad_enter = dot(gproj_ref[index, rows, :], in_ref[...], NT)
             normal, inverse = norm_parts(x_ref[index, rows, :].astype(jnp.float32))
             back = norm_back(grad_enter * small_ref[0:1, :], normal, inverse)
             xgrad_ref[index, rows, :] = (gy1_ref[index, rows, :] + back).astype(jnp.bfloat16)
-            small_acc[0] += jnp.sum((grad_enter * normal).reshape(BQ // 8, 8, D), 0)
-            small_acc[1] += jnp.sum(grad_enter.reshape(BQ // 8, 8, D), 0)
+            small_acc[0] += jnp.sum((grad_enter * normal).reshape(LAST_ROWS // 8, 8, D), 0)
+            small_acc[1] += jnp.sum(grad_enter.reshape(LAST_ROWS // 8, 8, D), 0)
             return carry
 
-        lax.fori_loop(0, MICRO * LEN // BQ, data_grad, 0)
+        lax.fori_loop(0, MICRO * LEN // LAST_ROWS, data_grad, 0)
 
         rows = [jnp.sum(small_acc[row], 0, keepdims=True) for row in range(2)]
         rows += [jnp.sum(sums_ref[row], 0, keepdims=True) for row in range(4)]
@@ -948,7 +998,12 @@
         small_held[0] = jnp.concatenate(rows, 0)
         small_sum.start(0)
 
-        grads = [None, early[0].result().T, early[1].result(), early[2].result()]
+        grads = [
+            None,
+            out_sum.result().T,
+            jnp.concatenate([up_a.result(), up_b.result()], 0),
+            jnp.concatenate([down_a.result(), down_b.result()], 0),
+        ]
         grad_refs[1][0] = grads[1][:HEAD_DIM]
         grad_refs[1][1] = grads[1][HEAD_DIM:]
         grad_refs[2][...] = grads[2]
@@ -986,8 +1041,9 @@
 
 def lamb_kernel(*refs):
     state, grads, refs = refs[:12], refs[12:16], refs[16:]
-    small_ref, small_first_ref, small_second_ref, all_ref, norm_ref, refs = *refs[:5], refs[5:]
-    outs, (grad_ref, new_ref, first_ref, second_ref, norms_ref) = refs[:16], refs[16:]
+    small_ref, small_first_ref, small_second_ref, all_ref, norm_ref, xgrad_ref, refs = *refs[:6], refs[6:]
+    outs, (grad_ref, new_ref, first_ref, second_ref, norms_ref, xgrad_out_ref) = refs[:16], refs[16:]
+    xgrad_out_ref[...] = xgrad_ref[...]
     weight_norm = jnp.sqrt(all_ref[6:7, 0:128])
     update_sq = norm_ref[0:1, :]
     ratio = learn_rate * weight_norm * lax.rsqrt(update_sq + 1e-12)
@@ -1149,45 +1205,50 @@
 def backward_tail(lengths, qkv, mixed, gmixed, totals, cosine, sine, x, small, gy1, sums, in_mat, gout, gup, gdown, state):
     widths = (IN_W, OUT_W, FF_W, FF_W)
     dma = pltpu.SemaphoreType.DMA
+    count = len(SUMMED)
     grad_shapes = [f32(*state[3 * which].shape) for which in range(4)]
+
+    def per_pair(width):
+        return pl.BlockSpec((1, LEN, width), lambda pair, bucket: (bucket, 0, PAIRS - 1 - pair))
+
+    tables = pl.BlockSpec((1, LEN, 128), lambda pair, bucket: (bucket, 0, 0))
     return pl.pallas_call(
         tail_kernel,
-        grid=(MICRO,),
-        in_specs=[
-            SCALARS, per_bucket(LEN, 3 * D), per_bucket(LEN, D), per_bucket(LEN, D), per_bucket(LEN, D),
-            per_bucket(LEN, 128), per_bucket(LEN, 128), whole((MICRO, LEN, D)), whole((6, D)), whole((MICRO, LEN, D)),
-            whole((4, 8, D)), whole((D, 3 * D)), ANYWHERE, ANYWHERE, ANYWHERE,
-        ]
+        grid=(PAIRS, MICRO),
+        in_specs=[SCALARS, per_pair(IN_W), per_pair(128), per_pair(128), per_pair(128), tables, tables]
+        + [whole((MICRO, LEN, D)), whole((6, D)), whole((4, 8, D))]
+        + [ANYWHERE] * 5
         + [whole(item.shape) for item in state],
         out_specs=[whole(item.shape) for item in grad_shapes] + [whole((MICRO, LEN, D)), whole((8, D)), whole((8, 128))],
         out_shape=grad_shapes + [bf16(MICRO, LEN, D), f32(8, D), f32(8, 128)],
         scratch_shapes=[
-            vmem16(MICRO, LEN, 3 * D), vmem32(LEN, D), vmem32(LEN, D), vmem16(D, MICRO * LEN), vmem16(2, 4, 2, 64, IN_W), vmem32(2, 8, D),
+            vmem16(MICRO, LEN, 3 * D), vmem32(LEN, 128), vmem32(LEN, 128), vmem16(D, MICRO * LEN), vmem32(MICRO, BLOCKS, BH, KEYS),
+            vmem32(MICRO, LEN, D), vmem16(D, 3 * D), vmem16(2, 4, 2, 64, IN_W), vmem32(2, 8, D),
         ]
         + [vmem16(2, 4, 2, 64, width) for width in widths]
         + [vmem16(2, 4, 2, 64, width) for width in widths]
-        + [vmem16(*middle_shape(index)) for index in range(5)]
-        + [vmem16(4, SUMMED[index][2], SUMMED[index][3]) for index in range(5)]
-        + [vmem16(3, SUMMED[index][2], SUMMED[index][3]) for index in range(5)]
+        + [vmem16(*middle_shape(index)) for index in range(count)]
+        + [vmem16(4, SUMMED[index][2], SUMMED[index][3]) for index in range(count)]
+        + [vmem16(3, SUMMED[index][2], SUMMED[index][3]) for index in range(count)]
         + [vmem32(4, 8, D), vmem32(3, 8, D), vmem32(4, 8, D), vmem32(4, 8, 128), vmem32(3, 8, 128), vmem32(4, 8, 128)]
-        + [dma((5, 7)), dma((5, 7)), dma((6,)), dma((6,)), dma((6,)), dma((6,)), dma((3, 2))],
-        compiler_params=params(1, 2),
+        + [dma((count, 7)), dma((count, 7)), dma((6,)), dma((6,)), dma((6,)), dma((6,)), dma((3, 2)), dma((2,))],
+        compiler_params=params(2, 2),
         name="backward_tail",
-    )(lengths, qkv, mixed, gmixed, totals, cosine, sine, x, small, gy1, sums, in_mat, gout, gup, gdown, *state)
-
-
-def lamb_all(state, grads, small, small_first, small_second, everything, norm_squares):
+    )(lengths, qkv, mixed, gmixed, totals, cosine, sine, x, small, sums, gy1, in_mat, gout, gup, gdown, *state)
+
+
+def lamb_all(state, grads, small, small_first, small_second, everything, norm_squares, input_grad):
     outs = []
     for which in range(4):
         shape = state[3 * which].shape
         outs += [f32(*shape)] * 3 + [bf16(*shape)]
-    outs += [f32(6, D)] * 4 + [f32(2, 10)]
+    outs += [f32(6, D)] * 4 + [f32(2, 10), bf16(MICRO, LEN, D)]
     return pl.pallas_call(
         lamb_kernel,
         out_shape=outs,
         compiler_params=pltpu.CompilerParams(vmem_limit_bytes=VMEM_LIMIT),
         name="lamb_all",
-    )(*state, *grads, small, small_first, small_second, everything, norm_squares)
+    )(*state, *grads, small, small_first, small_second, everything, norm_squares, input_grad)
 
 
 def tile_shard(in_proj, out_proj, up_proj, down_proj):
@@ -1216,7 +1277,7 @@
         lengths, qkv, mixed, gmixed, totals, cosine, sine, frames, small_params, gy1, sums, in_full.reshape(D, 3 * D),
         gout.reshape(4, 2, 64, D), gup.reshape(4, 2, 64, FF), gdown.reshape(4, 2, 64, FF), state,
     )
-    outs = list(lamb_all(state, grads, small_params, small_first, small_second, everything, norm_squares))
+    *outs, input_grad = lamb_all(state, grads, small_params, small_first, small_second, everything, norm_squares, input_grad)
     outs[12:16] = [item.T for item in outs[12:16]]
     return (block_out, input_grad, *outs)
 

time: 204 us -> 191 us (0.936)
  Pallas kernels: 200 us -> 190 us
  local copies, waits for them, and re-layouts: 3.05 us -> 0 us
    pallas_call x1, Pallas kernels: 63.7 us -> 57 us  [gather_forward(): pl.pallas_call(gather_kernel, grid=(PAIRS, MICRO), in_specs=[SCALARS, who...]
    pallas_call x1, Pallas kernels: 85.7 us -> 81.8 us  [backward_tail(): pl.pallas_call(tail_kernel, grid=(PAIRS, MICRO), in_specs=[SCALARS, per_p...]
    unnamed x1 -> x0, local copies, waits for them, and re-layouts: 3.05 us -> none
where the time goes in v5:
time: 191 us; the launch traced here: 190 us
  Pallas kernels  190 us (99%)
    pallas_call x1, Pallas kernels, backward_tail(): pl.pallas_call(tail_kernel, grid=(PAIRS, MICRO), in_specs=[SCALARS, per_p...  81.8 us
    pallas_call x1, Pallas kernels, gather_forward(): pl.pallas_call(gather_kernel, grid=(PAIRS, MICRO), in_specs=[SCALARS, who...  57 us
    pallas_call x1, Pallas kernels, mlp_both(): pl.pallas_call(mlp_kernel, grid=(count, LEN // MLP_ROWS), in_specs=[SCALA...  45.5 us
    pallas_call x1, Pallas kernels, lamb_all(): pl.pallas_call(lamb_kernel, out_shape=outs, compiler_params=pltpu.Compile...  5.26 us

profile of v5, /device:TPU:0, one launch (start us, length us, event | category | flops | bytes accessed | tf_op | source)
XLA Modules:
  0.0 190.5 jit_solution(12268125295490937232)
XLA Ops:
  0.7 57.0 %gather_forward.1 = (bf16[2,1024,1536]{2,1,0:T(8,128)(2,1)}, bf16[2,1024,512]{2,1,0:T(8,128)(2,1)}, f32[2,1024,512]{2,1,0:T(8,128)}, f32[2,1024,128]{2,1,0:T(8,1...) custom-call(s32[2,4,4]{2,1,0:T(4,128)} %lengths_ref.5, ...), custom_call_target="tpu_custom_call" | custom-call | tf_op jit(solution)/shard_map/gather_forward/pallas_call | solution.py:1145
  57.7 45.5 %mlp_both.1 = (bf16[2,1024,512]{2,1,0:T(8,128)(2,1)}, f32[2,1024,512]{2,1,0:T(8,128)}, bf16[2,1024,512]{2,1,0:T(8,128)(2,1)}, f32[4,8,512]{2,1,0:T(8,128)}, bf16...) custom-call(s32[2,4,4]{2,1,0:T(4,128)} %lengths_ref.5, bf16[2,1024,512]{2,1,0:T(8,128)(2,1)} %x_ref.5, ...), custom_call_target="tpu_custom_call" | custom-call | tf_op jit(solution)/shard_map/mlp_both/pallas_call | solution.py:1175
  103.2 81.8 %backward_tail.1 = (f32[64,2,192]{2,1,0:T(2,128)}, f32[2,64,64]{2,1,0:T(8,128)}, f32[64,512]{1,0:T(8,128)}, f32[64,512]{1,0:T(8,128)}, bf16[2,1024,512]{2,1,0:T(...) custom-call(s32[2,4,4]{2,1,0:T(4,128)} %lengths_ref.5, bf16[2,1024,1536]{2,1,0:T(8,128)(2,1)} %get-tuple-element.73.qkv_ref, ...), custom_call_target="tpu_custom_call" | custom-call | tf_op jit(solution)/shard_map/backward_tail/pallas_call | solution.py:1215
  185.0 5.3 %lamb_all.1 = (f32[64,2,192]{2,1,0:T(2,128)}, f32[64,2,192]{2,1,0:T(2,128)}, f32[64,2,192]{2,1,0:T(2,128)}, bf16[64,2,192]{2,1,0:T(2,128)(2,1)}, f32[2,64,64]{2,...) custom-call(f32[64,2,192]{2,1,0:T(2,128)} %refs_0_.3, ...), custom_call_target="tpu_custom_call" | custom-call | tf_op jit(solution)/shard_map/lamb_all/pallas_call | solution.py:1246

commit v6 on v5

--- a/solution.py
+++ b/solution.py
@@ -425,7 +425,7 @@
         band_biases(lengths, bias_ref)
         arrive(1, IN)
 
-    def at_0_1():
+    def send_pair():
         arrive(0, UP_A, DOWN_A)
         start(1, DOWN_A, UP_A)
         start(2, IN)
@@ -433,46 +433,46 @@
         arrive(1, OUT)
         start(2, OUT)
 
-    def at_2_0():
+    def take_core():
         arrive(3, IN)
 
-    def at_2_1():
+    def start_rest():
         arrive(0, UP_B, DOWN_B)
         start(1, DOWN_B, UP_B)
 
-    def at_2_2():
+    def turn_first():
         arrive(1, DOWN_A, UP_A)
         start(2, DOWN_A, UP_A)
         start(3, UP_A)
 
-    def at_4_0():
+    def take_y():
         arrive(2, IN)
         start(4, IN)
 
-    def at_5_2():
+    def turn_rest():
         arrive(1, DOWN_B, UP_B)
         start(2, DOWN_B, UP_B)
         start(3, UP_B)
 
-    def at_6_0():
+    def take_last():
         arrive(4, IN)
         keep(IN).start()
 
-    def at_6_1():
+    def core_first():
         arrive(2, OUT, DOWN_A)
         start(3, OUT, DOWN_A)
         start(4, OUT, DOWN_A)
 
-    def at_7_1():
+    def core_up():
         arrive(2, UP_A)
         start(4, UP_A)
 
-    def at_7_3():
+    def keep_first():
         finish(OUT, DOWN_A)
 
     events = {
-        (0, 0): begin, (0, 1): at_0_1, (2, 0): at_2_0, (2, 1): at_2_1, (2, 2): at_2_2, (4, 0): at_4_0,
-        (5, 2): at_5_2, (6, 0): at_6_0, (6, 1): at_6_1, (7, 1): at_7_1, (7, 3): at_7_3,
+        (0, 0): begin, (0, 1): send_pair, (1, 2): start_rest, (2, 0): take_core, (2, 1): turn_first, (4, 0): take_y,
+        (4, 2): turn_rest, (5, 2): core_first, (6, 0): take_last, (6, 2): core_up, (7, 2): keep_first,
     }
 
     def progress(point):
@@ -569,12 +569,12 @@
         gout_ref[...] = dot(gbranch_t[...], keep_ref[...]).astype(jnp.bfloat16)
 
         def weight_grads(part, carry):
-            cols = pl.ds(pl.multiple_of(part * 256, 256), 256)
+            cols = pl.ds(pl.multiple_of(part * 512, 512), 512)
             gup_out_ref[:, cols] = dot(enter_t[...], gup_ref[:, cols]).astype(jnp.bfloat16)
             gdown_ref[:, cols] = dot(gmlp_t[...], act_ref[:, cols]).astype(jnp.bfloat16)
             return carry
 
-        lax.fori_loop(0, FF // 256, weight_grads, 0)
+        lax.fori_loop(0, FF // 512, weight_grads, 0)
 
 
 def attend_backward(

time: 191 us -> 189 us (0.990)
  Pallas kernels: 190 us -> 188 us
where the time goes in v6:
time: 189 us
  Pallas kernels  188 us (99%)
    pallas_call x1, Pallas kernels, backward_tail(): pl.pallas_call(tail_kernel, grid=(PAIRS, MICRO), in_specs=[SCALARS, per_p...  81.5 us
    pallas_call x1, Pallas kernels, gather_forward(): pl.pallas_call(gather_kernel, grid=(PAIRS, MICRO), in_specs=[SCALARS, who...  56.2 us
    pallas_call x1, Pallas kernels, mlp_both(): pl.pallas_call(mlp_kernel, grid=(count, LEN // MLP_ROWS), in_specs=[SCALA...  44.6 us
    pallas_call x1, Pallas kernels, lamb_all(): pl.pallas_call(lamb_kernel, out_shape=outs, compiler_params=pltpu.Compile...  5.26 us

profile of v6, /device:TPU:0, one launch (start us, length us, event | category | flops | bytes accessed | tf_op | source)
XLA Modules:
  0.0 188.5 jit_solution(6496026278416615345)
XLA Ops:
  0.7 56.2 %gather_forward.1 = (bf16[2,1024,1536]{2,1,0:T(8,128)(2,1)}, bf16[2,1024,512]{2,1,0:T(8,128)(2,1)}, f32[2,1024,512]{2,1,0:T(8,128)}, f32[2,1024,128]{2,1,0:T(8,1...) custom-call(s32[2,4,4]{2,1,0:T(4,128)} %lengths_ref.5, ...), custom_call_target="tpu_custom_call" | custom-call | tf_op jit(solution)/shard_map/gather_forward/pallas_call | solution.py:1145
  56.9 44.6 %mlp_both.1 = (bf16[2,1024,512]{2,1,0:T(8,128)(2,1)}, f32[2,1024,512]{2,1,0:T(8,128)}, bf16[2,1024,512]{2,1,0:T(8,128)(2,1)}, f32[4,8,512]{2,1,0:T(8,128)}, bf16...) custom-call(s32[2,4,4]{2,1,0:T(4,128)} %lengths_ref.5, bf16[2,1024,512]{2,1,0:T(8,128)(2,1)} %x_ref.5, ...), custom_call_target="tpu_custom_call" | custom-call | tf_op jit(solution)/shard_map/mlp_both/pallas_call | solution.py:1175
  101.5 81.5 %backward_tail.1 = (f32[64,2,192]{2,1,0:T(2,128)}, f32[2,64,64]{2,1,0:T(8,128)}, f32[64,512]{1,0:T(8,128)}, f32[64,512]{1,0:T(8,128)}, bf16[2,1024,512]{2,1,0:T(...) custom-call(s32[2,4,4]{2,1,0:T(4,128)} %lengths_ref.5, bf16[2,1024,1536]{2,1,0:T(8,128)(2,1)} %get-tuple-element.73.qkv_ref, ...), custom_call_target="tpu_custom_call" | custom-call | tf_op jit(solution)/shard_map/backward_tail/pallas_call | solution.py:1215
  183.1 5.3 %lamb_all.1 = (f32[64,2,192]{2,1,0:T(2,128)}, f32[64,2,192]{2,1,0:T(2,128)}, f32[64,2,192]{2,1,0:T(2,128)}, bf16[64,2,192]{2,1,0:T(2,128)(2,1)}, f32[2,64,64]{2,...) custom-call(f32[64,2,192]{2,1,0:T(2,128)} %refs_0_.3, ...), custom_call_target="tpu_custom_call" | custom-call | tf_op jit(solution)/shard_map/lamb_all/pallas_call | solution.py:1246
